TPU v7x, 32 devices: a whole 2x2x4 slice. The times are simulated.
32 devices in a mesh: wide: 8 (over z, y), narrow: 4 (over x, core).
Axes of the slice: x: 2, y: 2, z: 4, core: 2. Of those that a mesh axis runs over, the one named last changes fastest.
Arguments:
- tokens: bfloat16 [4096, 768], P('wide'), may hold values from -6 to 6
- store: bfloat16 [8, 1664, 768], P('wide', 'narrow'), may hold values from -6 to 6
- summary_length: int32 [8], P('wide'), may hold values from 64 to 512, as said below
- top_index: int32 [4096, 12, 4, 256], P('wide', 'narrow'), may hold values from 0 to 415, as said below
- cotangent: bfloat16 [4096, 768], P('wide'), may hold values from -6 to 6
- self_qkv_weight: bfloat16 [3, 768, 768], P(None, None, 'narrow'), may hold values from -0.21875 to 0.21875
- self_qv_bias: float32 [2, 768], P(None, 'narrow'), may hold values from -3 to 3
- self_out_weight: bfloat16 [768, 768], P('narrow'), may hold values from -0.875 to 0.875
- self_out_bias: float32 [768], replicated, may hold values from -3 to 3
- qkv_weight: bfloat16 [3, 768, 768], P(None, None, 'narrow'), may hold values from -0.21875 to 0.21875
- qv_bias: float32 [2, 768], P(None, 'narrow'), may hold values from -3 to 3
- out_weight: bfloat16 [768, 768], P('narrow'), may hold values from -0.875 to 0.875
- out_bias: float32 [768], replicated, may hold values from -3 to 3
- fc1_weight: bfloat16 [768, 3072], P(None, 'narrow'), may hold values from -0.21875 to 0.21875
- fc1_bias: float32 [3072], P('narrow'), may hold values from -3 to 3
- fc2_weight: bfloat16 [3072, 768], P('narrow'), may hold values from -0.109375 to 0.109375
- fc2_bias: float32 [768], replicated, may hold values from -3 to 3
- norm_gain: float32 [3, 768], replicated, may hold values from 0.4 to 1.6
- norm_shift: float32 [3, 768], replicated, may hold values from -2 to 2
Outputs:
- mixed: bfloat16 [4096, 768], P('wide')
- tokens_grad: float32 [4096, 768], P('wide')
- store_grad: float32 [8, 1664, 768], P('wide', 'narrow')
- self_qkv_grad: float32 [3, 768, 768], P(None, 'wide', 'narrow')
- self_qv_bias_grad: float32 [2, 768], P(None, 'narrow')
- self_out_weight_grad: float32 [768, 768], P('narrow', 'wide')
- self_out_bias_grad: float32 [768], replicated
- qkv_grad: float32 [3, 768, 768], P(None, 'wide', 'narrow')
- qv_bias_grad: float32 [2, 768], P(None, 'narrow')
- out_weight_grad: float32 [768, 768], P('narrow', 'wide')
- out_bias_grad: float32 [768], replicated
- fc1_grad: float32 [768, 3072], P('wide', 'narrow')
- fc1_bias_grad: float32 [3072], P('narrow')
- fc2_grad: float32 [3072, 768], P('narrow', 'wide')
- fc2_bias_grad: float32 [768], replicated
- norm_gain_grad: float32 [3, 768], replicated
- norm_shift_grad: float32 [3, 768], replicated
Inputs may be any that keep to these rules, and one draw needn't show every extreme that they name: `summary_length`: the longest summary has exactly 512 tokens and the shortest exactly 64. `top_index`: each list of 256 indices is strictly increasing, starts at 0 and ends at 415.
All inputs are finite; a program needn't handle non-finite values.
Results may differ from a plain program's by a relative error of at most 0.025.
Values may be sent and summed in bfloat16 or wider, within the bound.
No kernel may reach another device: no remote copies, remote signals or barrier semaphores. Data moves between devices by JAX's collectives and lax.ppermute only.
A program may use at most 128 MiB of HBM per device.

v0:
```python
import functools

import jax
import jax.numpy as jnp
from jax import lax
from jax.experimental import pallas as pl
from jax.experimental.pallas import tpu as pltpu
from jax.sharding import PartitionSpec as P

F32 = jnp.float32
BF = jnp.bfloat16
NN = (((1,), (0,)), ((), ()))
NT = (((1,), (1,)), ((), ()))
TN = (((0,), (0,)), ((), ()))
EPS = 1e-05
PACE = 1.1e8
SELF_MIB = 60
EXTRA = 16

CORE = [(i, i ^ 1) for i in range(4)]
ACROSS = [(i, i ^ 2) for i in range(4)]


def mm(left, right, dims=NN):
    return lax.dot_general(left, right, dims, preferred_element_type=F32)


def shape(*dims, dtype=F32):
    return jax.ShapeDtypeStruct(dims, dtype)


def tie(value, *earlier):
    return lax.optimization_barrier((value, *earlier))[0]


class Operand:
    def __init__(self, source, buffer, sems, first, parts):
        self.buffer = buffer
        self.parts = parts
        if parts:
            self.copies = [
                pltpu.make_async_copy(source.at[i], buffer.at[i], sems.at[first + i]) for i in range(buffer.shape[0])
            ]
        else:
            self.copies = [pltpu.make_async_copy(source, buffer, sems.at[first])]
        self.waited = [False] * len(self.copies)
        for copy in self.copies:
            copy.start()

    def ready(self, part=None):
        for i, copy in enumerate(self.copies):
            if not self.waited[i] and (part is None or i == part):
                copy.wait()
                self.waited[i] = True

    @property
    def shape(self):
        return self.buffer.shape

    def __getitem__(self, at):
        self.ready(at if self.parts and isinstance(at, int) else None)
        return self.buffer[at]


class Result:
    def __init__(self, target, buffer, sems, first, parts):
        self.buffer = buffer
        if parts:
            self.copies = [
                pltpu.make_async_copy(buffer.at[i], target.at[i], sems.at[first + i]) for i in range(buffer.shape[0])
            ]
        else:
            self.copies = [pltpu.make_async_copy(buffer, target, sems.at[first])]
        self.started = [False] * len(self.copies)

    @property
    def shape(self):
        return self.buffer.shape

    @property
    def dtype(self):
        return self.buffer.dtype

    def __setitem__(self, at, value):
        self.buffer[at] = value

    def flush(self, part=0):
        self.copies[part].start()
        self.started[part] = True

    def finish(self):
        for i in range(len(self.copies)):
            if not self.started[i]:
                self.flush(i)
        for copy in self.copies:
            copy.wait()


def far(array, take=None, dims=None, parts=False):
    return ("far", array, take, tuple(dims or array.shape), parts)


def near(array, take=None):
    return ("near", array, take, None, False)


def raw(array):
    return ("raw", array, None, None, False)


def launch(body, name, at, ins, outs, scratch=(), mib=16, us=2.0):
    in_specs = [pl.BlockSpec(memory_space=pltpu.SMEM)]
    buffers, n_in, n_out = [], 0, 0
    for kind, array, _, dims, parts in ins:
        in_specs.append(pl.BlockSpec(memory_space=pltpu.VMEM if kind == "near" else pltpu.HBM))
        if kind == "far":
            buffers.append(pltpu.VMEM(dims, array.dtype))
            n_in += dims[0] if parts else 1
    out_specs, structs = [], []
    for out in outs:
        if isinstance(out, tuple):
            struct, parts = out
            out_specs.append(pl.BlockSpec(memory_space=pltpu.HBM))
            buffers.append(pltpu.VMEM(struct.shape, struct.dtype))
            n_out += struct.shape[0] if parts else 1
        else:
            struct = out
            out_specs.append(pl.BlockSpec(memory_space=pltpu.VMEM))
        structs.append(struct)
    n_buffers = len(buffers)
    sems = [pltpu.SemaphoreType.DMA((max(n, 1),)) for n in (n_in, n_out)]

    def kernel(at_ref, *refs):
        in_refs, out_refs = refs[: len(ins)], refs[len(ins) : len(ins) + len(outs)]
        rest = refs[len(ins) + len(outs) :]
        bufs, user, (in_sems, out_sems) = list(rest[:n_buffers]), rest[n_buffers:-2], rest[-2:]
        place, given = 0, []
        for ref, (kind, _, take, dims, parts) in zip(in_refs, ins):
            source = take(ref, at_ref) if take else ref
            if kind == "far":
                given.append(Operand(source, bufs.pop(0), in_sems, place, parts))
                place += dims[0] if parts else 1
            else:
                given.append(source)
        place, results = 0, []
        for ref, out in zip(out_refs, outs):
            if isinstance(out, tuple):
                results.append(Result(ref, bufs.pop(0), out_sems, place, out[1]))
                place += out[0].shape[0] if out[1] else 1
            else:
                results.append(ref)
        body(at_ref, given, results, user)
        for operand in given:
            if isinstance(operand, Operand):
                operand.ready()
        for result in results:
            if isinstance(result, Result):
                result.finish()

    return pl.pallas_call(
        kernel,
        in_specs=in_specs,
        out_specs=out_specs,
        out_shape=structs,
        scratch_shapes=buffers + list(scratch) + sems,
        compiler_params=pltpu.CompilerParams(vmem_limit_bytes=mib << 20),
        cost_estimate=pl.CostEstimate(flops=int(us * PACE), bytes_accessed=1000, transcendentals=0),
        name=name,
    )(at, *[entry[1] for entry in ins])


def norm_stats(value):
    centre = value - jnp.mean(value, axis=-1, keepdims=True)
    spread = jnp.mean(centre * centre, axis=-1, keepdims=True)
    inverse = lax.rsqrt(spread + EPS)
    return centre * inverse, inverse


def norm_backward(grad, normed, inverse, gain):
    scaled = grad * gain
    centred = scaled - jnp.mean(scaled, axis=-1, keepdims=True)
    return inverse * (centred - normed * jnp.mean(scaled * normed, axis=-1, keepdims=True))


def column_sum(value):
    return jnp.sum(value, axis=0, keepdims=True)


def erf(value):
    x = jnp.clip(value, -4.0, 4.0)
    y = x * x
    top = jnp.full_like(y, -2.72614225801306e-10)
    for factor in (
        2.77068142495902e-08,
        -2.10102402082508e-06,
        -5.69250639462346e-05,
        -7.34990630326855e-04,
        -2.95459980854025e-03,
        -1.60960333262415e-02,
    ):
        top = top * y + factor
    low = jnp.full_like(y, -1.45660718464996e-05)
    for factor in (
        -2.13374055278905e-04,
        -1.68282697438203e-03,
        -7.37332916720468e-03,
        -1.42647390514189e-02,
    ):
        low = low * y + factor
    return x * top / low


def two_terms(value):
    high = value.astype(BF)
    return jnp.concatenate([high, (value - high.astype(F32)).astype(BF)], axis=0)


def from_terms(stacked):
    rows = stacked.shape[0] // 2
    terms = stacked.astype(F32)
    return terms[:rows] + terms[rows:]


def rows_at(place, rows):
    return pl.ds(pl.multiple_of(place * rows, rows), rows)


def self_forward(at, tokens, w, b, wo, nh):
    rows, width = tokens.shape
    local = w.shape[1]
    half = rows // 2
    hd = local // nh
    scale = hd**-0.5

    def body(at, ins, outs, _):
        tok, w, wo, b = ins
        qkv, prob, flat, send, keep = outs
        x = tok[...]
        q = (mm(x, w[0], NT) + b[0:1]).astype(BF)
        k = mm(x, w[1], NT).astype(BF)
        v = (mm(x, w[2], NT) + b[1:2]).astype(BF)
        for i, value in enumerate((q, k, v)):
            qkv[i] = value
            qkv.flush(i)
        row_ids = lax.broadcasted_iota(jnp.int32, (rows, rows), 0)
        key_ids = lax.broadcasted_iota(jnp.int32, (rows, rows), 1)
        allowed = (key_ids <= row_ids) & (key_ids < at[3])
        found = []
        for h in range(nh):
            part = slice(h * hd, (h + 1) * hd)
            scores = mm(q[:, part], k[:, part], NT) * scale
            scores = jnp.where(allowed, scores, -1e30)
            shifted = jnp.exp(scores - jnp.max(scores, axis=1, keepdims=True))
            weights = (shifted * (1.0 / jnp.sum(shifted, axis=1, keepdims=True))).astype(BF)
            prob[h] = weights
            prob.flush(h)
            found.append(mm(weights, v[:, part]).astype(BF))
        flat[...] = jnp.concatenate(found, axis=1)
        flat.flush()
        send[...] = mm(flat.buffer[rows_at(1 - at[0], half), :], wo[...]).astype(BF)
        send.flush()
        keep[...] = mm(flat.buffer[rows_at(at[0], half), :], wo[...])

    return launch(
        body,
        "self_fwd",
        at,
        [far(tokens), far(w, parts=True), far(wo), far(b)],
        [
            (shape(3, rows, local, dtype=BF), True),
            (shape(nh, rows, rows, dtype=BF), True),
            (shape(rows, local, dtype=BF), False),
            (shape(half, width, dtype=BF), False),
            (shape(half, width), False),
        ],
        mib=SELF_MIB,
        us=4,
    )


def first_norm(at, mine, other, tokens, bias, gain, shift):
    half, width = mine.shape

    def body(at, ins, outs, _):
        mine, other, tok, bias, gain, shift = ins
        total, after, low = outs
        value = tok[...].astype(F32) + (mine[...].astype(F32) + other[...].astype(F32)) + bias[...]
        total[...] = value
        normed, _ = norm_stats(value)
        result = normed * gain[0:1] + shift[0:1]
        after[...] = result
        low[...] = result.astype(BF)

    return launch(
        body,
        "first_norm",
        at,
        [
            near(mine),
            near(other),
            near(tokens, lambda ref, at: ref.at[rows_at(at[0], half), :]),
            near(bias),
            near(gain),
            near(shift),
        ],
        [shape(half, width), shape(half, width), shape(half, width, dtype=BF)],
        us=1.7,
    )


def index_rows(top_index):
    rows, nh, ns, keep = top_index.shape
    flat = top_index.reshape(rows, nh, ns, keep // 128, 128).transpose(0, 1, 3, 2, 4)
    return flat.reshape(rows * nh * ns * (keep // 128), 128)


def make_mask(at, flat, dims, seg, tile, turn):
    rows, nh, ns, keep = dims
    halves = keep // 128
    per_row = nh * ns * halves
    tiles = rows // 2 // tile
    columns = ns * seg
    blocks = columns // 128
    group = 32

    def body(at, ins, outs, _):
        (index,) = ins
        (bias,) = outs
        lane = lax.broadcasted_iota(jnp.int32, (group, 128), 1).astype(F32)
        lane_low = lane.astype(BF)
        empty = jnp.full((group, 128), -1.0, BF)
        own = at[2]
        steps = []
        step = 1
        while step <= seg - keep:
            steps.insert(0, step)
            step *= 2
        turns = steps + [(seg * s) % 128 for s in range(ns)]
        below = {s: lane_low < jnp.asarray(s, BF) for s in turns if 0 < s < 128}

        for t in range(tiles):
            index.ready(t)
            source = index.buffer.at[t]

            def one_group(g, _):
                for h in range(nh):
                    v = [empty] * blocks
                    for slot in range(ns):
                        first, turn = divmod(seg * slot, 128)
                        for c in range(halves):
                            start = g * (group * per_row) + h * ns * halves + c * ns + (own ^ slot)
                            found = jnp.concatenate(
                                [source[pl.ds(start + q * 8 * per_row, 8, stride=per_row), :] for q in range(group // 8)],
                                axis=0,
                            )
                            ahead = (found.astype(F32) - (lane + float(128 * c))).astype(BF)
                            at_block = first + c
                            if turn == 0:
                                v[at_block] = ahead
                            else:
                                turned = pltpu.roll(ahead, turn, axis=1)
                                v[at_block] = jnp.where(below[turn], v[at_block], turned)
                                v[at_block + 1] = jnp.where(below[turn], turned, v[at_block + 1])
                    for s in steps:
                        gap = jnp.asarray(s, BF)
                        moved = [x - gap for x in v]
                        stay = [jnp.where(x >= gap, empty, x) for x in v]
                        if s % 128 == 0:
                            hop = s // 128
                            v = stay[:hop] + [jnp.maximum(stay[i], moved[i - hop]) for i in range(hop, blocks)]
                        else:
                            turned = [pltpu.roll(x, s, axis=1) for x in moved]
                            v = [
                                jnp.maximum(stay[i], jnp.where(below[s], turned[i - 1], turned[i])) for i in range(blocks)
                            ]
                    for i in range(blocks):
                        bias[h, pl.ds(pl.multiple_of(t * tile + g * group, group), group), i * 128 : (i + 1) * 128] = v[
                            i
                        ] * jnp.asarray(1e30, BF)
                return 0

            lax.fori_loop(0, tile // group, one_group, 0)

    flat = flat.reshape(2 * tiles, tile * per_row, 128)
    return launch(
        body,
        "mask",
        at,
        [
            far(
                flat,
                lambda ref, at: ref.at[pl.ds((at[0] ^ turn) * tiles, tiles)],
                (tiles, tile * per_row, 128),
                parts=True,
            )
        ],
        [shape(nh, rows // 2, columns, dtype=BF)],
        us=10,
    )[0]


def keys_values(at, shards, w, nh):
    seg, width = shards[0].shape
    local = w.shape[1]
    hd = local // nh

    def body(at, ins, outs, _):
        for slot in range(4):
            x = ins[slot][...]
            span = slice(slot * seg, (slot + 1) * seg)
            for i, out in enumerate(outs):
                full = mm(x, ins[4][i + 1], NT)
                high = full.astype(BF)
                low = (full - high.astype(F32)).astype(BF)
                for h in range(nh):
                    part = slice(h * hd, (h + 1) * hd)
                    out[h, span, :] = jnp.concatenate([high[:, part], low[:, part]], axis=1)

    out = shape(nh, 4 * seg, 2 * hd, dtype=BF)
    return launch(body, "keys_values", at, [near(s) for s in shards] + [near(w)], [out, out], us=2)


def cross_forward(at, mine, other, bias_mine, bias_other, keys, values, w, b, wo, nh):
    half, width = mine.shape
    rows = 2 * half
    local = w.shape[1]
    hd = local // nh
    slots = keys.shape[1]
    scale = hd**-0.5

    def body(at, ins, outs, scratch):
        mine, other, wq, keys, bias_mine, bias_other, values, wo, b = ins
        keep, send, raised, inverse, query, heads = outs
        twice, found = scratch
        for r, x in enumerate((mine, other)):
            q = (mm(x[...], wq[0], NT) + b[0:1]).astype(BF)
            query[r * half : (r + 1) * half, :] = q
            scaled = q * jnp.asarray(scale, BF)
            for h in range(nh):
                part = scaled[:, h * hd : (h + 1) * hd]
                twice[h, r * half : (r + 1) * half, :] = jnp.concatenate([part, part], axis=1)

        def one_head(h, _):
            for r, bias in enumerate((bias_mine, bias_other)):
                span = slice(r * half, (r + 1) * half)
                scores = mm(twice[h, span, :], keys[h], NT) + bias[h].astype(F32)
                e = jnp.exp(scores - jnp.max(scores, axis=1, keepdims=True))
                total = 1.0 / jnp.sum(e, axis=1, keepdims=True)
                low = e.astype(BF)
                raised[h, span, :] = low
                inverse[h, span, :] = jnp.broadcast_to(total, (half, 128))
                both = mm(low, values[h])
                found[h, span, :] = (both[:, :hd] + both[:, hd:]) * total
            return 0

        lax.fori_loop(0, nh, one_head, 0)
        for r, target in enumerate((keep, send)):
            span = slice(r * half, (r + 1) * half)
            out = (jnp.concatenate([found[h, span, :] for h in range(nh)], axis=1) + b[1:2]).astype(BF)
            heads[span, :] = out
            target[...] = mm(out, wo[...]).astype(target.dtype)

    return launch(
        body,
        "cross_fwd",
        at,
        [near(a) for a in (mine, other, w, keys, bias_mine, bias_other, values, wo, b)],
        [
            shape(half, width),
            shape(half, width, dtype=BF),
            shape(nh, rows, slots, dtype=BF),
            shape(nh, rows, 128),
            shape(rows, local, dtype=BF),
            shape(rows, local, dtype=BF),
        ],
        scratch=[pltpu.VMEM((nh, rows, 2 * hd), BF), pltpu.VMEM((nh, rows, hd), F32)],
        mib=30,
        us=9,
    )


def counted_rows(at, half):
    rows = half // 2
    place = lax.broadcasted_iota(jnp.int32, (half, 1), 0)
    return ((place >= at[1] * rows) & (place < (at[1] + 1) * rows)).astype(F32)


def stacked_sums(*values):
    sums = [column_sum(value) for value in values]
    return jnp.concatenate(sums + [jnp.zeros((8 - len(sums), values[0].shape[1]), F32)], axis=0)


def second_norm(at, after, mine, other, bias, gain, shift):
    half, width = mine.shape

    def body(at, ins, outs, _):
        after, mine, other, bias, gain, shift = ins
        total, low = outs
        value = after[...] + (mine[...].astype(F32) + other[...].astype(F32)) + bias[...]
        total[...] = value
        normed, _ = norm_stats(value)
        low[...] = (normed * gain[1:2] + shift[1:2]).astype(BF)

    ins = [near(a) for a in (after, mine, other, bias, gain, shift)]
    return launch(body, "second_norm", at, ins, [shape(half, width), shape(half, width, dtype=BF)], us=1.5)


def feed_up(at, mine, other, f1, f2, b1):
    half, width = mine.shape
    units = f1.shape[1]

    def body(at, ins, outs, _):
        mine, other, f1, f2, b1 = ins
        keep, send, hidden, slope = outs
        for r, (x, target) in enumerate(((other, send), (mine, keep))):
            span = slice((1 - r) * half, (2 - r) * half)
            low, steep = gelu_pair(mm(x[...], f1[...]) + b1[...])
            hidden[span, :] = low
            slope[span, :] = steep
            target[...] = mm(low, f2[...]).astype(target.dtype)

    ins = [near(a) for a in (mine, other, f1, f2, b1)]
    outs = [
        shape(half, width),
        shape(half, width, dtype=BF),
        shape(2 * half, units, dtype=BF),
        shape(2 * half, units),
    ]
    return launch(body, "feed_up", at, ins, outs, us=4)


def third_norm(at, total, mine, other, cot, bias, gain, shift):
    half, width = mine.shape

    def body(at, ins, outs, _):
        total, mine, other, cot, bias, gain, shift = ins
        mixed, dlast_out, low, sums = outs
        normed_mid, _ = norm_stats(total[...])
        last = normed_mid * gain[1:2] + shift[1:2] + (mine[...].astype(F32) + other[...].astype(F32)) + bias[...]
        normed, inverse = norm_stats(last)
        first_row = at[0] * half
        live = (first_row + lax.broadcasted_iota(jnp.int32, (half, 1), 0) < at[3]).astype(F32)
        mixed[...] = ((normed * gain[2:3] + shift[2:3]) * live).astype(BF)
        delta = cot[...].astype(F32) * live
        dlast = norm_backward(delta, normed, inverse, gain[2:3])
        dlast_out[...] = dlast
        low[...] = dlast.astype(BF)
        counted = counted_rows(at, half)
        sums[...] = stacked_sums(delta * normed * counted, delta * counted, dlast * counted)

    ins = [
        near(total),
        near(mine),
        near(other),
        near(cot, lambda ref, at: ref.at[rows_at(at[0], half), :]),
        near(bias),
        near(gain),
        near(shift),
    ]
    outs = [shape(half, width, dtype=BF), shape(half, width), shape(half, width, dtype=BF), shape(8, width)]
    return launch(body, "third_norm", at, ins, outs, us=2.5)


def feed_down(at, mine, other, f1, f2, slope):
    half, width = mine.shape
    units = f1.shape[1]

    def body(at, ins, outs, _):
        mine, other, f1, f2, slope = ins
        keep, send, dpre, sums = outs
        total = jnp.zeros((1, units), F32)
        for r, (x, target) in enumerate(((other, send), (mine, keep))):
            span = slice((1 - r) * half, (2 - r) * half)
            grad = mm(x[...], f2[...], NT) * slope[span, :]
            total = total + column_sum(grad)
            low = grad.astype(BF)
            dpre[span, :] = low
            target[...] = mm(low, f1[...], NT).astype(target.dtype)
        sums[...] = total

    ins = [near(a) for a in (mine, other, f1, f2, slope)]
    outs = [
        shape(half, width),
        shape(half, width, dtype=BF),
        shape(2 * half, units, dtype=BF),
        shape(1, units),
    ]
    return launch(body, "feed_down", at, ins, outs, us=3)


def second_back(at, dlast, mine, other, total, gain):
    half, width = mine.shape

    def body(at, ins, outs, _):
        dlast, mine, other, total, gain = ins
        dsecond, low, sums = outs
        dmid = dlast[...] + (mine[...].astype(F32) + other[...].astype(F32))
        normed, inverse = norm_stats(total[...])
        result = norm_backward(dmid, normed, inverse, gain[1:2])
        dsecond[...] = result
        low[...] = result.astype(BF)
        counted = counted_rows(at, half)
        sums[...] = stacked_sums(dmid * normed * counted, dmid * counted, result * counted)

    ins = [near(a) for a in (dlast, mine, other, total, gain)]
    outs = [shape(half, width), shape(half, width, dtype=BF), shape(8, width)]
    return launch(body, "second_back", at, ins, outs, us=1.8)


def gelu_pair(pre):
    phi = 0.5 * (1.0 + erf(pre * 0.7071067811865476))
    return (pre * phi).astype(BF), phi + pre * (jnp.exp(pre * pre * -0.5) * 0.3989422804014327)


def cross_backward(at, z_mine, z_other, raised, inverse, query, keys, values, w, wo, nh):
    half, width = z_mine.shape
    rows = 2 * half
    local = w.shape[1]
    hd = local // nh
    slots = keys.shape[1]
    scale = hd**-0.5

    def body(at, ins, outs, scratch):
        z_halves, (wo, inverse, values, raised, query, keys, w) = ins[:2], ins[2:]
        keep, send, dquery, dkv, sums = outs
        douts, right, found = scratch
        zero = jnp.zeros((half, hd), BF)
        head_sum = jnp.zeros((1, local), F32)
        for r in range(2):
            span = slice(r * half, (r + 1) * half)
            dhead = mm(z_halves[r][...], wo[...], NT)
            head_sum = head_sum + column_sum(dhead)
            scaled = query[span, :] * jnp.asarray(scale, BF)
            for h in range(nh):
                part = slice(h * hd, (h + 1) * hd)
                dout = (dhead[:, part] * inverse[h, span, 0:1]).astype(BF)
                douts[h, span, :] = jnp.concatenate([dout, dout], axis=1)
                right[h, 0, span, :] = jnp.concatenate([scaled[:, part], zero], axis=1)
                right[h, 1, span, :] = jnp.concatenate([zero, dout], axis=1)

        def one_head(h, _):
            grad = None
            for r in range(2):
                span = slice(r * half, (r + 1) * half)
                dprob = mm(douts[h, span, :], values[h], NT)
                low = raised[h, span, :]
                e = low.astype(F32)
                weighed = e * dprob
                mean = jnp.sum(weighed, axis=1, keepdims=True) * inverse[h, span, 0:1]
                dscore = (weighed - e * mean).astype(BF)
                both = mm(dscore, keys[h])
                found[h, span, :] = both[:, :hd] + both[:, hd:]
                part = mm(dscore, right[h, 0, span, :], TN) + mm(low, right[h, 1, span, :], TN)
                grad = part if grad is None else grad + part
            dkv[h] = grad.astype(BF)
            return 0

        lax.fori_loop(0, nh, one_head, 0)
        query_sum = jnp.zeros((1, local), F32)
        for r, target in enumerate((keep, send)):
            span = slice(r * half, (r + 1) * half)
            dq = jnp.concatenate([found[h, span, :] for h in range(nh)], axis=1) * scale
            query_sum = query_sum + column_sum(dq)
            dq_low = dq.astype(BF)
            dquery[span, :] = dq_low
            target[...] = mm(dq_low, w[0]).astype(target.dtype)
        sums[...] = jnp.concatenate([query_sum, head_sum], axis=0)

    return launch(
        body,
        "cross_bwd",
        at,
        [near(a) for a in (z_mine, z_other, wo, inverse, values, raised, query, keys, w)],
        [
            shape(half, width),
            shape(half, width, dtype=BF),
            shape(rows, local, dtype=BF),
            shape(nh, slots, 2 * hd, dtype=BF),
            shape(2, local),
        ],
        scratch=[
            pltpu.VMEM((nh, rows, 2 * hd), BF),
            pltpu.VMEM((nh, 2, rows, 2 * hd), BF),
            pltpu.VMEM((nh, rows, hd), F32),
        ],
        mib=30,
        us=11,
    )


def store_gradient(at, dkv, w, nh):
    _, slots, twice = dkv.shape
    _, local, width = w.shape
    hd = twice // 2
    seg = slots // 4

    def body(at, ins, outs, _):
        dkv, w = ins
        keep, send = outs
        weights = []
        for h in range(nh):
            part = slice(h * hd, (h + 1) * hd)
            weights += [w[1][part], w[2][part]]
        weight = jnp.concatenate(weights, axis=0)
        for slot in (1, 3, 0, 2):
            rows = jnp.concatenate([dkv[h, slot * seg : (slot + 1) * seg, :] for h in range(nh)], axis=1)
            part = mm(rows, weight)
            if slot % 2 == 0:
                keep[slot // 2] = part
            else:
                send[slot // 2] = part.astype(BF)

    return launch(
        body,
        "store_grad",
        at,
        [near(dkv), near(w)],
        [shape(2, seg, width), shape(2, seg, width, dtype=BF)],
        us=2.6,
    )


def group_outs(width, columns, blocks):
    if not blocks:
        return [shape(width, columns)]
    n, r = blocks
    return [shape(n * r, columns, dtype=BF), shape(n, r, columns)]


def emit_group(at, grad, outs, blocks, first, columns, kept_first=None):
    if not blocks:
        outs[0][:, first : first + columns] = grad[...]
        return
    n, r = blocks
    kept_first = first if kept_first is None else kept_first
    span, kept = slice(first, first + columns), slice(kept_first, kept_first + columns)
    for b in range(n):
        theirs = pl.ds(pl.multiple_of((2 * b + 1 - at[4]) * r, 8), r)
        outs[0][b * r : (b + 1) * r, span] = grad[theirs, :].astype(BF)
        outs[1][b, :, kept] = grad[pl.ds(pl.multiple_of((2 * b + at[4]) * r, 8), r), :]


def turned_product(out, left, right, step=256):
    if left.shape[1] % step:
        out[...] = mm(left[...], right[...], TN)
        return

    def some(i, _):
        span = pl.ds(pl.multiple_of(i * step, step), step)
        out[span, :] = mm(left[:, span], right[...], TN)
        return 0

    lax.fori_loop(0, left.shape[1] // step, some, 0)


def feed_grads(at, mid_mine, mid_other, dpre, dlast_mine, dlast_other, hidden, blocks):
    half, width = mid_mine.shape
    units = dpre.shape[1]
    if blocks:
        n, r = blocks
        structs = [shape(n * r, 2 * units, dtype=BF), shape(n, r, 2 * units)]
    else:
        structs = [shape(width, units), shape(width, units)]

    def body(at, ins, outs, scratch):
        mid_mine, mid_other, dpre, dlast_mine, dlast_other, hidden = ins
        left, grad = scratch
        for i, (mine, other, right) in enumerate(((mid_mine, mid_other, dpre), (dlast_mine, dlast_other, hidden))):
            left[:half, :] = mine[...]
            left[half:, :] = other[...]
            turned_product(grad, left, right)
            emit_group(at, grad, outs if blocks else outs[i:], blocks, i * units if blocks else 0, units)

    return launch(
        body,
        "feed_grads",
        at,
        [near(a) for a in (mid_mine, mid_other, dpre, dlast_mine, dlast_other, hidden)],
        structs,
        scratch=[pltpu.VMEM((2 * half, width), BF), pltpu.VMEM((width, units), F32)],
        us=4,
    )


def cross_grads(at, z_mine, z_other, mine, other, dquery, heads, shards, dkv, nh, blocks):
    half, width = mine.shape
    local = dquery.shape[1]
    hd = local // nh
    seg = shards[0].shape[0]

    def body(at, ins, outs, scratch):
        shards, (z_mine, z_other, mine, other, dquery, heads, dkv) = ins[0:4], ins[4:]
        (grad,) = scratch
        grad[...] = mm(mine[...], dquery[:half], TN) + mm(other[...], dquery[half:], TN)
        emit_group(at, grad, outs, blocks, 0, local)
        grad[...] = mm(z_mine[...], heads[:half], TN) + mm(z_other[...], heads[half:], TN)
        emit_group(at, grad, outs, blocks, 3 * local, local)
        both = None
        for slot, block in enumerate(shards):
            rows = jnp.concatenate([dkv[h, slot * seg : (slot + 1) * seg, :] for h in range(nh)], axis=1)
            part = mm(block[...], rows, TN)
            both = part if both is None else both + part
        for i in range(2):
            grad[...] = jnp.concatenate([both[:, (2 * h + i) * hd : (2 * h + i + 1) * hd] for h in range(nh)], axis=1)
            emit_group(at, grad, outs, blocks, (1 + i) * local, local)

    return launch(
        body,
        "cross_grads",
        at,
        [near(a) for a in (*shards, z_mine, z_other, mine, other, dquery, heads, dkv)],
        group_outs(width, 4 * local, blocks),
        scratch=[pltpu.VMEM((width, local), F32)],
        us=4,
    )


def first_back(at, dsecond, mine, other, total, gain):
    half, width = mine.shape

    def body(at, ins, outs, _):
        dsecond, mine, other, total, gain = ins
        dfirst, low, sums = outs
        value = dsecond[...] + (mine[...].astype(F32) + other[...].astype(F32))
        normed, inverse = norm_stats(total[...])
        result = norm_backward(value, normed, inverse, gain[0:1])
        dfirst[...] = result
        low[...] = result.astype(BF)
        counted = counted_rows(at, half)
        sums[...] = stacked_sums(value * normed * counted, value * counted, result * counted)

    ins = [near(a) for a in (dsecond, mine, other, total, gain)]
    outs = [shape(half, width), shape(half, width, dtype=BF), shape(8, width)]
    return launch(body, "first_back", at, ins, outs, us=1.8)


def self_backward(at, mine, other, tokens, w, wo, qkv, prob, flat, mixed, sums, nh, blocks):
    half, width = mine.shape
    rows = 2 * half
    local = wo.shape[0]
    hd = local // nh
    scale = hd**-0.5

    def body(at, ins, outs, scratch):
        mine, other, wo, qkv, prob, tok, w, mixed, flat = ins[:9]
        third_sums, second_sums, first_sums, fc1_sum, head_sums = ins[9:]
        send, keep = outs[0:2]
        group, extra = outs[2:-1], outs[-1]
        z, dqkv, grad = scratch
        own, distant = rows_at(at[0], half), rows_at(1 - at[0], half)
        z[own, :] = mine[...]
        z[distant, :] = other[...]
        dself = mm(z[...], wo[...], NT).astype(BF)
        v, k, q = qkv[2], qkv[1], qkv[0]
        dq, dk, dv = [], [], []
        for h in range(nh):
            part = slice(h * hd, (h + 1) * hd)
            weights_low = prob[h]
            weights = weights_low.astype(F32)
            weighed = weights * mm(dself[:, part], v[:, part], NT)
            dscore = (weighed - weights * jnp.sum(weighed, axis=1, keepdims=True)).astype(BF)
            dq.append(mm(dscore, k[:, part]))
            dk.append(mm(dscore, q[:, part], TN))
            dv.append(mm(weights_low, dself[:, part], TN))
        dquery = jnp.concatenate(dq, axis=1) * scale
        dvalue = jnp.concatenate(dv, axis=1)
        dqkv[0] = dquery.astype(BF)
        dqkv[1] = (jnp.concatenate(dk, axis=1) * scale).astype(BF)
        dqkv[2] = dvalue.astype(BF)
        x = tok[...]
        for i in range(3):
            grad[...] = mm(x, dqkv[i], TN)
            emit_group(at, grad, group, blocks, i * local, local)
        grad[...] = mm(z[...], flat[...], TN)
        emit_group(at, grad, group, blocks, 3 * local, local)
        pad = jnp.zeros((1, width - 2 * local), F32)
        extra[...] = jnp.concatenate(
            [
                third_sums[0:3],
                second_sums[0:3],
                first_sums[0:3],
                fc1_sum[...],
                jnp.concatenate([head_sums[0:1], head_sums[1:2], pad], axis=1),
                jnp.concatenate([column_sum(dquery), column_sum(dvalue), pad], axis=1),
                jnp.zeros((EXTRA - 12, width), F32),
            ],
            axis=0,
        )
        send[half:, :] = mixed[...]
        for place, out in ((distant, send), (own, keep)):
            total = mm(dqkv[0, place, :], w[0]) + mm(dqkv[1, place, :], w[1]) + mm(dqkv[2, place, :], w[2])
            out[0:half, :] = total.astype(out.dtype)

    return launch(
        body,
        "self_bwd",
        at,
        [near(a) for a in (mine, other, wo, qkv, prob, tokens, w, mixed, flat, *sums)],
        [shape(2 * half, width, dtype=BF), shape(half, width)]
        + group_outs(width, 4 * local, blocks)
        + [shape(EXTRA, width)],
        scratch=[
            pltpu.VMEM((rows, width), BF),
            pltpu.VMEM((3, rows, local), BF),
            pltpu.VMEM((width, local), F32),
        ],
        mib=20,
        us=6,
    )


def add_stage(at, keep, got, small, bit, apart=False):
    n, rows, _ = keep[0].shape
    starts = [0]
    for part in keep:
        starts.append(starts[-1] + part.shape[2])
    columns = starts[-1]
    tail = 0 if small is None else 2 * small.shape[0]
    reach = small.shape[1] if tail else 0

    def body(at, ins, outs, _):
        keeps, gots = ins[: len(keep)], ins[len(keep) : len(keep) + len(got)]
        mine = at[bit]
        send, stay = outs[:2]
        for b in range(n // 2):
            for chosen, out in ((1 - mine, send), (mine, stay)):
                block = 2 * b + chosen
                for i, part in enumerate(keeps):
                    span = slice(starts[i], starts[i + 1])
                    source, first = (gots[i], 0) if len(got) == len(keep) else (gots[0], starts[i])
                    arrived = source[
                        pl.ds(pl.multiple_of(block * rows, 8), rows), first : first + starts[i + 1] - starts[i]
                    ]
                    value = part[block] + arrived.astype(F32)
                    if out is send:
                        send[b * rows : (b + 1) * rows, span] = value.astype(BF)
                    else:
                        stay[b, :, span] = value
        if tail:
            total = ins[-1][...]
            if not apart:
                total = total + from_terms(gots[0][n * rows :, 0:reach])
            outs[2][...] = total
            send[n // 2 * rows :, 0:reach] = two_terms(total)
            if reach < columns:
                send[n // 2 * rows :, reach:] = jnp.zeros((tail, columns - reach), BF)

    ins = [near(part) for part in (*keep, *got)] + ([near(small)] if tail else [])
    outs = [shape(n // 2 * rows + tail, columns, dtype=BF), shape(n // 2, rows, columns)]
    if tail:
        outs.append(shape(small.shape[0], reach))
    return launch(body, "add_stage", at, ins, outs, us=1)


def last_stage(at, keep, got, small, parts):
    _, rows, columns = keep.shape
    each = columns // sum(count for count, _ in parts)
    reach = 0 if small is None else small.shape[1]

    def body(at, ins, outs, _):
        total = ins[0][0] + ins[1][0:rows].astype(F32)
        first = 0
        for out, (count, turned) in zip(outs, parts):
            if count == 1:
                value = total[:, first * each : (first + 1) * each]
                out[...] = value.T if turned else value
            else:
                for i in range(count):
                    out[i] = total[:, (first + i) * each : (first + i + 1) * each]
            first += count
        if reach:
            outs[-1][...] = ins[2][...] + from_terms(ins[1][rows:, 0:reach])

    outs = []
    for count, turned in parts:
        dims = (rows, each) if count == 1 else (count, rows, each)
        outs.append(shape(*(dims[::-1] if turned else dims)))
    ins = [near(keep), near(got)]
    if reach:
        ins.append(near(small))
        outs.append(shape(small.shape[0], reach))
    return launch(body, "last_stage", at, ins, outs, us=1)


def join_halves(at, mine, other):
    half, width = mine.shape
    skip = other.shape[0] - half

    def body(at, ins, outs, _):
        outs[0][rows_at(at[0], half), :] = ins[0][...]
        outs[0][rows_at(1 - at[0], half), :] = ins[1][...]

    out = shape(2 * half, width, dtype=mine.dtype)
    ins = [near(mine), near(other, lambda ref, at: ref.at[pl.ds(skip, half), :])]
    return launch(body, "join_halves", at, ins, [out])[0]


def flip(bit, size):
    return [(i, i ^ bit) for i in range(size)]


def butterfly(value, axis, size):
    bit = 1
    while bit < size:
        value = value + lax.ppermute(value, axis, flip(bit, size))
        bit *= 2
    return value


def on_device(
    tokens,
    store,
    summary_length,
    top_index,
    cotangent,
    self_qkv_weight,
    self_qv_bias,
    self_out_weight,
    self_out_bias,
    qkv_weight,
    qv_bias,
    out_weight,
    out_bias,
    fc1_weight,
    fc1_bias,
    fc2_weight,
    fc2_bias,
    norm_gain,
    norm_shift,
):
    rows, width = tokens.shape
    half = rows // 2
    nh = top_index.shape[1]
    local = qkv_weight.shape[2]
    units = fc1_weight.shape[1]
    seg = store.shape[1]
    wide = lax.axis_size("wide")
    place = lax.axis_index("narrow")
    doc = lax.axis_index("wide")
    core, across = place % 2, place // 2
    at = jnp.stack([core, across, place, summary_length[0], doc % 2, doc // 2 % 2, doc // 4]).astype(jnp.int32)
    blocks = (wide // 2, width // wide) if wide == 8 else None
    row = lambda v: v.reshape(1, -1)
    self_w = jnp.swapaxes(self_qkv_weight, 1, 2)
    cross_w = jnp.swapaxes(qkv_weight, 1, 2)

    def to_core(v):
        return lax.ppermute(v, "narrow", CORE)

    def to_across(v):
        return lax.ppermute(v, "narrow", ACROSS)

    def over(v, bit):
        return lax.ppermute(v, "wide", flip(bit, wide))

    def chip_sum(keep, send):
        return (keep + to_core(send).astype(F32)).astype(BF)

    store_x = to_across(store[0])
    qkv, prob, flat, send, keep = self_forward(at, tokens, self_w, self_qv_bias, self_out_weight, nh)
    mine = chip_sum(keep, send)
    other = to_across(mine)
    index = index_rows(top_index)
    bias_mine = make_mask(tie(at, mine), index, top_index.shape, seg, 128, 0)
    store_x, store_own = tie((store_x, store[0]), bias_mine)
    shards = [store_own, to_core(store_own), store_x, to_core(store_x)]
    bias_other = make_mask(tie(at, bias_mine), index, top_index.shape, seg, 128, 1)
    other = tie(other, bias_other)
    first_total, after, after_low = first_norm(at, mine, other, tokens, row(self_out_bias), norm_gain, norm_shift)
    after_other = to_core(after_low)

    keys, values = keys_values(tie(at, after_low), shards, cross_w, nh)
    keep, send, raised, inverse, query, heads = cross_forward(
        tie(at, keys), after_low, after_other, bias_mine, bias_other, keys, values, cross_w, qv_bias, out_weight, nh
    )
    mine = chip_sum(keep, send)
    second_total, mid_low = second_norm(at, after, mine, to_across(mine), row(out_bias), norm_gain, norm_shift)
    mid_other = to_core(mid_low)

    keep, send, hidden, slope = feed_up(at, mid_low, mid_other, fc1_weight, fc2_weight, row(fc1_bias))
    mine = chip_sum(keep, send)
    mixed_half, dlast, dlast_low, third_sums = third_norm(
        at, second_total, mine, to_across(mine), cotangent, row(fc2_bias), norm_gain, norm_shift
    )
    dlast_other = to_core(dlast_low)
    keep, send, dpre, fc1_sum = feed_down(at, dlast_low, dlast_other, fc1_weight, fc2_weight, slope)
    mine = chip_sum(keep, send)
    other = to_across(mine)
    feed_out = feed_grads(tie(at, mine), mid_low, mid_other, dpre, dlast_low, dlast_other, hidden, blocks)
    other = tie(other, feed_out[0])
    dsecond, z, second_sums = second_back(at, dlast, mine, other, second_total, norm_gain)
    z_other = to_core(z)

    keep, send, dquery, dkv, cross_sums = cross_backward(
        at, z, z_other, raised, inverse, query, keys, values, cross_w, out_weight, nh
    )
    mine = chip_sum(keep, send)
    other = to_across(mine)
    cross_out = cross_grads(
        tie(at, mine), z, z_other, after_low, after_other, dquery, heads, shards, dkv, nh, blocks
    )
    started = cross_out[0]
    if blocks:
        feed_send, feed_keep = add_stage(tie(at, started), [feed_out[1]], [over(feed_out[0], 1)], None, 5)
        feed_next = over(feed_send, 2)
        started = feed_send
    store_keep, store_send = store_gradient(tie(at, started), dkv, cross_w, nh)
    other = tie(other, store_send)
    dfirst, dfirst_low, first_sums = first_back(at, dsecond, mine, other, first_total, norm_gain)
    dfirst_other = to_core(dfirst_low)
    store_close = to_core(tie(store_send, dfirst_other))
    started = dfirst_low

    send, keep, *self_out, small = self_backward(
        tie(at, dfirst_other, store_close),
        dfirst_low,
        dfirst_other,
        tokens,
        self_w,
        self_out_weight,
        qkv,
        prob,
        flat,
        mixed_half,
        (third_sums, second_sums, first_sums, fc1_sum, cross_sums),
        nh,
        blocks,
    )
    small_rows = butterfly(small[:9], "narrow", 4)
    if blocks:
        cross_got = tie(over(cross_out[0], 1), small)
        feed_send, feed_keep = add_stage(tie(at, cross_got), [feed_keep], [feed_next], None, 6)
        feed_next = over(feed_send, 4)
        send = tie(send, feed_send)
    close = to_core(send)
    mine = (keep + close[:half].astype(F32)).astype(BF)
    other = to_across(mine)
    small = jnp.concatenate([tie(small_rows, mine), small[9:]], axis=0)
    if blocks:
        small = small + over(small, 1)
        later = tie(at, small)
        both_send, both_keep, small = add_stage(
            later, [cross_out[1], self_out[1]], [cross_got, over(self_out[0], 1)], small, 5, True
        )
        both_next = over(both_send, 2)
        other = tie(other, both_send)
    tokens_half = dfirst + (mine.astype(F32) + other.astype(F32))
    tokens_other = to_core(tokens_half)
    store_distant = to_across(tie((store_keep[1] + store_close[1].astype(F32)).astype(BF), other))
    mixed = join_halves(tie(at, tokens_half), mixed_half, close)
    if blocks:
        fc1_grad, fc2_grad = last_stage(tie(at, mixed), feed_keep, feed_next, None, [(1, False), (1, False)])
        fc2_grad = fc2_grad.T
        tokens_other = tie(tokens_other, fc1_grad)
    tokens_grad = join_halves(at, tokens_half, tokens_other)
    if blocks:
        both_send, both_keep, small = add_stage(tie(at, tokens_grad), [both_keep], [both_next], small, 6)
        both_next = over(both_send, 4)
        store_distant = tie(store_distant, both_send)
    store_grad = (store_keep[0] + store_close[0].astype(F32) + store_distant.astype(F32))[None]

    if blocks:
        qkv_grad, out_grad, self_qkv_grad, self_out_grad, small = last_stage(
            tie(at, store_grad), both_keep, both_next, small, [(3, False), (1, True), (3, False), (1, True)]
        )
    else:
        scatter = functools.partial(lax.psum_scatter, axis_name="wide", tiled=True)
        parts = lambda g: jnp.stack([g[:, i * local : (i + 1) * local] for i in range(3)])
        fc1_grad = scatter(feed_out[0], scatter_dimension=0)
        fc2_grad = scatter(feed_out[1].T, scatter_dimension=1)
        qkv_grad = scatter(parts(cross_out[0]), scatter_dimension=1)
        out_grad = scatter(cross_out[0][:, 3 * local :].T, scatter_dimension=1)
        self_qkv_grad = scatter(parts(self_out[0]), scatter_dimension=1)
        self_out_grad = scatter(self_out[0][:, 3 * local :].T, scatter_dimension=1)
        small = butterfly(small, "wide", wide)
    gain_last, shift_last, fc2_b, gain_mid, shift_mid, out_b, gain_first, shift_first, self_out_b = (
        small[i] for i in range(9)
    )
    return (
        mixed,
        tokens_grad,
        store_grad,
        self_qkv_grad,
        small[11, : 2 * local].reshape(2, local),
        self_out_grad,
        self_out_b,
        qkv_grad,
        small[10, : 2 * local].reshape(2, local),
        out_grad,
        out_b,
        fc1_grad,
        small[9],
        fc2_grad,
        fc2_b,
        jnp.stack([gain_first, gain_mid, gain_last]),
        jnp.stack([shift_first, shift_mid, shift_last]),
    )


def solution(mesh):
    placed = (
        P("wide", None),
        P("wide", "narrow", None),
        P("wide"),
        P("wide", "narrow", None, None),
        P("wide", None),
        P(None, None, "narrow"),
        P(None, "narrow"),
        P("narrow", None),
        P(),
        P(None, None, "narrow"),
        P(None, "narrow"),
        P("narrow", None),
        P(),
        P(None, "narrow"),
        P("narrow"),
        P("narrow", None),
        P(),
        P(),
        P(),
    )
    return jax.shard_map(
        on_device,
        mesh=mesh,
        in_specs=placed,
        out_specs=(
            P("wide", None),
            P("wide", None),
            P("wide", "narrow", None),
            P(None, "wide", "narrow"),
            P(None, "narrow"),
            P("narrow", "wide"),
            P(),
            P(None, "wide", "narrow"),
            P(None, "narrow"),
            P("narrow", "wide"),
            P(),
            P("wide", "narrow"),
            P("narrow"),
            P("narrow", "wide"),
            P(),
            P(),
            P(),
        ),
        check_vma=False,
    )
```

profile of v0, /device:TPU:0, one launch (start us, length us, event | category | flops | bytes accessed | tf_op | source)
XLA Modules:
  0.0 224.5 jit_solution(10659173425356344124)
XLA Ops:
  2.0 7.2 %self_fwd.1 = (bf16[3,512,192]{2,1,0:T(8,128)(2,1)}, bf16[3,512,512]{2,1,0:T(8,128)(2,1)}, bf16[512,192]{1,0:T(8,128)(2,1)}, bf16[256,768]{1,0:T(8,128)(2,1)}, f32[256,768]{1,0:T(8,128)}) custom-call(s32[7]{0:T(128)} %stack.33.at_ref, bf16[512,768]{1,0:T(8,128)(2,1)} %refs_5_.7, bf16[3,192,768]{2,1,0:T(8,128)(2,1)} %bitcast.30, bf16[192,768]{1,0:T(8,128)(2,1)} %refs_2_.11, ...), custom_call_target="tpu_custom_call" | custom-call | flops 440000000 | bytes 1000 | tf_op jit(solution)/shard_map/self_fwd/pallas_call | solution.py:160
  9.8 2.6 %collective-permute-start.2 = (bf16[416,768]{1,0:T(8,128)(2,1)S(1)}, bf16[416,768]{1,0:T(8,128)(2,1)S(1)}, u32[]{:S(2)}, u32[]{:S(2)}) collective-permute-start(bf16[416,768]{1,0:T(8,128)(2,1)S(1)} %bitcast.32), channel_id=1, source_target_pairs={{0,2},{1,3},{2,0},{3,1},{4,6},{5,7},{6,4},{7,5},{8,10},{9,11},{10,... | collective-permute-start | bytes 1916936 | tf_op jit(solution)/shard_map/ppermute | solution.py:1051
  13.6 1.9 collective-permute-start.1
  15.5 2.8 %copy-done = s32[512,3,4,256]{3,2,1,0:T(4,128)S(1)} copy-done((s32[512,3,4,256]{3,2,1,0:T(4,128)S(1)}, s32[512,3,4,256]{3,2,1,0:T(4,128)}, u32[]{:S(2)}) %copy-start) | copy-done | bytes 6291480
  18.3 9.6 %mask.2.refs_4_ = bf16[3,256,1664]{2,1,0:T(8,128)(2,1)S(1)} custom-call(s32[7]{0:T(128)S(1)} %copy-done.12, s32[4,3072,128]{2,1,0:T(8,128)S(1)} %bitcast.24), custom_call_target="tpu_custom_call" | custom-call | flops 1100000000 | bytes 1000 | tf_op jit(solution)/shard_map/mask/pallas_call | solution.py:160
  28.6 9.6 %mask.3.refs_5_ = bf16[3,256,1664]{2,1,0:T(8,128)(2,1)S(1)} custom-call(s32[7]{0:T(128)S(1)} %copy-done.12, s32[4,3072,128]{2,1,0:T(8,128)S(1)} %bitcast.25), custom_call_target="tpu_custom_call" | custom-call | flops 1100000000 | bytes 1000 | tf_op jit(solution)/shard_map/mask/pallas_call | solution.py:160
  39.4 2.3 %keys_values.1 = (bf16[3,1664,128]{2,1,0:T(8,128)(2,1)S(1)}, bf16[3,1664,128]{2,1,0:T(8,128)(2,1)S(1)}) custom-call(s32[7]{0:T(128)S(1)} %copy-done.12, bf16[416,768]{1,0:T(8,128)(2,1)S(1)} %bitcast.34, bf16[416,768]{1,0:T(8,128)(2,1)S(1)} %collective-permute-done.3.refs_1_, bf16[416,768]{1,0:T(8,128)(2,1)S(1)} %collective-permute-done.2.refs_2_, ...), custom_call_target="tpu_custom_call" | custom-call | flops 220000000 | bytes 1000 | tf_op jit(solution)/shard_map/keys_values/pallas_call | solution.py:160
  41.7 7.7 %cross_fwd.1 = (f32[256,768]{1,0:T(8,128)S(1)}, bf16[256,768]{1,0:T(8,128)(2,1)S(1)}, bf16[3,512,1664]{2,1,0:T(8,128)(2,1)S(1)}, f32[3,512,128]{2,1,0:T(8,128)S(...) custom-call(s32[7]{0:T(128)S(1)} %copy-done.12, bf16[256,768]{1,0:T(8,128)(2,1)S(1)} %get-tuple-element.120.refs_0_.refs_6_, ...), custom_call_target="tpu_custom_call" | custom-call | flops 990000000 | bytes 1000 | tf_op jit(solution)/shard_map/cross_fwd/pallas_call | solution.py:160
  51.4 1.6 collective-permute-start.7
  53.0 9.8 %collective-permute-done.7.refs_2_ = bf16[256,768]{1,0:T(8,128)(2,1)S(1)} collective-permute-done((bf16[256,768]{1,0:T(8,128)(2,1)S(1)}, bf16[256,768]{1,0:T(8,128)(2,1)S(1)}, u32[]{:S(2)}, u32[]{:S(2)}) %collective-permute-start.7) | collective-permute-done | bytes 393248 | tf_op jit(solution)/shard_map/ppermute | solution.py:1051
  63.9 1.7 collective-permute-done.8.refs_1_
  65.6 3.5 %feed_up.1 = (f32[256,768]{1,0:T(8,128)S(1)}, bf16[256,768]{1,0:T(8,128)(2,1)S(1)}, bf16[512,768]{1,0:T(8,128)(2,1)S(1)}, f32[512,768]{1,0:T(8,128)S(1)}) custom-call(s32[7]{0:T(128)S(1)} %copy-done.12, bf16[256,768]{1,0:T(8,128)(2,1)S(1)} %get-tuple-element.130.refs_0_, bf16[256,768]{1,0:T(8,128)(2,1)S(1)} %collective-permute-done.8.refs_1_, ...), custom_call_target="tpu_custom_call" | custom-call | flops 440000000 | bytes 1000 | tf_op jit(solution)/shard_map/feed_up/pallas_call | solution.py:160
  69.3 1.6 collective-permute-done.9
  71.0 1.6 collective-permute-start.10
  72.6 9.6 %collective-permute-done.10.refs_2_ = bf16[256,768]{1,0:T(8,128)(2,1)S(1)} collective-permute-done((bf16[256,768]{1,0:T(8,128)(2,1)S(1)}, bf16[256,768]{1,0:T(8,128)(2,1)S(1)}, u32[]{:S(2)}, u32[]{:S(2)}) %collective-permute-start.10) | collective-permute-done | bytes 393248 | tf_op jit(solution)/shard_map/ppermute | solution.py:1051
  82.2 1.8 third_norm.1
  84.1 1.7 collective-permute-done.11.refs_1_.refs_4_
  85.8 2.1 feed_down.1
  88.1 1.6 collective-permute-done.12
  89.8 1.6 collective-permute-start.13
  91.4 3.4 %feed_grads.1 = (bf16[384,1536]{1,0:T(8,128)(2,1)S(1)}, f32[4,96,1536]{2,1,0:T(8,128)S(1)}) custom-call(s32[7]{0:T(128)S(1)} %copy-done.12, bf16[256,768]{1,0:T(8,128)(2,1)S(1)} %get-tuple-element.130.refs_0_, bf16[256,768]{1,0:T(8,128)(2,1)S(1)} %collective-permute-done.8.refs_1_, bf16[512,768]{1,0:T(8,128)(2,1)S(1)} %get-tuple-element.139.refs_2_, ...), custom_call_target="tpu_custom_call" | custom-call | flops 440000000 | bytes 1000 | tf_op jit(solution)/shard_map/feed_grads/pallas_call | solution.py:160
  94.9 6.2 %collective-permute-done.13.refs_2_ = bf16[256,768]{1,0:T(8,128)(2,1)S(1)} collective-permute-done((bf16[256,768]{1,0:T(8,128)(2,1)S(1)}, bf16[256,768]{1,0:T(8,128)(2,1)S(1)}, u32[]{:S(2)}, u32[]{:S(2)}) %collective-permute-start.13) | collective-permute-done | bytes 393248 | tf_op jit(solution)/shard_map/ppermute | solution.py:1051
  102.4 1.7 collective-permute-start.17
  104.1 10.6 %cross_bwd.1 = (f32[256,768]{1,0:T(8,128)S(1)}, bf16[256,768]{1,0:T(8,128)(2,1)S(1)}, bf16[512,192]{1,0:T(8,128)(2,1)S(1)}, bf16[3,1664,128]{2,1,0:T(8,128)(2,1)S(1)}, f32[2,192]{1,0:T(2,128)S(1)}) custom-call(s32[7]{0:T(128)S(1)} %copy-done.12, bf16[256,768]{1,0:T(8,128)(2,1)S(1)} %get-tuple-element.144.refs_0_.refs_4_, ...), custom_call_target="tpu_custom_call" | custom-call | flops 1210000000 | bytes 1000 | tf_op jit(solution)/shard_map/cross_bwd/pallas_call | solution.py:160
  114.9 1.6 collective-permute-done.15
  116.6 1.6 collective-permute-start.16
  118.2 3.5 %cross_grads.1 = (bf16[384,768]{1,0:T(8,128)(2,1)S(1)}, f32[4,96,768]{2,1,0:T(8,128)S(1)}) custom-call(s32[7]{0:T(128)S(1)} %copy-done.12, bf16[416,768]{1,0:T(8,128)(2,1)S(1)} %bitcast.35, bf16[416,768]{1,0:T(8,128)(2,1)S(1)} %collective-permute-done.3.refs_1_, bf16[416,768]{1,0:T(8,128)(2,1)S(1)} %collective-permute-done.2.refs_2_, ...), custom_call_target="tpu_custom_call" | custom-call | flops 440000000 | bytes 1000 | tf_op jit(solution)/shard_map/cross_grads/pallas_call | solution.py:160
  121.7 9.1 %collective-permute-done.17.refs_1_ = bf16[384,1536]{1,0:T(8,128)(2,1)S(1)} collective-permute-done((bf16[384,1536]{1,0:T(8,128)(2,1)S(1)}, bf16[384,1536]{1,0:T(8,128)(2,1)S(1)}, u32[]{:S(2)}, u32[]{:S(2)}) %collective-permute-start.17) | collective-permute-done | bytes 1179680 | tf_op jit(solution)/shard_map/ppermute | solution.py:1054
  131.7 2.1 store_grad.1
  135.2 1.7 collective-permute-done.18.refs_1_
  137.0 1.6 collective-permute-start.20
  138.6 1.6 collective-permute-start.21
  140.2 5.5 %self_bwd.1 = (bf16[512,768]{1,0:T(8,128)(2,1)S(1)}, f32[256,768]{1,0:T(8,128)S(1)}, bf16[384,768]{1,0:T(8,128)(2,1)S(1)}, f32[4,96,768]{2,1,0:T(8,128)S(1)}, f32[16,768]{1,0:T(8,128)S(1)}) custom-call(s32[7]{0:T(128)S(1)} %copy-done.12, bf16[256,768]{1,0:T(8,128)(2,1)S(1)} %get-tuple-element.163.refs_0_, ...), custom_call_target="tpu_custom_call" | custom-call | flops 660000000 | bytes 1000 | tf_op jit(solution)/shard_map/self_bwd/pallas_call | solution.py:160
  145.8 6.9 %collective-permute-done.20.refs_2_ = bf16[384,768]{1,0:T(8,128)(2,1)S(1)} collective-permute-done((bf16[384,768]{1,0:T(8,128)(2,1)S(1)}, bf16[384,768]{1,0:T(8,128)(2,1)S(1)}, u32[]{:S(2)}, u32[]{:S(2)}) %collective-permute-start.20) | collective-permute-done | bytes 589856 | tf_op jit(solution)/shard_map/ppermute | solution.py:1054
  155.2 1.8 collective-permute-done.24
  157.0 1.5 collective-permute-start.25
  159.1 2.1 collective-permute-done.25
  161.3 1.6 collective-permute-start.23
  163.4 11.3 %collective-permute-done.26 = f32[16,768]{1,0:T(8,128)S(1)} collective-permute-done((f32[16,768]{1,0:T(8,128)S(1)}, f32[16,768]{1,0:T(8,128)S(1)}, u32[]{:S(2)}, u32[]{:S(2)}) %collective-permute-start.26) | collective-permute-done | bytes 49184 | tf_op jit(solution)/shard_map/ppermute | solution.py:1054
  175.5 1.6 collective-permute-start.31
  178.1 2.6 %collective-permute-start.29 = (bf16[96,1536]{1,0:T(8,128)(2,1)S(1)}, bf16[96,1536]{1,0:T(8,128)(2,1)S(1)}, u32[]{:S(2)}, u32[]{:S(2)}) collective-permute-start(bf16[96,1536]{1,0:T(8,128)(2,1)S(1)} %get-tuple-element.181), channel_id=1, source_target_pairs={{0,16},{4,20},{8,24},{12,28},{16,0},{20,4},{24,8},{28,12},{1,17},{... | collective-permute-start | bytes 884744 | tf_op jit(solution)/shard_map/ppermute | solution.py:1054
  180.7 1.5 join_halves.2
  182.2 15.1 %collective-permute-done.29.refs_1_ = bf16[96,1536]{1,0:T(8,128)(2,1)S(1)} collective-permute-done((bf16[96,1536]{1,0:T(8,128)(2,1)S(1)}, bf16[96,1536]{1,0:T(8,128)(2,1)S(1)}, u32[]{:S(2)}, u32[]{:S(2)}) %collective-permute-start.29) | collective-permute-done | bytes 294944 | tf_op jit(solution)/shard_map/ppermute | solution.py:1054
  197.2 1.4 last_stage.2
  198.6 1.8 join_halves.3
  201.1 3.4 %collective-permute-start.32 = (bf16[128,1536]{1,0:T(8,128)(2,1)S(1)}, bf16[128,1536]{1,0:T(8,128)(2,1)S(1)}, u32[]{:S(2)}, u32[]{:S(2)}) collective-permute-start(bf16[128,1536]{1,0:T(8,128)(2,1)S(1)} %get-tuple-element.200), channel_id=1, source_target_pairs={{0,16},{4,20},{8,24},{12,28},{16,0},{20,4},{24,8},{28,12},{1,17},{... | collective-permute-start | bytes 1179656 | tf_op jit(solution)/shard_map/ppermute | solution.py:1054
  205.8 14.4 %collective-permute-done.32.refs_1_ = bf16[128,1536]{1,0:T(8,128)(2,1)S(1)} collective-permute-done((bf16[128,1536]{1,0:T(8,128)(2,1)S(1)}, bf16[128,1536]{1,0:T(8,128)(2,1)S(1)}, u32[]{:S(2)}, u32[]{:S(2)}) %collective-permute-start.32) | collective-permute-done | bytes 393248 | tf_op jit(solution)/shard_map/ppermute | solution.py:1054
  220.3 1.5 last_stage.3
  (109 shorter events, 21.8 us)
Async XLA Ops:
  0.7 9.2 %copy-start.6 = (bf16[1,416,768]{2,1,0:T(8,128)(2,1)S(1)}, bf16[1,416,768]{2,1,0:T(8,128)(2,1)}, u32[]{:S(2)}) copy-start(bf16[1,416,768]{2,1,0:T(8,128)(2,1)} %param.20) | copy-start | bytes 1916932
  9.3 6.2 %copy-start.12 = (s32[7]{0:T(128)S(1)}, s32[7]{0:T(128)}, u32[]{:S(2)}) copy-start(s32[7]{0:T(128)} %stack.33.at_ref) | copy-start | bytes 88
  9.3 3.1 %collective-permute-start = (bf16[256,768]{1,0:T(8,128)(2,1)}, bf16[256,768]{1,0:T(8,128)(2,1)S(1)}, u32[]{:S(2)}, u32[]{:S(2)}) collective-permute-start(bf16[256,768]{1,0:T(8,128)(2,1)} %get-tuple-element.115), channel_id=1, source_target_pairs={{0,1},{1,0},{2,3},{3,2},{4,5},{5,4},{6,7},{7,6},{8,9},{9,8},{10,11... | collective-permute-start | bytes 1179656 | tf_op jit(solution)/shard_map/ppermute | solution.py:1048
  9.8 18.1 %collective-permute-start.2 = (bf16[416,768]{1,0:T(8,128)(2,1)S(1)}, bf16[416,768]{1,0:T(8,128)(2,1)S(1)}, u32[]{:S(2)}, u32[]{:S(2)}) collective-permute-start(bf16[416,768]{1,0:T(8,128)(2,1)S(1)} %bitcast.32), channel_id=1, source_target_pairs={{0,2},{1,3},{2,0},{3,1},{4,6},{5,7},{6,4},{7,5},{8,10},{9,11},{10,... | collective-permute-start | bytes 1916936 | tf_op jit(solution)/shard_map/ppermute | solution.py:1051
  13.6 24.6 %collective-permute-start.1 = (bf16[256,768]{1,0:T(8,128)(2,1)S(1)}, bf16[256,768]{1,0:T(8,128)(2,1)S(1)}, u32[]{:S(2)}, u32[]{:S(2)}) collective-permute-start(bf16[256,768]{1,0:T(8,128)(2,1)S(1)} %add_convert_fusion.6.refs_0_), channel_id=1, source_target_pairs={{0,2},{1,3},{2,0},{3,1},{4,6},{5,7},{6,4},{7,5},{8,10},{9,11},{10,... | collective-permute-start | bytes 1179656 | tf_op jit(solution)/shard_map/ppermute | solution.py:1051
  18.3 10.2 %copy-start.17 = (f32[768]{0:T(1024)S(1)}, f32[768]{0:T(1024)}, u32[]{:S(2)}) copy-start(f32[768]{0:T(1024)} %param.27) | copy-start | bytes 9220
  28.0 11.4 %collective-permute-start.3 = (bf16[416,768]{1,0:T(8,128)(2,1)S(1)}, bf16[416,768]{1,0:T(8,128)(2,1)S(1)}, u32[]{:S(2)}, u32[]{:S(2)}) collective-permute-start(bf16[416,768]{1,0:T(8,128)(2,1)S(1)} %bitcast.33), channel_id=1, source_target_pairs={{0,1},{1,0},{2,3},{3,2},{4,5},{5,4},{6,7},{7,6},{8,9},{9,8},{10,11... | collective-permute-start | bytes 1916936 | tf_op jit(solution)/shard_map/ppermute | solution.py:1048
  28.0 11.3 %collective-permute-start.4 = (bf16[416,768]{1,0:T(8,128)(2,1)S(1)}, bf16[416,768]{1,0:T(8,128)(2,1)S(1)}, u32[]{:S(2)}, u32[]{:S(2)}) collective-permute-start(bf16[416,768]{1,0:T(8,128)(2,1)S(1)} %collective-permute-done.2.refs_2_), channel_id=1, source_target_pairs={{0,1},{1,0},{2,3},{3,2},{4,5},{5,4},{6,7},{7,6},{8,9},{9,8},{10,11... | collective-permute-start | bytes 1916936 | tf_op jit(solution)/shard_map/ppermute | solution.py:1048
  28.5 9.7 %copy-start.2 = (bf16[512,768]{1,0:T(8,128)(2,1)S(1)}, bf16[512,768]{1,0:T(8,128)(2,1)}, u32[]{:S(2)}) copy-start(bf16[512,768]{1,0:T(8,128)(2,1)} %refs_5_.7) | copy-start | bytes 2359300
  28.5 9.7 %copy-start.13 = (f32[3,768]{1,0:T(4,128)S(1)}, f32[3,768]{1,0:T(4,128)}, u32[]{:S(2)}) copy-start(f32[3,768]{1,0:T(4,128)} %refs_4_.7) | copy-start | bytes 27652
  28.6 9.7 %copy-start.15 = (f32[3,768]{1,0:T(4,128)S(1)}, f32[3,768]{1,0:T(4,128)}, u32[]{:S(2)}) copy-start(f32[3,768]{1,0:T(4,128)} %refs_6_.1) | copy-start | bytes 27652
  39.2 2.5 %collective-permute-start.5 = (bf16[256,768]{1,0:T(8,128)(2,1)S(1)}, bf16[256,768]{1,0:T(8,128)(2,1)S(1)}, u32[]{:S(2)}, u32[]{:S(2)}) collective-permute-start(bf16[256,768]{1,0:T(8,128)(2,1)S(1)} %get-tuple-element.120.refs_0_.refs_6_), channel_id=1, source_target_pairs={{0,1},{1,0},{2,3},{3,2},{4,5},{5,4},{6,7},{7,6},{8,9},{9,8},{10,11... | collective-permute-start | bytes 1179656 | tf_op jit(solution)/shard_map/ppermute | solution.py:1048
  49.4 1.8 collective-permute-start.6
  51.3 12.6 %copy-start.19 = (f32[768]{0:T(1024)S(1)}, f32[768]{0:T(1024)}, u32[]{:S(2)}) copy-start(f32[768]{0:T(1024)} %param.33) | copy-start | bytes 9220
  51.3 14.3 %copy-start.3 = (bf16[768,768]{1,0:T(8,128)(2,1)S(1)}, bf16[768,768]{1,0:T(8,128)(2,1)}, u32[]{:S(2)}) copy-start(bf16[768,768]{1,0:T(8,128)(2,1)} %refs_2_.9) | copy-start | bytes 3538948
  51.3 14.3 %copy-start.4 = (bf16[768,768]{1,0:T(8,128)(2,1)S(1)}, bf16[768,768]{1,0:T(8,128)(2,1)}, u32[]{:S(2)}) copy-start(bf16[768,768]{1,0:T(8,128)(2,1)} %refs_3_.7) | copy-start | bytes 3538948
  51.4 11.5 %collective-permute-start.7 = (bf16[256,768]{1,0:T(8,128)(2,1)S(1)}, bf16[256,768]{1,0:T(8,128)(2,1)S(1)}, u32[]{:S(2)}, u32[]{:S(2)}) collective-permute-start(bf16[256,768]{1,0:T(8,128)(2,1)S(1)} %add_convert_fusion.5.refs_1_), channel_id=1, source_target_pairs={{0,2},{1,3},{2,0},{3,1},{4,6},{5,7},{6,4},{7,5},{8,10},{9,11},{10,... | collective-permute-start | bytes 1179656 | tf_op jit(solution)/shard_map/ppermute | solution.py:1051
  63.8 1.8 collective-permute-start.8
  69.1 13.1 %copy-start.10 = (bf16[512,768]{1,0:T(8,128)(2,1)S(1)}, bf16[512,768]{1,0:T(8,128)(2,1)}, u32[]{:S(2)}) copy-start(bf16[512,768]{1,0:T(8,128)(2,1)} %refs_3_.6) | copy-start | bytes 2359300
  69.1 1.8 collective-permute-start.9
  71.0 11.2 %collective-permute-start.10 = (bf16[256,768]{1,0:T(8,128)(2,1)S(1)}, bf16[256,768]{1,0:T(8,128)(2,1)S(1)}, u32[]{:S(2)}, u32[]{:S(2)}) collective-permute-start(bf16[256,768]{1,0:T(8,128)(2,1)S(1)} %add_convert_fusion.4.refs_1_), channel_id=1, source_target_pairs={{0,2},{1,3},{2,0},{3,1},{4,6},{5,7},{6,4},{7,5},{8,10},{9,11},{10,... | collective-permute-start | bytes 1179656 | tf_op jit(solution)/shard_map/ppermute | solution.py:1051
  84.0 1.8 collective-permute-start.11
  87.9 1.8 collective-permute-start.12
  89.8 11.2 %collective-permute-start.13 = (bf16[256,768]{1,0:T(8,128)(2,1)S(1)}, bf16[256,768]{1,0:T(8,128)(2,1)S(1)}, u32[]{:S(2)}, u32[]{:S(2)}) collective-permute-start(bf16[256,768]{1,0:T(8,128)(2,1)S(1)} %add_convert_fusion.3.refs_1_), channel_id=1, source_target_pairs={{0,2},{1,3},{2,0},{3,1},{4,6},{5,7},{6,4},{7,5},{8,10},{9,11},{10,... | collective-permute-start | bytes 1179656 | tf_op jit(solution)/shard_map/ppermute | solution.py:1051
  102.3 1.8 collective-permute-start.14
  102.4 28.4 %collective-permute-start.17 = (bf16[384,1536]{1,0:T(8,128)(2,1)S(1)}, bf16[384,1536]{1,0:T(8,128)(2,1)S(1)}, u32[]{:S(2)}, u32[]{:S(2)}) collective-permute-start(bf16[384,1536]{1,0:T(8,128)(2,1)S(1)} %get-tuple-element.141), channel_id=1, source_target_pairs={{0,4},{4,0},{8,12},{12,8},{16,20},{20,16},{24,28},{28,24},{1,5},{5... | collective-permute-start | bytes 3538952 | tf_op jit(solution)/shard_map/ppermute | solution.py:1054
  114.7 1.8 collective-permute-start.15
  116.6 17.2 %collective-permute-start.16 = (bf16[256,768]{1,0:T(8,128)(2,1)S(1)}, bf16[256,768]{1,0:T(8,128)(2,1)S(1)}, u32[]{:S(2)}, u32[]{:S(2)}) collective-permute-start(bf16[256,768]{1,0:T(8,128)(2,1)S(1)} %add_convert_fusion.2.refs_1_), channel_id=1, source_target_pairs={{0,2},{1,3},{2,0},{3,1},{4,6},{5,7},{6,4},{7,5},{8,10},{9,11},{10,... | collective-permute-start | bytes 1179656 | tf_op jit(solution)/shard_map/ppermute | solution.py:1051
  131.6 8.6 %copy-start.7 = (bf16[3,512,512]{2,1,0:T(8,128)(2,1)S(1)}, bf16[3,512,512]{2,1,0:T(8,128)(2,1)}, u32[]{:S(2)}) copy-start(bf16[3,512,512]{2,1,0:T(8,128)(2,1)} %get-tuple-element.167.refs_4_) | copy-start | bytes 4718596
  133.7 6.5 %copy-start.5 = (bf16[3,768,192]{1,2,0:T(8,128)(2,1)S(1)}, bf16[3,768,192]{1,2,0:T(8,128)(2,1)}, u32[]{:S(2)}) copy-start(bf16[3,768,192]{1,2,0:T(8,128)(2,1)} %param.24) | copy-start | bytes 2654212
  133.7 6.5 %copy-start.9 = (bf16[192,768]{1,0:T(8,128)(2,1)S(1)}, bf16[192,768]{1,0:T(8,128)(2,1)}, u32[]{:S(2)}) copy-start(bf16[192,768]{1,0:T(8,128)(2,1)} %refs_2_.11) | copy-start | bytes 884740
  133.7 6.5 %copy-start.11 = (bf16[3,512,192]{2,1,0:T(8,128)(2,1)S(1)}, bf16[3,512,192]{2,1,0:T(8,128)(2,1)}, u32[]{:S(2)}) copy-start(bf16[3,512,192]{2,1,0:T(8,128)(2,1)} %get-tuple-element.166.refs_3_) | copy-start | bytes 1769476
  133.8 6.5 %copy-start.14 = (bf16[512,192]{1,0:T(8,128)(2,1)S(1)}, bf16[512,192]{1,0:T(8,128)(2,1)}, u32[]{:S(2)}) copy-start(bf16[512,192]{1,0:T(8,128)(2,1)} %get-tuple-element.169.refs_8_) | copy-start | bytes 589828
  135.1 1.8 collective-permute-start.18
  136.9 3.3 %collective-permute-start.19 = (bf16[2,416,768]{2,1,0:T(8,128)(2,1)S(1)}, bf16[2,416,768]{2,1,0:T(8,128)(2,1)S(1)}, u32[]{:S(2)}, u32[]{:S(2)}) collective-permute-start(bf16[2,416,768]{2,1,0:T(8,128)(2,1)S(1)} %get-tuple-element.164), channel_id=1, source_target_pairs={{0,1},{1,0},{2,3},{3,2},{4,5},{5,4},{6,7},{7,6},{8,9},{9,8},{10,11... | collective-permute-start | bytes 3833864 | tf_op jit(solution)/shard_map/ppermute | solution.py:1048
  137.0 15.6 %collective-permute-start.20 = (bf16[384,768]{1,0:T(8,128)(2,1)S(1)}, bf16[384,768]{1,0:T(8,128)(2,1)S(1)}, u32[]{:S(2)}, u32[]{:S(2)}) collective-permute-start(bf16[384,768]{1,0:T(8,128)(2,1)S(1)} %get-tuple-element.154), channel_id=1, source_target_pairs={{0,4},{4,0},{8,12},{12,8},{16,20},{20,16},{24,28},{28,24},{1,5},{5... | collective-permute-start | bytes 1769480 | tf_op jit(solution)/shard_map/ppermute | solution.py:1054
  138.6 15.3 %collective-permute-start.21 = (bf16[192,1536]{1,0:T(8,128)(2,1)S(1)}, bf16[192,1536]{1,0:T(8,128)(2,1)S(1)}, u32[]{:S(2)}, u32[]{:S(2)}) collective-permute-start(bf16[192,1536]{1,0:T(8,128)(2,1)S(1)} %get-tuple-element.157), channel_id=1, source_target_pairs={{0,8},{4,12},{8,0},{12,4},{16,24},{20,28},{24,16},{28,20},{1,9},{5... | collective-permute-start | bytes 1769480 | tf_op jit(solution)/shard_map/ppermute | solution.py:1054
  154.6 6.6 %collective-permute-start.22 = (bf16[512,768]{1,0:T(8,128)(2,1)S(1)}, bf16[512,768]{1,0:T(8,128)(2,1)S(1)}, u32[]{:S(2)}, u32[]{:S(2)}) collective-permute-start(bf16[512,768]{1,0:T(8,128)(2,1)S(1)} %get-tuple-element.182), channel_id=1, source_target_pairs={{0,1},{1,0},{2,3},{3,2},{4,5},{5,4},{6,7},{7,6},{8,9},{9,8},{10,11... | collective-permute-start | bytes 2359304 | tf_op jit(solution)/shard_map/ppermute | solution.py:1048
  154.7 2.3 %collective-permute-start.24 = (f32[9,768]{1,0:T(8,128)S(1)}, f32[9,768]{1,0:T(8,128)S(1)}, u32[]{:S(2)}, u32[]{:S(2)}) collective-permute-start(f32[9,768]{1,0:T(8,128)S(1)} %bitcast.36), channel_id=1, source_target_pairs={{0,1},{1,0},{2,3},{3,2},{4,5},{5,4},{6,7},{7,6},{8,9},{9,8},{10,11... | collective-permute-start | bytes 82952 | tf_op jit(solution)/shard_map/ppermute | solution.py:1005
  157.0 4.2 %collective-permute-start.25 = (f32[9,768]{1,0:T(8,128)S(1)}, f32[9,768]{1,0:T(8,128)S(1)}, u32[]{:S(2)}, u32[]{:S(2)}) collective-permute-start(f32[9,768]{1,0:T(8,128)S(1)} %slice_add_fusion), channel_id=1, source_target_pairs={{0,2},{1,3},{2,0},{3,1},{4,6},{5,7},{6,4},{7,5},{8,10},{9,11},{10,... | collective-permute-start | bytes 82952 | tf_op jit(solution)/shard_map/ppermute | solution.py:1005
  158.6 16.1 %collective-permute-start.27 = (bf16[384,768]{1,0:T(8,128)(2,1)S(1)}, bf16[384,768]{1,0:T(8,128)(2,1)S(1)}, u32[]{:S(2)}, u32[]{:S(2)}) collective-permute-start(bf16[384,768]{1,0:T(8,128)(2,1)S(1)} %get-tuple-element.187), channel_id=1, source_target_pairs={{0,4},{4,0},{8,12},{12,8},{16,20},{20,16},{24,28},{28,24},{1,5},{5... | collective-permute-start | bytes 1769480 | tf_op jit(solution)/shard_map/ppermute | solution.py:1054
  161.3 15.8 %collective-permute-start.23 = (bf16[256,768]{1,0:T(8,128)(2,1)S(1)}, bf16[256,768]{1,0:T(8,128)(2,1)S(1)}, u32[]{:S(2)}, u32[]{:S(2)}) collective-permute-start(bf16[256,768]{1,0:T(8,128)(2,1)S(1)} %add_convert_fusion.1), channel_id=1, source_target_pairs={{0,2},{1,3},{2,0},{3,1},{4,6},{5,7},{6,4},{7,5},{8,10},{9,11},{10,... | collective-permute-start | bytes 1179656 | tf_op jit(solution)/shard_map/ppermute | solution.py:1051
  162.8 11.8 %collective-permute-start.26 = (f32[16,768]{1,0:T(8,128)S(1)}, f32[16,768]{1,0:T(8,128)S(1)}, u32[]{:S(2)}, u32[]{:S(2)}) collective-permute-start(f32[16,768]{1,0:T(8,128)S(1)} %pad_maximum_fusion), channel_id=1, source_target_pairs={{0,4},{4,0},{8,12},{12,8},{16,20},{20,16},{24,28},{28,24},{1,5},{5... | collective-permute-start | bytes 147464 | tf_op jit(solution)/shard_map/ppermute | solution.py:1054
  175.5 25.0 %collective-permute-start.31 = (bf16[224,1536]{1,0:T(8,128)(2,1)S(1)}, bf16[224,1536]{1,0:T(8,128)(2,1)S(1)}, u32[]{:S(2)}, u32[]{:S(2)}) collective-permute-start(bf16[224,1536]{1,0:T(8,128)(2,1)S(1)} %get-tuple-element.188), channel_id=1, source_target_pairs={{0,8},{4,12},{8,0},{12,4},{16,24},{20,28},{24,16},{28,20},{1,9},{5... | collective-permute-start | bytes 2064392 | tf_op jit(solution)/shard_map/ppermute | solution.py:1054
  177.2 21.4 %collective-permute-start.28 = (f32[256,768]{1,0:T(8,128)S(1)}, f32[256,768]{1,0:T(8,128)S(1)}, u32[]{:S(2)}, u32[]{:S(2)}) collective-permute-start(f32[256,768]{1,0:T(8,128)S(1)} %add_add_fusion.refs_0_), channel_id=1, source_target_pairs={{0,1},{1,0},{2,3},{3,2},{4,5},{5,4},{6,7},{7,6},{8,9},{9,8},{10,11... | collective-permute-start | bytes 2359304 | tf_op jit(solution)/shard_map/ppermute | solution.py:1048
  177.5 27.1 %collective-permute-start.30 = (bf16[416,768]{1,0:T(8,128)(2,1)S(1)}, bf16[416,768]{1,0:T(8,128)(2,1)S(1)}, u32[]{:S(2)}, u32[]{:S(2)}) collective-permute-start(bf16[416,768]{1,0:T(8,128)(2,1)S(1)} %fusion.1), channel_id=1, source_target_pairs={{0,2},{1,3},{2,0},{3,1},{4,6},{5,7},{6,4},{7,5},{8,10},{9,11},{10,... | collective-permute-start | bytes 1916936 | tf_op jit(solution)/shard_map/ppermute | solution.py:1051
  178.1 19.1 %collective-permute-start.29 = (bf16[96,1536]{1,0:T(8,128)(2,1)S(1)}, bf16[96,1536]{1,0:T(8,128)(2,1)S(1)}, u32[]{:S(2)}, u32[]{:S(2)}) collective-permute-start(bf16[96,1536]{1,0:T(8,128)(2,1)S(1)} %get-tuple-element.181), channel_id=1, source_target_pairs={{0,16},{4,20},{8,24},{12,28},{16,0},{20,4},{24,8},{28,12},{1,17},{... | collective-permute-start | bytes 884744 | tf_op jit(solution)/shard_map/ppermute | solution.py:1054
  201.1 19.1 %collective-permute-start.32 = (bf16[128,1536]{1,0:T(8,128)(2,1)S(1)}, bf16[128,1536]{1,0:T(8,128)(2,1)S(1)}, u32[]{:S(2)}, u32[]{:S(2)}) collective-permute-start(bf16[128,1536]{1,0:T(8,128)(2,1)S(1)} %get-tuple-element.200), channel_id=1, source_target_pairs={{0,16},{4,20},{8,24},{12,28},{16,0},{20,4},{24,8},{28,12},{1,17},{... | collective-permute-start | bytes 1179656 | tf_op jit(solution)/shard_map/ppermute | solution.py:1054
  (6 other events, 15.7 us)
where the time goes:
time: 225 us; the launch traced here: 224 us
  waiting for transfers between devices  98.9 us (44%)
  Pallas kernels  82.6 us (37%)
  starting transfers between devices  31.7 us (14%)
  local copies, waits for them, and re-layouts  5.5 us (2%)
  other arithmetic  3.79 us (2%)
    pallas_call x25, Pallas kernels, launch(): pl.pallas_call(kernel, in_specs=in_specs, out_specs=out_specs, out_shape=...  82.6 us
    ppermute x8, waiting for transfers between devices, over(): return lax.ppermute(v, 'wide', flip(bit, wide))  58.1 us
    ppermute x8, waiting for transfers between devices, to_across(): return lax.ppermute(v, 'narrow', ACROSS)  25.6 us
    ppermute x8, starting transfers between devices, over(): return lax.ppermute(v, 'wide', flip(bit, wide))  13.6 us
    ppermute x8, starting transfers between devices, to_across(): return lax.ppermute(v, 'narrow', ACROSS)  13.1 us
    ppermute x15, waiting for transfers between devices, to_core(): return lax.ppermute(v, 'narrow', CORE)  11.3 us
  transfers between devices with their start and end apart: 33, of which 19 were waited for; matrix products, arithmetic and copies ran while one was open for 1% of the time, Pallas kernels for 24%

commit v1 on v0

--- a/solution.py
+++ b/solution.py
@@ -1126,7 +1126,6 @@
         nh,
         blocks,
     )
-    small_rows = butterfly(small[:9], "narrow", 4)
     if blocks:
         cross_got = tie(over(cross_out[0], 1), small)
         feed_send, feed_keep = add_stage(tie(at, cross_got), [feed_keep], [feed_next], None, 6)
@@ -1135,33 +1134,45 @@
     close = to_core(send)
     mine = (keep + close[:half].astype(F32)).astype(BF)
     other = to_across(mine)
-    small = jnp.concatenate([tie(small_rows, mine), small[9:]], axis=0)
+    started = mine
     if blocks:
-        small = small + over(small, 1)
-        later = tie(at, small)
-        both_send, both_keep, small = add_stage(
-            later, [cross_out[1], self_out[1]], [cross_got, over(self_out[0], 1)], small, 5, True
+        fc1_grad, fc2_grad = last_stage(tie(at, mine), feed_keep, feed_next, None, [(1, False), (1, False)])
+        fc2_grad = fc2_grad.T
+        both_send, both_keep = add_stage(
+            tie(at, fc1_grad), [cross_out[1], self_out[1]], [cross_got, over(self_out[0], 1)], None, 5
         )
         both_next = over(both_send, 2)
-        other = tie(other, both_send)
+        started = both_send
+    other, small = tie((other, small), started)
     tokens_half = dfirst + (mine.astype(F32) + other.astype(F32))
     tokens_other = to_core(tokens_half)
-    store_distant = to_across(tie((store_keep[1] + store_close[1].astype(F32)).astype(BF), other))
+    small = jnp.concatenate([butterfly(small[:9], "narrow", 4), small[9:]], axis=0)
+    store_distant = to_across(tie((store_keep[1] + store_close[1].astype(F32)).astype(BF), small))
+    small = butterfly(small, "wide", wide)
     mixed = join_halves(tie(at, tokens_half), mixed_half, close)
+    tokens_grad = join_halves(at, tokens_half, tie(tokens_other, mixed))
     if blocks:
-        fc1_grad, fc2_grad = last_stage(tie(at, mixed), feed_keep, feed_next, None, [(1, False), (1, False)])
-        fc2_grad = fc2_grad.T
-        tokens_other = tie(tokens_other, fc1_grad)
-    tokens_grad = join_halves(at, tokens_half, tokens_other)
+        both_send, both_keep = add_stage(tie(at, tokens_grad), [both_keep], [both_next], None, 6)
+        both_next = over(both_send, 4)
+        store_distant, small = tie((store_distant, small), both_send)
+    store_grad = (store_keep[0] + store_close[0].astype(F32) + store_distant.astype(F32))[None]
+    (
+        (gain_last, shift_last, fc2_b, gain_mid, shift_mid, out_b, gain_first, shift_first, self_out_b),
+        fc1_b,
+        cross_line,
+        self_line,
+    ) = (tuple(small[i] for i in range(9)), small[9], small[10], small[11])
+    gain_grad = jnp.stack([gain_first, gain_mid, gain_last])
+    shift_grad = jnp.stack([shift_first, shift_mid, shift_last])
+    qv_grad, self_qv_grad = cross_line[: 2 * local].reshape(2, local), self_line[: 2 * local].reshape(2, local)
+
     if blocks:
-        both_send, both_keep, small = add_stage(tie(at, tokens_grad), [both_keep], [both_next], small, 6)
-        both_next = over(both_send, 4)
-        store_distant = tie(store_distant, both_send)
-    store_grad = (store_keep[0] + store_close[0].astype(F32) + store_distant.astype(F32))[None]
-
-    if blocks:
-        qkv_grad, out_grad, self_qkv_grad, self_out_grad, small = last_stage(
-            tie(at, store_grad), both_keep, both_next, small, [(3, False), (1, True), (3, False), (1, True)]
+        qkv_grad, out_grad, self_qkv_grad, self_out_grad = last_stage(
+            tie(at, store_grad, gain_grad, shift_grad, qv_grad, self_qv_grad, fc1_b, fc2_b, out_b, self_out_b),
+            both_keep,
+            both_next,
+            None,
+            [(3, False), (1, True), (3, False), (1, True)],
         )
     else:
         scatter = functools.partial(lax.psum_scatter, axis_name="wide", tiled=True)
@@ -1172,28 +1183,24 @@
         out_grad = scatter(cross_out[0][:, 3 * local :].T, scatter_dimension=1)
         self_qkv_grad = scatter(parts(self_out[0]), scatter_dimension=1)
         self_out_grad = scatter(self_out[0][:, 3 * local :].T, scatter_dimension=1)
-        small = butterfly(small, "wide", wide)
-    gain_last, shift_last, fc2_b, gain_mid, shift_mid, out_b, gain_first, shift_first, self_out_b = (
-        small[i] for i in range(9)
-    )
     return (
         mixed,
         tokens_grad,
         store_grad,
         self_qkv_grad,
-        small[11, : 2 * local].reshape(2, local),
+        self_qv_grad,
         self_out_grad,
         self_out_b,
         qkv_grad,
-        small[10, : 2 * local].reshape(2, local),
+        qv_grad,
         out_grad,
         out_b,
         fc1_grad,
-        small[9],
+        fc1_b,
         fc2_grad,
         fc2_b,
-        jnp.stack([gain_first, gain_mid, gain_last]),
-        jnp.stack([shift_first, shift_mid, shift_last]),
+        gain_grad,
+        shift_grad,
     )
 
 

time: 225 us -> 223 us (level)
  waiting for transfers between devices: 98.9 us -> 92.9 us
    ppermute x8 -> x7, waiting for transfers between devices: 58.1 us -> 36.8 us  [over(): return lax.ppermute(v, 'wide', flip(bit, wide))]
    ppermute x2 -> x5, waiting for transfers between devices: 3.93 us -> 17.5 us  [butterfly(): value = value + lax.ppermute(value, axis, flip(bit, size))]
    ppermute x2 -> x5, starting transfers between devices: 2.05 us -> 4.96 us  [butterfly(): value = value + lax.ppermute(value, axis, flip(bit, size))]
    ppermute x8 -> x7, starting transfers between devices: 13.6 us -> 10.9 us  [over(): return lax.ppermute(v, 'wide', flip(bit, wide))]
  transfers between devices with their start and end apart: 33 -> 35, of which waited for: 19 -> 22; matrix products, arithmetic and copies ran while one was open for 1% -> 3% of each run, Pallas kernels for 24% -> 25%
where the time goes in v1:
time: 223 us; the launch traced here: 222 us
  waiting for transfers between devices  92.9 us (42%)
  Pallas kernels  83.5 us (37%)
  starting transfers between devices  32.4 us (15%)
  local copies, waits for them, and re-layouts  6.3 us (3%)
  other arithmetic  5.13 us (2%)
    pallas_call x25, Pallas kernels, launch(): pl.pallas_call(kernel, in_specs=in_specs, out_specs=out_specs, out_shape=...  83.5 us
    ppermute x7, waiting for transfers between devices, over(): return lax.ppermute(v, 'wide', flip(bit, wide))  36.8 us
    ppermute x8, waiting for transfers between devices, to_across(): return lax.ppermute(v, 'narrow', ACROSS)  25.6 us
    ppermute x5, waiting for transfers between devices, butterfly(): value = value + lax.ppermute(value, axis, flip(bit, size))  17.5 us
    ppermute x8, starting transfers between devices, to_across(): return lax.ppermute(v, 'narrow', ACROSS)  13.1 us
    ppermute x15, waiting for transfers between devices, to_core(): return lax.ppermute(v, 'narrow', CORE)  13.1 us
    ppermute x7, starting transfers between devices, over(): return lax.ppermute(v, 'wide', flip(bit, wide))  10.9 us
    ppermute x5, starting transfers between devices, butterfly(): value = value + lax.ppermute(value, axis, flip(bit, size))  4.96 us
  transfers between devices with their start and end apart: 35, of which 22 were waited for; matrix products, arithmetic and copies ran while one was open for 3% of the time, Pallas kernels for 25%

profile of v1, /device:TPU:0, one launch (start us, length us, event | category | flops | bytes accessed | tf_op | source)
XLA Modules:
  0.0 222.4 jit_solution(8387641137674851947)
XLA Ops:
  2.0 7.3 %self_fwd.1 = (bf16[3,512,192]{2,1,0:T(8,128)(2,1)}, bf16[3,512,512]{2,1,0:T(8,128)(2,1)}, bf16[512,192]{1,0:T(8,128)(2,1)}, bf16[256,768]{1,0:T(8,128)(2,1)}, f32[256,768]{1,0:T(8,128)}) custom-call(s32[7]{0:T(128)} %stack.33.at_ref, bf16[512,768]{1,0:T(8,128)(2,1)} %refs_5_.7, bf16[3,192,768]{2,1,0:T(8,128)(2,1)} %bitcast.30, bf16[192,768]{1,0:T(8,128)(2,1)} %refs_2_.11, ...), custom_call_target="tpu_custom_call" | custom-call | flops 440000000 | bytes 1000 | tf_op jit(solution)/shard_map/self_fwd/pallas_call | solution.py:160
  9.9 2.6 %collective-permute-start.2 = (bf16[416,768]{1,0:T(8,128)(2,1)S(1)}, bf16[416,768]{1,0:T(8,128)(2,1)S(1)}, u32[]{:S(2)}, u32[]{:S(2)}) collective-permute-start(bf16[416,768]{1,0:T(8,128)(2,1)S(1)} %bitcast.32), channel_id=1, source_target_pairs={{0,2},{1,3},{2,0},{3,1},{4,6},{5,7},{6,4},{7,5},{8,10},{9,11},{10,... | collective-permute-start | bytes 1916936 | tf_op jit(solution)/shard_map/ppermute | solution.py:1051
  13.7 1.9 collective-permute-start.1
  15.6 2.8 %copy-done = s32[512,3,4,256]{3,2,1,0:T(4,128)S(1)} copy-done((s32[512,3,4,256]{3,2,1,0:T(4,128)S(1)}, s32[512,3,4,256]{3,2,1,0:T(4,128)}, u32[]{:S(2)}) %copy-start) | copy-done | bytes 6291480
  18.4 9.6 %mask.2.refs_4_ = bf16[3,256,1664]{2,1,0:T(8,128)(2,1)S(1)} custom-call(s32[7]{0:T(128)S(1)} %copy-done.12, s32[4,3072,128]{2,1,0:T(8,128)S(1)} %bitcast.24), custom_call_target="tpu_custom_call" | custom-call | flops 1100000000 | bytes 1000 | tf_op jit(solution)/shard_map/mask/pallas_call | solution.py:160
  28.6 9.6 %mask.3.refs_5_ = bf16[3,256,1664]{2,1,0:T(8,128)(2,1)S(1)} custom-call(s32[7]{0:T(128)S(1)} %copy-done.12, s32[4,3072,128]{2,1,0:T(8,128)S(1)} %bitcast.25), custom_call_target="tpu_custom_call" | custom-call | flops 1100000000 | bytes 1000 | tf_op jit(solution)/shard_map/mask/pallas_call | solution.py:160
  39.5 2.2 %keys_values.1 = (bf16[3,1664,128]{2,1,0:T(8,128)(2,1)S(1)}, bf16[3,1664,128]{2,1,0:T(8,128)(2,1)S(1)}) custom-call(s32[7]{0:T(128)S(1)} %copy-done.12, bf16[416,768]{1,0:T(8,128)(2,1)S(1)} %bitcast.34, bf16[416,768]{1,0:T(8,128)(2,1)S(1)} %collective-permute-done.3.refs_1_, bf16[416,768]{1,0:T(8,128)(2,1)S(1)} %collective-permute-done.2.refs_2_, ...), custom_call_target="tpu_custom_call" | custom-call | flops 220000000 | bytes 1000 | tf_op jit(solution)/shard_map/keys_values/pallas_call | solution.py:160
  41.8 7.8 %cross_fwd.1 = (f32[256,768]{1,0:T(8,128)S(1)}, bf16[256,768]{1,0:T(8,128)(2,1)S(1)}, bf16[3,512,1664]{2,1,0:T(8,128)(2,1)S(1)}, f32[3,512,128]{2,1,0:T(8,128)S(...) custom-call(s32[7]{0:T(128)S(1)} %copy-done.12, bf16[256,768]{1,0:T(8,128)(2,1)S(1)} %get-tuple-element.118.refs_0_.refs_6_, ...), custom_call_target="tpu_custom_call" | custom-call | flops 990000000 | bytes 1000 | tf_op jit(solution)/shard_map/cross_fwd/pallas_call | solution.py:160
  51.5 1.6 collective-permute-start.7
  53.1 9.8 %collective-permute-done.7.refs_2_ = bf16[256,768]{1,0:T(8,128)(2,1)S(1)} collective-permute-done((bf16[256,768]{1,0:T(8,128)(2,1)S(1)}, bf16[256,768]{1,0:T(8,128)(2,1)S(1)}, u32[]{:S(2)}, u32[]{:S(2)}) %collective-permute-start.7) | collective-permute-done | bytes 393248 | tf_op jit(solution)/shard_map/ppermute | solution.py:1051
  64.0 1.7 collective-permute-done.8.refs_1_
  65.7 3.5 %feed_up.1 = (f32[256,768]{1,0:T(8,128)S(1)}, bf16[256,768]{1,0:T(8,128)(2,1)S(1)}, bf16[512,768]{1,0:T(8,128)(2,1)S(1)}, f32[512,768]{1,0:T(8,128)S(1)}) custom-call(s32[7]{0:T(128)S(1)} %copy-done.12, bf16[256,768]{1,0:T(8,128)(2,1)S(1)} %get-tuple-element.128.refs_0_, bf16[256,768]{1,0:T(8,128)(2,1)S(1)} %collective-permute-done.8.refs_1_, ...), custom_call_target="tpu_custom_call" | custom-call | flops 440000000 | bytes 1000 | tf_op jit(solution)/shard_map/feed_up/pallas_call | solution.py:160
  69.5 1.6 collective-permute-done.9
  71.1 1.6 collective-permute-start.10
  72.7 9.6 %collective-permute-done.10.refs_2_ = bf16[256,768]{1,0:T(8,128)(2,1)S(1)} collective-permute-done((bf16[256,768]{1,0:T(8,128)(2,1)S(1)}, bf16[256,768]{1,0:T(8,128)(2,1)S(1)}, u32[]{:S(2)}, u32[]{:S(2)}) %collective-permute-start.10) | collective-permute-done | bytes 393248 | tf_op jit(solution)/shard_map/ppermute | solution.py:1051
  82.4 1.8 third_norm.1
  84.2 1.7 collective-permute-done.11.refs_1_.refs_4_
  85.9 2.1 feed_down.1
  88.3 1.6 collective-permute-done.12
  89.9 1.6 collective-permute-start.13
  91.5 3.4 %feed_grads.1 = (bf16[384,1536]{1,0:T(8,128)(2,1)S(1)}, f32[4,96,1536]{2,1,0:T(8,128)S(1)}) custom-call(s32[7]{0:T(128)S(1)} %copy-done.12, bf16[256,768]{1,0:T(8,128)(2,1)S(1)} %get-tuple-element.128.refs_0_, bf16[256,768]{1,0:T(8,128)(2,1)S(1)} %collective-permute-done.8.refs_1_, bf16[512,768]{1,0:T(8,128)(2,1)S(1)} %get-tuple-element.137.refs_2_, ...), custom_call_target="tpu_custom_call" | custom-call | flops 440000000 | bytes 1000 | tf_op jit(solution)/shard_map/feed_grads/pallas_call | solution.py:160
  95.0 6.2 %collective-permute-done.13.refs_2_ = bf16[256,768]{1,0:T(8,128)(2,1)S(1)} collective-permute-done((bf16[256,768]{1,0:T(8,128)(2,1)S(1)}, bf16[256,768]{1,0:T(8,128)(2,1)S(1)}, u32[]{:S(2)}, u32[]{:S(2)}) %collective-permute-start.13) | collective-permute-done | bytes 393248 | tf_op jit(solution)/shard_map/ppermute | solution.py:1051
  102.6 1.6 collective-permute-start.17
  104.3 10.6 %cross_bwd.1 = (f32[256,768]{1,0:T(8,128)S(1)}, bf16[256,768]{1,0:T(8,128)(2,1)S(1)}, bf16[512,192]{1,0:T(8,128)(2,1)S(1)}, bf16[3,1664,128]{2,1,0:T(8,128)(2,1)S(1)}, f32[2,192]{1,0:T(2,128)S(1)}) custom-call(s32[7]{0:T(128)S(1)} %copy-done.12, bf16[256,768]{1,0:T(8,128)(2,1)S(1)} %get-tuple-element.142.refs_0_.refs_4_, ...), custom_call_target="tpu_custom_call" | custom-call | flops 1210000000 | bytes 1000 | tf_op jit(solution)/shard_map/cross_bwd/pallas_call | solution.py:160
  115.0 1.6 collective-permute-done.15
  116.7 1.6 collective-permute-start.16
  118.3 3.5 %cross_grads.1 = (bf16[384,768]{1,0:T(8,128)(2,1)S(1)}, f32[4,96,768]{2,1,0:T(8,128)S(1)}) custom-call(s32[7]{0:T(128)S(1)} %copy-done.12, bf16[416,768]{1,0:T(8,128)(2,1)S(1)} %bitcast.35, bf16[416,768]{1,0:T(8,128)(2,1)S(1)} %collective-permute-done.3.refs_1_, bf16[416,768]{1,0:T(8,128)(2,1)S(1)} %collective-permute-done.2.refs_2_, ...), custom_call_target="tpu_custom_call" | custom-call | flops 440000000 | bytes 1000 | tf_op jit(solution)/shard_map/cross_grads/pallas_call | solution.py:160
  121.8 9.1 %collective-permute-done.17.refs_1_ = bf16[384,1536]{1,0:T(8,128)(2,1)S(1)} collective-permute-done((bf16[384,1536]{1,0:T(8,128)(2,1)S(1)}, bf16[384,1536]{1,0:T(8,128)(2,1)S(1)}, u32[]{:S(2)}, u32[]{:S(2)}) %collective-permute-start.17) | collective-permute-done | bytes 1179680 | tf_op jit(solution)/shard_map/ppermute | solution.py:1054
  131.7 2.1 store_grad.1
  135.2 1.7 collective-permute-done.18.refs_1_
  137.1 1.6 collective-permute-start.20
  138.7 1.6 collective-permute-start.21
  140.3 5.5 %self_bwd.1 = (bf16[512,768]{1,0:T(8,128)(2,1)S(1)}, f32[256,768]{1,0:T(8,128)S(1)}, bf16[384,768]{1,0:T(8,128)(2,1)S(1)}, f32[4,96,768]{2,1,0:T(8,128)S(1)}, f32[16,768]{1,0:T(8,128)S(1)}) custom-call(s32[7]{0:T(128)S(1)} %copy-done.12, bf16[256,768]{1,0:T(8,128)(2,1)S(1)} %get-tuple-element.161.refs_0_, ...), custom_call_target="tpu_custom_call" | custom-call | flops 660000000 | bytes 1000 | tf_op jit(solution)/shard_map/self_bwd/pallas_call | solution.py:160
  145.9 6.8 %collective-permute-done.20.refs_2_ = bf16[384,768]{1,0:T(8,128)(2,1)S(1)} collective-permute-done((bf16[384,768]{1,0:T(8,128)(2,1)S(1)}, bf16[384,768]{1,0:T(8,128)(2,1)S(1)}, u32[]{:S(2)}, u32[]{:S(2)}) %collective-permute-start.20) | collective-permute-done | bytes 589856 | tf_op jit(solution)/shard_map/ppermute | solution.py:1054
  155.3 1.8 collective-permute-done.22.refs_1_
  157.2 1.6 collective-permute-start.23
  158.7 2.6 %collective-permute-start.24 = (bf16[96,1536]{1,0:T(8,128)(2,1)S(1)}, bf16[96,1536]{1,0:T(8,128)(2,1)S(1)}, u32[]{:S(2)}, u32[]{:S(2)}) collective-permute-start(bf16[96,1536]{1,0:T(8,128)(2,1)S(1)} %get-tuple-element.179), channel_id=1, source_target_pairs={{0,16},{4,20},{8,24},{12,28},{16,0},{20,4},{24,8},{28,12},{1,17},{... | collective-permute-start | bytes 884744 | tf_op jit(solution)/shard_map/ppermute | solution.py:1054
  161.3 13.4 %collective-permute-done.24.refs_1_ = bf16[96,1536]{1,0:T(8,128)(2,1)S(1)} collective-permute-done((bf16[96,1536]{1,0:T(8,128)(2,1)S(1)}, bf16[96,1536]{1,0:T(8,128)(2,1)S(1)}, u32[]{:S(2)}, u32[]{:S(2)}) %collective-permute-start.24) | collective-permute-done | bytes 294944 | tf_op jit(solution)/shard_map/ppermute | solution.py:1054
  179.0 3.4 %collective-permute-done.28 = f32[9,768]{1,0:T(8,128)S(1)} collective-permute-done((f32[9,768]{1,0:T(8,128)S(1)}, f32[9,768]{1,0:T(8,128)S(1)}, u32[]{:S(2)}, u32[]{:S(2)}) %collective-permute-start.28) | collective-permute-done | bytes 27680 | tf_op jit(solution)/shard_map/ppermute | solution.py:1005
  184.2 3.6 %collective-permute-done.30 = f32[16,768]{1,0:T(8,128)S(1)} collective-permute-done((f32[16,768]{1,0:T(8,128)S(1)}, f32[16,768]{1,0:T(8,128)S(1)}, u32[]{:S(2)}, u32[]{:S(2)}) %collective-permute-start.30) | collective-permute-done | bytes 49184 | tf_op jit(solution)/shard_map/ppermute | solution.py:1005
  189.2 8.8 %collective-permute-done.31 = f32[16,768]{1,0:T(8,128)S(1)} collective-permute-done((f32[16,768]{1,0:T(8,128)S(1)}, f32[16,768]{1,0:T(8,128)S(1)}, u32[]{:S(2)}, u32[]{:S(2)}) %collective-permute-start.31) | collective-permute-done | bytes 49184 | tf_op jit(solution)/shard_map/ppermute | solution.py:1005
  198.0 2.4 %collective-permute-start.32 = (f32[16,768]{1,0:T(8,128)S(1)}, f32[16,768]{1,0:T(8,128)S(1)}, u32[]{:S(2)}, u32[]{:S(2)}) collective-permute-start(f32[16,768]{1,0:T(8,128)S(1)} %add.82), channel_id=1, source_target_pairs={{0,16},{4,20},{8,24},{12,28},{16,0},{20,4},{24,8},{28,12},{1,17},{... | collective-permute-start | bytes 147464 | tf_op jit(solution)/shard_map/ppermute | solution.py:1005
  200.4 1.5 join_halves.2
  203.1 1.8 join_halves.3
  207.8 2.3 %collective-permute-start.34 = (bf16[96,1536]{1,0:T(8,128)(2,1)}, bf16[96,1536]{1,0:T(8,128)(2,1)S(1)}, u32[]{:S(2)}, u32[]{:S(2)}) collective-permute-start(bf16[96,1536]{1,0:T(8,128)(2,1)} %get-tuple-element.197), channel_id=1, source_target_pairs={{0,16},{4,20},{8,24},{12,28},{16,0},{20,4},{24,8},{28,12},{1,17},{... | collective-permute-start | bytes 884744 | tf_op jit(solution)/shard_map/ppermute | solution.py:1054
  212.0 2.5 %fusion = f32[1,416,768]{2,1,0:T(8,128)} fusion(bf16[416,768]{1,0:T(8,128)(2,1)} %copy-done.18, f32[2,416,768]{2,1,0:T(8,128)S(1)} %get-tuple-element.192, bf16[2,416,768]{2,1,0:T(8,128)(2,1)} %copy-done.17), kind=kLoop, calls=%fused_computation.1 | loop fusion | flops 1277952 | bytes 3833856 | tf_op jit(solution)/shard_map/broadcast_in_dim | solution.py:1158
  214.6 6.1 %collective-permute-done.34.refs_1_ = bf16[96,1536]{1,0:T(8,128)(2,1)S(1)} collective-permute-done((bf16[96,1536]{1,0:T(8,128)(2,1)}, bf16[96,1536]{1,0:T(8,128)(2,1)S(1)}, u32[]{:S(2)}, u32[]{:S(2)}) %collective-permute-start.34) | collective-permute-done | bytes 294944 | tf_op jit(solution)/shard_map/ppermute | solution.py:1054
  220.7 1.5 last_stage.3
  (119 shorter events, 27.9 us)
Async XLA Ops:
  0.7 9.2 %copy-start.6 = (bf16[1,416,768]{2,1,0:T(8,128)(2,1)S(1)}, bf16[1,416,768]{2,1,0:T(8,128)(2,1)}, u32[]{:S(2)}) copy-start(bf16[1,416,768]{2,1,0:T(8,128)(2,1)} %param.20) | copy-start | bytes 1916932
  9.4 3.1 %collective-permute-start = (bf16[256,768]{1,0:T(8,128)(2,1)}, bf16[256,768]{1,0:T(8,128)(2,1)S(1)}, u32[]{:S(2)}, u32[]{:S(2)}) collective-permute-start(bf16[256,768]{1,0:T(8,128)(2,1)} %get-tuple-element.113), channel_id=1, source_target_pairs={{0,1},{1,0},{2,3},{3,2},{4,5},{5,4},{6,7},{7,6},{8,9},{9,8},{10,11... | collective-permute-start | bytes 1179656 | tf_op jit(solution)/shard_map/ppermute | solution.py:1048
  9.9 18.1 %collective-permute-start.2 = (bf16[416,768]{1,0:T(8,128)(2,1)S(1)}, bf16[416,768]{1,0:T(8,128)(2,1)S(1)}, u32[]{:S(2)}, u32[]{:S(2)}) collective-permute-start(bf16[416,768]{1,0:T(8,128)(2,1)S(1)} %bitcast.32), channel_id=1, source_target_pairs={{0,2},{1,3},{2,0},{3,1},{4,6},{5,7},{6,4},{7,5},{8,10},{9,11},{10,... | collective-permute-start | bytes 1916936 | tf_op jit(solution)/shard_map/ppermute | solution.py:1051
  13.7 24.6 %collective-permute-start.1 = (bf16[256,768]{1,0:T(8,128)(2,1)S(1)}, bf16[256,768]{1,0:T(8,128)(2,1)S(1)}, u32[]{:S(2)}, u32[]{:S(2)}) collective-permute-start(bf16[256,768]{1,0:T(8,128)(2,1)S(1)} %add_convert_fusion.6.refs_0_), channel_id=1, source_target_pairs={{0,2},{1,3},{2,0},{3,1},{4,6},{5,7},{6,4},{7,5},{8,10},{9,11},{10,... | collective-permute-start | bytes 1179656 | tf_op jit(solution)/shard_map/ppermute | solution.py:1051
  18.4 10.2 %copy-start.19 = (f32[768]{0:T(1024)S(1)}, f32[768]{0:T(1024)}, u32[]{:S(2)}) copy-start(f32[768]{0:T(1024)} %param.27) | copy-start | bytes 9220
  28.0 11.4 %collective-permute-start.3 = (bf16[416,768]{1,0:T(8,128)(2,1)S(1)}, bf16[416,768]{1,0:T(8,128)(2,1)S(1)}, u32[]{:S(2)}, u32[]{:S(2)}) collective-permute-start(bf16[416,768]{1,0:T(8,128)(2,1)S(1)} %bitcast.33), channel_id=1, source_target_pairs={{0,1},{1,0},{2,3},{3,2},{4,5},{5,4},{6,7},{7,6},{8,9},{9,8},{10,11... | collective-permute-start | bytes 1916936 | tf_op jit(solution)/shard_map/ppermute | solution.py:1048
  28.1 11.3 %collective-permute-start.4 = (bf16[416,768]{1,0:T(8,128)(2,1)S(1)}, bf16[416,768]{1,0:T(8,128)(2,1)S(1)}, u32[]{:S(2)}, u32[]{:S(2)}) collective-permute-start(bf16[416,768]{1,0:T(8,128)(2,1)S(1)} %collective-permute-done.2.refs_2_), channel_id=1, source_target_pairs={{0,1},{1,0},{2,3},{3,2},{4,5},{5,4},{6,7},{7,6},{8,9},{9,8},{10,11... | collective-permute-start | bytes 1916936 | tf_op jit(solution)/shard_map/ppermute | solution.py:1048
  28.6 9.7 %copy-start.2 = (bf16[512,768]{1,0:T(8,128)(2,1)S(1)}, bf16[512,768]{1,0:T(8,128)(2,1)}, u32[]{:S(2)}) copy-start(bf16[512,768]{1,0:T(8,128)(2,1)} %refs_5_.7) | copy-start | bytes 2359300
  28.6 9.7 %copy-start.13 = (f32[3,768]{1,0:T(4,128)S(1)}, f32[3,768]{1,0:T(4,128)}, u32[]{:S(2)}) copy-start(f32[3,768]{1,0:T(4,128)} %refs_4_.7) | copy-start | bytes 27652
  28.6 9.7 %copy-start.15 = (f32[3,768]{1,0:T(4,128)S(1)}, f32[3,768]{1,0:T(4,128)}, u32[]{:S(2)}) copy-start(f32[3,768]{1,0:T(4,128)} %refs_6_.1) | copy-start | bytes 27652
  39.3 2.4 %collective-permute-start.5 = (bf16[256,768]{1,0:T(8,128)(2,1)S(1)}, bf16[256,768]{1,0:T(8,128)(2,1)S(1)}, u32[]{:S(2)}, u32[]{:S(2)}) collective-permute-start(bf16[256,768]{1,0:T(8,128)(2,1)S(1)} %get-tuple-element.118.refs_0_.refs_6_), channel_id=1, source_target_pairs={{0,1},{1,0},{2,3},{3,2},{4,5},{5,4},{6,7},{7,6},{8,9},{9,8},{10,11... | collective-permute-start | bytes 1179656 | tf_op jit(solution)/shard_map/ppermute | solution.py:1048
  49.6 1.9 collective-permute-start.6
  51.4 12.6 %copy-start.21 = (f32[768]{0:T(1024)S(1)}, f32[768]{0:T(1024)}, u32[]{:S(2)}) copy-start(f32[768]{0:T(1024)} %param.33) | copy-start | bytes 9220
  51.4 14.3 %copy-start.3 = (bf16[768,768]{1,0:T(8,128)(2,1)S(1)}, bf16[768,768]{1,0:T(8,128)(2,1)}, u32[]{:S(2)}) copy-start(bf16[768,768]{1,0:T(8,128)(2,1)} %refs_2_.9) | copy-start | bytes 3538948
  51.4 14.3 %copy-start.4 = (bf16[768,768]{1,0:T(8,128)(2,1)S(1)}, bf16[768,768]{1,0:T(8,128)(2,1)}, u32[]{:S(2)}) copy-start(bf16[768,768]{1,0:T(8,128)(2,1)} %refs_3_.7) | copy-start | bytes 3538948
  51.5 11.5 %collective-permute-start.7 = (bf16[256,768]{1,0:T(8,128)(2,1)S(1)}, bf16[256,768]{1,0:T(8,128)(2,1)S(1)}, u32[]{:S(2)}, u32[]{:S(2)}) collective-permute-start(bf16[256,768]{1,0:T(8,128)(2,1)S(1)} %add_convert_fusion.5.refs_1_), channel_id=1, source_target_pairs={{0,2},{1,3},{2,0},{3,1},{4,6},{5,7},{6,4},{7,5},{8,10},{9,11},{10,... | collective-permute-start | bytes 1179656 | tf_op jit(solution)/shard_map/ppermute | solution.py:1051
  63.9 1.8 collective-permute-start.8
  69.3 13.1 %copy-start.10 = (bf16[512,768]{1,0:T(8,128)(2,1)S(1)}, bf16[512,768]{1,0:T(8,128)(2,1)}, u32[]{:S(2)}) copy-start(bf16[512,768]{1,0:T(8,128)(2,1)} %refs_3_.6) | copy-start | bytes 2359300
  69.3 1.8 collective-permute-start.9
  71.1 11.2 %collective-permute-start.10 = (bf16[256,768]{1,0:T(8,128)(2,1)S(1)}, bf16[256,768]{1,0:T(8,128)(2,1)S(1)}, u32[]{:S(2)}, u32[]{:S(2)}) collective-permute-start(bf16[256,768]{1,0:T(8,128)(2,1)S(1)} %add_convert_fusion.4.refs_1_), channel_id=1, source_target_pairs={{0,2},{1,3},{2,0},{3,1},{4,6},{5,7},{6,4},{7,5},{8,10},{9,11},{10,... | collective-permute-start | bytes 1179656 | tf_op jit(solution)/shard_map/ppermute | solution.py:1051
  84.1 1.8 collective-permute-start.11
  88.0 1.8 collective-permute-start.12
  89.9 11.2 %collective-permute-start.13 = (bf16[256,768]{1,0:T(8,128)(2,1)S(1)}, bf16[256,768]{1,0:T(8,128)(2,1)S(1)}, u32[]{:S(2)}, u32[]{:S(2)}) collective-permute-start(bf16[256,768]{1,0:T(8,128)(2,1)S(1)} %add_convert_fusion.3.refs_1_), channel_id=1, source_target_pairs={{0,2},{1,3},{2,0},{3,1},{4,6},{5,7},{6,4},{7,5},{8,10},{9,11},{10,... | collective-permute-start | bytes 1179656 | tf_op jit(solution)/shard_map/ppermute | solution.py:1051
  102.5 1.8 collective-permute-start.14
  102.6 28.4 %collective-permute-start.17 = (bf16[384,1536]{1,0:T(8,128)(2,1)S(1)}, bf16[384,1536]{1,0:T(8,128)(2,1)S(1)}, u32[]{:S(2)}, u32[]{:S(2)}) collective-permute-start(bf16[384,1536]{1,0:T(8,128)(2,1)S(1)} %get-tuple-element.139), channel_id=1, source_target_pairs={{0,4},{4,0},{8,12},{12,8},{16,20},{20,16},{24,28},{28,24},{1,5},{5... | collective-permute-start | bytes 3538952 | tf_op jit(solution)/shard_map/ppermute | solution.py:1054
  114.8 1.8 collective-permute-start.15
  116.7 17.1 %collective-permute-start.16 = (bf16[256,768]{1,0:T(8,128)(2,1)S(1)}, bf16[256,768]{1,0:T(8,128)(2,1)S(1)}, u32[]{:S(2)}, u32[]{:S(2)}) collective-permute-start(bf16[256,768]{1,0:T(8,128)(2,1)S(1)} %add_convert_fusion.2.refs_1_), channel_id=1, source_target_pairs={{0,2},{1,3},{2,0},{3,1},{4,6},{5,7},{6,4},{7,5},{8,10},{9,11},{10,... | collective-permute-start | bytes 1179656 | tf_op jit(solution)/shard_map/ppermute | solution.py:1051
  131.7 8.6 %copy-start.7 = (bf16[3,512,512]{2,1,0:T(8,128)(2,1)S(1)}, bf16[3,512,512]{2,1,0:T(8,128)(2,1)}, u32[]{:S(2)}) copy-start(bf16[3,512,512]{2,1,0:T(8,128)(2,1)} %get-tuple-element.165.refs_4_) | copy-start | bytes 4718596
  133.8 6.5 %copy-start.5 = (bf16[3,768,192]{1,2,0:T(8,128)(2,1)S(1)}, bf16[3,768,192]{1,2,0:T(8,128)(2,1)}, u32[]{:S(2)}) copy-start(bf16[3,768,192]{1,2,0:T(8,128)(2,1)} %param.24) | copy-start | bytes 2654212
  133.8 6.5 %copy-start.9 = (bf16[192,768]{1,0:T(8,128)(2,1)S(1)}, bf16[192,768]{1,0:T(8,128)(2,1)}, u32[]{:S(2)}) copy-start(bf16[192,768]{1,0:T(8,128)(2,1)} %refs_2_.11) | copy-start | bytes 884740
  135.2 1.8 collective-permute-start.18
  137.0 3.3 %collective-permute-start.19 = (bf16[2,416,768]{2,1,0:T(8,128)(2,1)S(1)}, bf16[2,416,768]{2,1,0:T(8,128)(2,1)S(1)}, u32[]{:S(2)}, u32[]{:S(2)}) collective-permute-start(bf16[2,416,768]{2,1,0:T(8,128)(2,1)S(1)} %get-tuple-element.162), channel_id=1, source_target_pairs={{0,1},{1,0},{2,3},{3,2},{4,5},{5,4},{6,7},{7,6},{8,9},{9,8},{10,11... | collective-permute-start | bytes 3833864 | tf_op jit(solution)/shard_map/ppermute | solution.py:1048
  137.1 15.6 %collective-permute-start.20 = (bf16[384,768]{1,0:T(8,128)(2,1)S(1)}, bf16[384,768]{1,0:T(8,128)(2,1)S(1)}, u32[]{:S(2)}, u32[]{:S(2)}) collective-permute-start(bf16[384,768]{1,0:T(8,128)(2,1)S(1)} %get-tuple-element.152), channel_id=1, source_target_pairs={{0,4},{4,0},{8,12},{12,8},{16,20},{20,16},{24,28},{28,24},{1,5},{5... | collective-permute-start | bytes 1769480 | tf_op jit(solution)/shard_map/ppermute | solution.py:1054
  138.7 15.3 %collective-permute-start.21 = (bf16[192,1536]{1,0:T(8,128)(2,1)S(1)}, bf16[192,1536]{1,0:T(8,128)(2,1)S(1)}, u32[]{:S(2)}, u32[]{:S(2)}) collective-permute-start(bf16[192,1536]{1,0:T(8,128)(2,1)S(1)} %get-tuple-element.155), channel_id=1, source_target_pairs={{0,8},{4,12},{8,0},{12,4},{16,24},{20,28},{24,16},{28,20},{1,9},{5... | collective-permute-start | bytes 1769480 | tf_op jit(solution)/shard_map/ppermute | solution.py:1054
  140.3 38.6 %copy-start.17 = (bf16[2,416,768]{2,1,0:T(8,128)(2,1)}, bf16[2,416,768]{2,1,0:T(8,128)(2,1)S(1)}, u32[]{:S(2)}) copy-start(bf16[2,416,768]{2,1,0:T(8,128)(2,1)S(1)} %collective-permute-done.19) | copy-start | bytes 3833860
  154.7 2.4 %collective-permute-start.22 = (bf16[512,768]{1,0:T(8,128)(2,1)S(1)}, bf16[512,768]{1,0:T(8,128)(2,1)S(1)}, u32[]{:S(2)}, u32[]{:S(2)}) collective-permute-start(bf16[512,768]{1,0:T(8,128)(2,1)S(1)} %get-tuple-element.180), channel_id=1, source_target_pairs={{0,1},{1,0},{2,3},{3,2},{4,5},{5,4},{6,7},{7,6},{8,9},{9,8},{10,11... | collective-permute-start | bytes 2359304 | tf_op jit(solution)/shard_map/ppermute | solution.py:1048
  154.8 21.3 %collective-permute-start.25 = (bf16[384,768]{1,0:T(8,128)(2,1)S(1)}, bf16[384,768]{1,0:T(8,128)(2,1)S(1)}, u32[]{:S(2)}, u32[]{:S(2)}) collective-permute-start(bf16[384,768]{1,0:T(8,128)(2,1)S(1)} %get-tuple-element.187), channel_id=1, source_target_pairs={{0,4},{4,0},{8,12},{12,8},{16,20},{20,16},{24,28},{28,24},{1,5},{5... | collective-permute-start | bytes 1769480 | tf_op jit(solution)/shard_map/ppermute | solution.py:1054
  157.2 19.8 %collective-permute-start.23 = (bf16[256,768]{1,0:T(8,128)(2,1)S(1)}, bf16[256,768]{1,0:T(8,128)(2,1)S(1)}, u32[]{:S(2)}, u32[]{:S(2)}) collective-permute-start(bf16[256,768]{1,0:T(8,128)(2,1)S(1)} %add_convert_fusion.1), channel_id=1, source_target_pairs={{0,2},{1,3},{2,0},{3,1},{4,6},{5,7},{6,4},{7,5},{8,10},{9,11},{10,... | collective-permute-start | bytes 1179656 | tf_op jit(solution)/shard_map/ppermute | solution.py:1051
  158.7 16.0 %collective-permute-start.24 = (bf16[96,1536]{1,0:T(8,128)(2,1)S(1)}, bf16[96,1536]{1,0:T(8,128)(2,1)S(1)}, u32[]{:S(2)}, u32[]{:S(2)}) collective-permute-start(bf16[96,1536]{1,0:T(8,128)(2,1)S(1)} %get-tuple-element.179), channel_id=1, source_target_pairs={{0,16},{4,20},{8,24},{12,28},{16,0},{20,4},{24,8},{28,12},{1,17},{... | collective-permute-start | bytes 884744 | tf_op jit(solution)/shard_map/ppermute | solution.py:1054
  176.9 1.3 collective-permute-start.27
  177.2 25.9 %collective-permute-start.26 = (f32[256,768]{1,0:T(8,128)S(1)}, f32[256,768]{1,0:T(8,128)S(1)}, u32[]{:S(2)}, u32[]{:S(2)}) collective-permute-start(f32[256,768]{1,0:T(8,128)S(1)} %add_add_fusion.refs_0_), channel_id=1, source_target_pairs={{0,1},{1,0},{2,3},{3,2},{4,5},{5,4},{6,7},{7,6},{8,9},{9,8},{10,11... | collective-permute-start | bytes 2359304 | tf_op jit(solution)/shard_map/ppermute | solution.py:1048
  178.3 4.2 %collective-permute-start.28 = (f32[9,768]{1,0:T(8,128)S(1)}, f32[9,768]{1,0:T(8,128)S(1)}, u32[]{:S(2)}, u32[]{:S(2)}) collective-permute-start(f32[9,768]{1,0:T(8,128)S(1)} %slice_add_fusion), channel_id=1, source_target_pairs={{0,2},{1,3},{2,0},{3,1},{4,6},{5,7},{6,4},{7,5},{8,10},{9,11},{10,... | collective-permute-start | bytes 82952 | tf_op jit(solution)/shard_map/ppermute | solution.py:1005
  182.4 23.8 %collective-permute-start.29 = (bf16[416,768]{1,0:T(8,128)(2,1)S(1)}, bf16[416,768]{1,0:T(8,128)(2,1)S(1)}, u32[]{:S(2)}, u32[]{:S(2)}) collective-permute-start(bf16[416,768]{1,0:T(8,128)(2,1)S(1)} %fusion.1), channel_id=1, source_target_pairs={{0,2},{1,3},{2,0},{3,1},{4,6},{5,7},{6,4},{7,5},{8,10},{9,11},{10,... | collective-permute-start | bytes 1916936 | tf_op jit(solution)/shard_map/ppermute | solution.py:1051
  183.0 21.8 %collective-permute-start.33 = (bf16[192,1536]{1,0:T(8,128)(2,1)S(1)}, bf16[192,1536]{1,0:T(8,128)(2,1)S(1)}, u32[]{:S(2)}, u32[]{:S(2)}) collective-permute-start(bf16[192,1536]{1,0:T(8,128)(2,1)S(1)} %get-tuple-element.188), channel_id=1, source_target_pairs={{0,8},{4,12},{8,0},{12,4},{16,24},{20,28},{24,16},{28,20},{1,9},{5... | collective-permute-start | bytes 1769480 | tf_op jit(solution)/shard_map/ppermute | solution.py:1054
  183.7 4.1 %collective-permute-start.30 = (f32[16,768]{1,0:T(8,128)S(1)}, f32[16,768]{1,0:T(8,128)S(1)}, u32[]{:S(2)}, u32[]{:S(2)}) collective-permute-start(f32[16,768]{1,0:T(8,128)S(1)} %pad_maximum_fusion), channel_id=1, source_target_pairs={{0,4},{4,0},{8,12},{12,8},{16,20},{20,16},{24,28},{28,24},{1,5},{5... | collective-permute-start | bytes 147464 | tf_op jit(solution)/shard_map/ppermute | solution.py:1005
  187.8 10.2 %collective-permute-start.31 = (f32[16,768]{1,0:T(8,128)S(1)}, f32[16,768]{1,0:T(8,128)S(1)}, u32[]{:S(2)}, u32[]{:S(2)}) collective-permute-start(f32[16,768]{1,0:T(8,128)S(1)} %add.81), channel_id=1, source_target_pairs={{0,8},{4,12},{8,0},{12,4},{16,24},{20,28},{24,16},{28,20},{1,9},{5... | collective-permute-start | bytes 147464 | tf_op jit(solution)/shard_map/ppermute | solution.py:1005
  198.0 5.0 %collective-permute-start.32 = (f32[16,768]{1,0:T(8,128)S(1)}, f32[16,768]{1,0:T(8,128)S(1)}, u32[]{:S(2)}, u32[]{:S(2)}) collective-permute-start(f32[16,768]{1,0:T(8,128)S(1)} %add.82), channel_id=1, source_target_pairs={{0,16},{4,20},{8,24},{12,28},{16,0},{20,4},{24,8},{28,12},{1,17},{... | collective-permute-start | bytes 147464 | tf_op jit(solution)/shard_map/ppermute | solution.py:1005
  207.8 12.9 %collective-permute-start.34 = (bf16[96,1536]{1,0:T(8,128)(2,1)}, bf16[96,1536]{1,0:T(8,128)(2,1)S(1)}, u32[]{:S(2)}, u32[]{:S(2)}) collective-permute-start(bf16[96,1536]{1,0:T(8,128)(2,1)} %get-tuple-element.197), channel_id=1, source_target_pairs={{0,16},{4,20},{8,24},{12,28},{16,0},{20,4},{24,8},{28,12},{1,17},{... | collective-permute-start | bytes 884744 | tf_op jit(solution)/shard_map/ppermute | solution.py:1054
  (10 other events, 35.6 us)

commit v2 on v0

--- a/solution.py
+++ b/solution.py
@@ -479,12 +479,6 @@
     )
 
 
-def counted_rows(at, half):
-    rows = half // 2
-    place = lax.broadcasted_iota(jnp.int32, (half, 1), 0)
-    return ((place >= at[1] * rows) & (place < (at[1] + 1) * rows)).astype(F32)
-
-
 def stacked_sums(*values):
     sums = [column_sum(value) for value in values]
     return jnp.concatenate(sums + [jnp.zeros((8 - len(sums), values[0].shape[1]), F32)], axis=0)
@@ -545,8 +539,7 @@
         dlast = norm_backward(delta, normed, inverse, gain[2:3])
         dlast_out[...] = dlast
         low[...] = dlast.astype(BF)
-        counted = counted_rows(at, half)
-        sums[...] = stacked_sums(delta * normed * counted, delta * counted, dlast * counted)
+        sums[...] = stacked_sums(delta * normed, delta, dlast)
 
     ins = [
         near(total),
@@ -599,8 +592,7 @@
         result = norm_backward(dmid, normed, inverse, gain[1:2])
         dsecond[...] = result
         low[...] = result.astype(BF)
-        counted = counted_rows(at, half)
-        sums[...] = stacked_sums(dmid * normed * counted, dmid * counted, result * counted)
+        sums[...] = stacked_sums(dmid * normed, dmid, result)
 
     ins = [near(a) for a in (dlast, mine, other, total, gain)]
     outs = [shape(half, width), shape(half, width, dtype=BF), shape(8, width)]
@@ -720,11 +712,11 @@
     )
 
 
-def group_outs(width, columns, blocks):
+def group_outs(width, columns, blocks, tail=0):
     if not blocks:
         return [shape(width, columns)]
     n, r = blocks
-    return [shape(n * r, columns, dtype=BF), shape(n, r, columns)]
+    return [shape(n * r + tail, columns, dtype=BF), shape(n, r, columns)]
 
 
 def emit_group(at, grad, outs, blocks, first, columns, kept_first=None):
@@ -826,8 +818,7 @@
         result = norm_backward(value, normed, inverse, gain[0:1])
         dfirst[...] = result
         low[...] = result.astype(BF)
-        counted = counted_rows(at, half)
-        sums[...] = stacked_sums(value * normed * counted, value * counted, result * counted)
+        sums[...] = stacked_sums(value * normed, value, result)
 
     ins = [near(a) for a in (dsecond, mine, other, total, gain)]
     outs = [shape(half, width), shape(half, width, dtype=BF), shape(8, width)]
@@ -843,7 +834,7 @@
 
     def body(at, ins, outs, scratch):
         mine, other, wo, qkv, prob, tok, w, mixed, flat = ins[:9]
-        third_sums, second_sums, first_sums, fc1_sum, head_sums = ins[9:]
+        third_sums, second_sums, first_sums, third_other, second_other, first_other, fc1_sum, head_sums = ins[9:]
         send, keep = outs[0:2]
         group, extra = outs[2:-1], outs[-1]
         z, dqkv, grad = scratch
@@ -874,11 +865,11 @@
         grad[...] = mm(z[...], flat[...], TN)
         emit_group(at, grad, group, blocks, 3 * local, local)
         pad = jnp.zeros((1, width - 2 * local), F32)
-        extra[...] = jnp.concatenate(
+        small = jnp.concatenate(
             [
-                third_sums[0:3],
-                second_sums[0:3],
-                first_sums[0:3],
+                third_sums[0:3] + third_other[0:3],
+                second_sums[0:3] + second_other[0:3],
+                first_sums[0:3] + first_other[0:3],
                 fc1_sum[...],
                 jnp.concatenate([head_sums[0:1], head_sums[1:2], pad], axis=1),
                 jnp.concatenate([column_sum(dquery), column_sum(dvalue), pad], axis=1),
@@ -886,6 +877,9 @@
             ],
             axis=0,
         )
+        extra[...] = small
+        if blocks:
+            group[0][blocks[0] * blocks[1] :, :] = two_terms(small)
         send[half:, :] = mixed[...]
         for place, out in ((distant, send), (own, keep)):
             total = mm(dqkv[0, place, :], w[0]) + mm(dqkv[1, place, :], w[1]) + mm(dqkv[2, place, :], w[2])
@@ -897,7 +891,7 @@
         at,
         [near(a) for a in (mine, other, wo, qkv, prob, tokens, w, mixed, flat, *sums)],
         [shape(2 * half, width, dtype=BF), shape(half, width)]
-        + group_outs(width, 4 * local, blocks)
+        + group_outs(width, 4 * local, blocks, 2 * EXTRA)
         + [shape(EXTRA, width)],
         scratch=[
             pltpu.VMEM((rows, width), BF),
@@ -909,14 +903,29 @@
     )
 
 
-def add_stage(at, keep, got, small, bit, apart=False):
+def fold_lines(value, columns):
+    rows, width = value.shape
+    times = columns // width
+    each = rows // times
+    return value if times == 1 else jnp.concatenate([value[i * each : (i + 1) * each] for i in range(times)], axis=1)
+
+
+def unfold_lines(value, width):
+    times = value.shape[1] // width
+    return (
+        value
+        if times == 1
+        else jnp.concatenate([value[:, i * width : (i + 1) * width] for i in range(times)], axis=0)
+    )
+
+
+def add_stage(at, keep, got, small, bit):
     n, rows, _ = keep[0].shape
     starts = [0]
     for part in keep:
         starts.append(starts[-1] + part.shape[2])
     columns = starts[-1]
-    tail = 0 if small is None else 2 * small.shape[0]
-    reach = small.shape[1] if tail else 0
+    tail = 0 if small is None else 2 * small.shape[0] * small.shape[1] // columns
 
     def body(at, ins, outs, _):
         keeps, gots = ins[: len(keep)], ins[len(keep) : len(keep) + len(got)]
@@ -937,18 +946,14 @@
                     else:
                         stay[b, :, span] = value
         if tail:
-            total = ins[-1][...]
-            if not apart:
-                total = total + from_terms(gots[0][n * rows :, 0:reach])
+            total = ins[-1][...] + unfold_lines(from_terms(gots[-1][n * rows :, :]), small.shape[1])
             outs[2][...] = total
-            send[n // 2 * rows :, 0:reach] = two_terms(total)
-            if reach < columns:
-                send[n // 2 * rows :, reach:] = jnp.zeros((tail, columns - reach), BF)
+            send[n // 2 * rows :, :] = two_terms(fold_lines(total, columns))
 
     ins = [near(part) for part in (*keep, *got)] + ([near(small)] if tail else [])
     outs = [shape(n // 2 * rows + tail, columns, dtype=BF), shape(n // 2, rows, columns)]
     if tail:
-        outs.append(shape(small.shape[0], reach))
+        outs.append(shape(*small.shape))
     return launch(body, "add_stage", at, ins, outs, us=1)
 
 
@@ -969,7 +974,7 @@
                     out[i] = total[:, (first + i) * each : (first + i + 1) * each]
             first += count
         if reach:
-            outs[-1][...] = ins[2][...] + from_terms(ins[1][rows:, 0:reach])
+            outs[-1][...] = ins[2][...] + unfold_lines(from_terms(ins[1][rows:, :]), reach)
 
     outs = []
     for count, turned in parts:
@@ -1082,14 +1087,14 @@
     mixed_half, dlast, dlast_low, third_sums = third_norm(
         at, second_total, mine, to_across(mine), cotangent, row(fc2_bias), norm_gain, norm_shift
     )
-    dlast_other = to_core(dlast_low)
+    dlast_other, third_other = to_core(dlast_low), to_core(third_sums)
     keep, send, dpre, fc1_sum = feed_down(at, dlast_low, dlast_other, fc1_weight, fc2_weight, slope)
     mine = chip_sum(keep, send)
     other = to_across(mine)
     feed_out = feed_grads(tie(at, mine), mid_low, mid_other, dpre, dlast_low, dlast_other, hidden, blocks)
     other = tie(other, feed_out[0])
     dsecond, z, second_sums = second_back(at, dlast, mine, other, second_total, norm_gain)
-    z_other = to_core(z)
+    z_other, second_other = to_core(z), to_core(second_sums)
 
     keep, send, dquery, dkv, cross_sums = cross_backward(
         at, z, z_other, raised, inverse, query, keys, values, cross_w, out_weight, nh
@@ -1107,7 +1112,7 @@
     store_keep, store_send = store_gradient(tie(at, started), dkv, cross_w, nh)
     other = tie(other, store_send)
     dfirst, dfirst_low, first_sums = first_back(at, dsecond, mine, other, first_total, norm_gain)
-    dfirst_other = to_core(dfirst_low)
+    dfirst_other, first_other = to_core(dfirst_low), to_core(first_sums)
     store_close = to_core(tie(store_send, dfirst_other))
     started = dfirst_low
 
@@ -1122,41 +1127,34 @@
         prob,
         flat,
         mixed_half,
-        (third_sums, second_sums, first_sums, fc1_sum, cross_sums),
+        (third_sums, second_sums, first_sums, third_other, second_other, first_other, fc1_sum, cross_sums),
         nh,
         blocks,
     )
-    small_rows = butterfly(small[:9], "narrow", 4)
     if blocks:
         cross_got = tie(over(cross_out[0], 1), small)
         feed_send, feed_keep = add_stage(tie(at, cross_got), [feed_keep], [feed_next], None, 6)
         feed_next = over(feed_send, 4)
-        send = tie(send, feed_send)
+        fc1_grad, fc2_grad = last_stage(tie(at, feed_send), feed_keep, feed_next, None, [(1, False), (1, False)])
+        fc2_grad = fc2_grad.T
+        both_send, both_keep, small = add_stage(
+            tie(at, fc1_grad), [cross_out[1], self_out[1]], [cross_got, over(self_out[0], 1)], small, 5
+        )
+        both_next = over(both_send, 2)
+        send = tie(send, both_send)
     close = to_core(send)
     mine = (keep + close[:half].astype(F32)).astype(BF)
     other = to_across(mine)
-    small = jnp.concatenate([tie(small_rows, mine), small[9:]], axis=0)
     if blocks:
-        small = small + over(small, 1)
-        later = tie(at, small)
-        both_send, both_keep, small = add_stage(
-            later, [cross_out[1], self_out[1]], [cross_got, over(self_out[0], 1)], small, 5, True
-        )
-        both_next = over(both_send, 2)
+        both_send, both_keep, small = add_stage(tie(at, mine), [both_keep], [both_next], small, 6)
+        both_next = over(both_send, 4)
         other = tie(other, both_send)
     tokens_half = dfirst + (mine.astype(F32) + other.astype(F32))
     tokens_other = to_core(tokens_half)
-    store_distant = to_across(tie((store_keep[1] + store_close[1].astype(F32)).astype(BF), other))
     mixed = join_halves(tie(at, tokens_half), mixed_half, close)
-    if blocks:
-        fc1_grad, fc2_grad = last_stage(tie(at, mixed), feed_keep, feed_next, None, [(1, False), (1, False)])
-        fc2_grad = fc2_grad.T
-        tokens_other = tie(tokens_other, fc1_grad)
-    tokens_grad = join_halves(at, tokens_half, tokens_other)
-    if blocks:
-        both_send, both_keep, small = add_stage(tie(at, tokens_grad), [both_keep], [both_next], small, 6)
-        both_next = over(both_send, 4)
-        store_distant = tie(store_distant, both_send)
+    store_distant = to_across(tie((store_keep[1] + store_close[1].astype(F32)).astype(BF), mine))
+    tokens_grad = join_halves(at, tokens_half, tie(tokens_other, mixed))
+    store_distant = tie(store_distant, tokens_grad)
     store_grad = (store_keep[0] + store_close[0].astype(F32) + store_distant.astype(F32))[None]
 
     if blocks:

time: 225 us -> 214 us (0.951)
  waiting for transfers between devices: 98.9 us -> 91.7 us
  starting transfers between devices: 31.7 us -> 28.8 us
    ppermute x8 -> x7, waiting for transfers between devices: 58.1 us -> 42.4 us  [over(): return lax.ppermute(v, 'wide', flip(bit, wide))]
    ppermute x8, waiting for transfers between devices: 25.6 us -> 35.3 us  [to_across(): return lax.ppermute(v, 'narrow', ACROSS)]
    ppermute x2 -> x0, waiting for transfers between devices: 3.93 us -> none  [butterfly(): value = value + lax.ppermute(value, axis, flip(bit, size))]
    ppermute x15 -> x18, waiting for transfers between devices: 11.3 us -> 14 us  [to_core(): return lax.ppermute(v, 'narrow', CORE)]
    ppermute x8 -> x7, starting transfers between devices: 13.6 us -> 11.3 us  [over(): return lax.ppermute(v, 'wide', flip(bit, wide))]
  transfers between devices with their start and end apart: 33 -> 33, of which waited for: 19 -> 22; matrix products, arithmetic and copies ran while one was open for 1% -> 1% of each run, Pallas kernels for 24% -> 25%
where the time goes in v2:
time: 214 us
  waiting for transfers between devices  91.7 us (43%)
  Pallas kernels  82.4 us (39%)
  starting transfers between devices  28.8 us (13%)
  local copies, waits for them, and re-layouts  5.49 us (3%)
  other arithmetic  3.7 us (2%)
    pallas_call x25, Pallas kernels, launch(): pl.pallas_call(kernel, in_specs=in_specs, out_specs=out_specs, out_shape=...  82.4 us
    ppermute x7, waiting for transfers between devices, over(): return lax.ppermute(v, 'wide', flip(bit, wide))  42.4 us
    ppermute x8, waiting for transfers between devices, to_across(): return lax.ppermute(v, 'narrow', ACROSS)  35.3 us
    ppermute x8, starting transfers between devices, to_across(): return lax.ppermute(v, 'narrow', ACROSS)  14.1 us
    ppermute x18, waiting for transfers between devices, to_core(): return lax.ppermute(v, 'narrow', CORE)  14 us
    ppermute x7, starting transfers between devices, over(): return lax.ppermute(v, 'wide', flip(bit, wide))  11.3 us
  transfers between devices with their start and end apart: 33, of which 22 were waited for; matrix products, arithmetic and copies ran while one was open for 1% of the time, Pallas kernels for 25%

profile of v2, /device:TPU:0, one launch (start us, length us, event | category | flops | bytes accessed | tf_op | source)
XLA Modules:
  0.0 214.1 jit_solution(11206591270222863807)
XLA Ops:
  2.0 7.2 %self_fwd.1 = (bf16[3,512,192]{2,1,0:T(8,128)(2,1)}, bf16[3,512,512]{2,1,0:T(8,128)(2,1)}, bf16[512,192]{1,0:T(8,128)(2,1)}, bf16[256,768]{1,0:T(8,128)(2,1)}, f32[256,768]{1,0:T(8,128)}) custom-call(s32[7]{0:T(128)} %stack.33.at_ref, bf16[512,768]{1,0:T(8,128)(2,1)} %refs_5_.7, bf16[3,192,768]{2,1,0:T(8,128)(2,1)} %bitcast.29, bf16[192,768]{1,0:T(8,128)(2,1)} %refs_2_.11, ...), custom_call_target="tpu_custom_call" | custom-call | flops 440000000 | bytes 1000 | tf_op jit(solution)/shard_map/self_fwd/pallas_call | solution.py:160
  9.8 2.6 %collective-permute-start.2 = (bf16[416,768]{1,0:T(8,128)(2,1)S(1)}, bf16[416,768]{1,0:T(8,128)(2,1)S(1)}, u32[]{:S(2)}, u32[]{:S(2)}) collective-permute-start(bf16[416,768]{1,0:T(8,128)(2,1)S(1)} %bitcast.31), channel_id=1, source_target_pairs={{0,2},{1,3},{2,0},{3,1},{4,6},{5,7},{6,4},{7,5},{8,10},{9,11},{10,... | collective-permute-start | bytes 1916936 | tf_op jit(solution)/shard_map/ppermute | solution.py:1056
  13.6 1.9 collective-permute-start.1
  15.5 2.8 %copy-done = s32[512,3,4,256]{3,2,1,0:T(4,128)S(1)} copy-done((s32[512,3,4,256]{3,2,1,0:T(4,128)S(1)}, s32[512,3,4,256]{3,2,1,0:T(4,128)}, u32[]{:S(2)}) %copy-start) | copy-done | bytes 6291480
  18.3 9.6 %mask.2.refs_4_ = bf16[3,256,1664]{2,1,0:T(8,128)(2,1)S(1)} custom-call(s32[7]{0:T(128)S(1)} %copy-done.12, s32[4,3072,128]{2,1,0:T(8,128)S(1)} %bitcast.23), custom_call_target="tpu_custom_call" | custom-call | flops 1100000000 | bytes 1000 | tf_op jit(solution)/shard_map/mask/pallas_call | solution.py:160
  28.6 9.6 %mask.3.refs_5_ = bf16[3,256,1664]{2,1,0:T(8,128)(2,1)S(1)} custom-call(s32[7]{0:T(128)S(1)} %copy-done.12, s32[4,3072,128]{2,1,0:T(8,128)S(1)} %bitcast.24), custom_call_target="tpu_custom_call" | custom-call | flops 1100000000 | bytes 1000 | tf_op jit(solution)/shard_map/mask/pallas_call | solution.py:160
  39.4 2.3 %keys_values.1 = (bf16[3,1664,128]{2,1,0:T(8,128)(2,1)S(1)}, bf16[3,1664,128]{2,1,0:T(8,128)(2,1)S(1)}) custom-call(s32[7]{0:T(128)S(1)} %copy-done.12, bf16[416,768]{1,0:T(8,128)(2,1)S(1)} %bitcast.33, bf16[416,768]{1,0:T(8,128)(2,1)S(1)} %collective-permute-done.3.refs_1_, bf16[416,768]{1,0:T(8,128)(2,1)S(1)} %collective-permute-done.2.refs_2_, ...), custom_call_target="tpu_custom_call" | custom-call | flops 220000000 | bytes 1000 | tf_op jit(solution)/shard_map/keys_values/pallas_call | solution.py:160
  41.7 7.7 %cross_fwd.1 = (f32[256,768]{1,0:T(8,128)S(1)}, bf16[256,768]{1,0:T(8,128)(2,1)S(1)}, bf16[3,512,1664]{2,1,0:T(8,128)(2,1)S(1)}, f32[3,512,128]{2,1,0:T(8,128)S(...) custom-call(s32[7]{0:T(128)S(1)} %copy-done.12, bf16[256,768]{1,0:T(8,128)(2,1)S(1)} %get-tuple-element.119.refs_0_.refs_6_, ...), custom_call_target="tpu_custom_call" | custom-call | flops 990000000 | bytes 1000 | tf_op jit(solution)/shard_map/cross_fwd/pallas_call | solution.py:160
  49.9 1.3 collective-permute-done.6
  51.4 1.6 collective-permute-start.7
  53.0 9.8 %collective-permute-done.7.refs_2_ = bf16[256,768]{1,0:T(8,128)(2,1)S(1)} collective-permute-done((bf16[256,768]{1,0:T(8,128)(2,1)S(1)}, bf16[256,768]{1,0:T(8,128)(2,1)S(1)}, u32[]{:S(2)}, u32[]{:S(2)}) %collective-permute-start.7) | collective-permute-done | bytes 393248 | tf_op jit(solution)/shard_map/ppermute | solution.py:1056
  63.9 1.7 collective-permute-done.8.refs_1_
  65.6 3.5 %feed_up.1 = (f32[256,768]{1,0:T(8,128)S(1)}, bf16[256,768]{1,0:T(8,128)(2,1)S(1)}, bf16[512,768]{1,0:T(8,128)(2,1)S(1)}, f32[512,768]{1,0:T(8,128)S(1)}) custom-call(s32[7]{0:T(128)S(1)} %copy-done.12, bf16[256,768]{1,0:T(8,128)(2,1)S(1)} %get-tuple-element.129.refs_0_, bf16[256,768]{1,0:T(8,128)(2,1)S(1)} %collective-permute-done.8.refs_1_, ...), custom_call_target="tpu_custom_call" | custom-call | flops 440000000 | bytes 1000 | tf_op jit(solution)/shard_map/feed_up/pallas_call | solution.py:160
  69.3 1.6 collective-permute-done.9
  71.0 1.6 collective-permute-start.10
  72.6 9.6 %collective-permute-done.10.refs_2_ = bf16[256,768]{1,0:T(8,128)(2,1)S(1)} collective-permute-done((bf16[256,768]{1,0:T(8,128)(2,1)S(1)}, bf16[256,768]{1,0:T(8,128)(2,1)S(1)}, u32[]{:S(2)}, u32[]{:S(2)}) %collective-permute-start.10) | collective-permute-done | bytes 393248 | tf_op jit(solution)/shard_map/ppermute | solution.py:1056
  82.2 1.7 third_norm.1
  84.0 1.7 collective-permute-done.11.refs_1_.refs_4_
  85.7 2.1 feed_down.1
  88.0 1.6 collective-permute-done.12
  89.7 1.6 collective-permute-start.13
  91.3 3.4 %feed_grads.1 = (bf16[384,1536]{1,0:T(8,128)(2,1)S(1)}, f32[4,96,1536]{2,1,0:T(8,128)S(1)}) custom-call(s32[7]{0:T(128)S(1)} %copy-done.12, bf16[256,768]{1,0:T(8,128)(2,1)S(1)} %get-tuple-element.129.refs_0_, bf16[256,768]{1,0:T(8,128)(2,1)S(1)} %collective-permute-done.8.refs_1_, bf16[512,768]{1,0:T(8,128)(2,1)S(1)} %get-tuple-element.138.refs_2_, ...), custom_call_target="tpu_custom_call" | custom-call | flops 440000000 | bytes 1000 | tf_op jit(solution)/shard_map/feed_grads/pallas_call | solution.py:160
  94.8 6.2 %collective-permute-done.13.refs_2_ = bf16[256,768]{1,0:T(8,128)(2,1)S(1)} collective-permute-done((bf16[256,768]{1,0:T(8,128)(2,1)S(1)}, bf16[256,768]{1,0:T(8,128)(2,1)S(1)}, u32[]{:S(2)}, u32[]{:S(2)}) %collective-permute-start.13) | collective-permute-done | bytes 393248 | tf_op jit(solution)/shard_map/ppermute | solution.py:1056
  102.2 1.7 collective-permute-start.17
  103.9 10.6 %cross_bwd.1 = (f32[256,768]{1,0:T(8,128)S(1)}, bf16[256,768]{1,0:T(8,128)(2,1)S(1)}, bf16[512,192]{1,0:T(8,128)(2,1)S(1)}, bf16[3,1664,128]{2,1,0:T(8,128)(2,1)S(1)}, f32[2,192]{1,0:T(2,128)S(1)}) custom-call(s32[7]{0:T(128)S(1)} %copy-done.12, bf16[256,768]{1,0:T(8,128)(2,1)S(1)} %get-tuple-element.143.refs_0_.refs_4_, ...), custom_call_target="tpu_custom_call" | custom-call | flops 1210000000 | bytes 1000 | tf_op jit(solution)/shard_map/cross_bwd/pallas_call | solution.py:160
  114.7 1.6 collective-permute-done.15
  116.4 1.6 collective-permute-start.16
  118.0 3.5 %cross_grads.1 = (bf16[384,768]{1,0:T(8,128)(2,1)S(1)}, f32[4,96,768]{2,1,0:T(8,128)S(1)}) custom-call(s32[7]{0:T(128)S(1)} %copy-done.12, bf16[416,768]{1,0:T(8,128)(2,1)S(1)} %bitcast.34, bf16[416,768]{1,0:T(8,128)(2,1)S(1)} %collective-permute-done.3.refs_1_, bf16[416,768]{1,0:T(8,128)(2,1)S(1)} %collective-permute-done.2.refs_2_, ...), custom_call_target="tpu_custom_call" | custom-call | flops 440000000 | bytes 1000 | tf_op jit(solution)/shard_map/cross_grads/pallas_call | solution.py:160
  121.5 9.1 %collective-permute-done.17.refs_1_ = bf16[384,1536]{1,0:T(8,128)(2,1)S(1)} collective-permute-done((bf16[384,1536]{1,0:T(8,128)(2,1)S(1)}, bf16[384,1536]{1,0:T(8,128)(2,1)S(1)}, u32[]{:S(2)}, u32[]{:S(2)}) %collective-permute-start.17) | collective-permute-done | bytes 1179680 | tf_op jit(solution)/shard_map/ppermute | solution.py:1059
  131.5 2.1 store_grad.1
  134.9 1.7 collective-permute-done.18.refs_1_
  136.7 1.6 collective-permute-start.23
  138.4 1.6 collective-permute-start.24
  141.7 5.5 %self_bwd.1 = (bf16[512,768]{1,0:T(8,128)(2,1)S(1)}, f32[256,768]{1,0:T(8,128)S(1)}, bf16[416,768]{1,0:T(8,128)(2,1)S(1)}, f32[4,96,768]{2,1,0:T(8,128)S(1)}, f32[16,768]{1,0:T(8,128)S(1)}) custom-call(s32[7]{0:T(128)S(1)} %copy-done.12, bf16[256,768]{1,0:T(8,128)(2,1)S(1)} %get-tuple-element.162.refs_0_, ...), custom_call_target="tpu_custom_call" | custom-call | flops 660000000 | bytes 1000 | tf_op jit(solution)/shard_map/self_bwd/pallas_call | solution.py:160
  148.0 4.9 %collective-permute-done.23.refs_2_ = bf16[384,768]{1,0:T(8,128)(2,1)S(1)} collective-permute-done((bf16[384,768]{1,0:T(8,128)(2,1)S(1)}, bf16[384,768]{1,0:T(8,128)(2,1)S(1)}, u32[]{:S(2)}, u32[]{:S(2)}) %collective-permute-start.23) | collective-permute-done | bytes 589856 | tf_op jit(solution)/shard_map/ppermute | solution.py:1059
  154.4 2.7 %collective-permute-start.25 = (bf16[96,1536]{1,0:T(8,128)(2,1)S(1)}, bf16[96,1536]{1,0:T(8,128)(2,1)S(1)}, u32[]{:S(2)}, u32[]{:S(2)}) collective-permute-start(bf16[96,1536]{1,0:T(8,128)(2,1)S(1)} %get-tuple-element.180), channel_id=1, source_target_pairs={{0,16},{4,20},{8,24},{12,28},{16,0},{20,4},{24,8},{28,12},{1,17},{... | collective-permute-start | bytes 884744 | tf_op jit(solution)/shard_map/ppermute | solution.py:1059
  157.0 12.8 %collective-permute-done.25.refs_1_ = bf16[96,1536]{1,0:T(8,128)(2,1)S(1)} collective-permute-done((bf16[96,1536]{1,0:T(8,128)(2,1)S(1)}, bf16[96,1536]{1,0:T(8,128)(2,1)S(1)}, u32[]{:S(2)}, u32[]{:S(2)}) %collective-permute-start.25) | collective-permute-done | bytes 294944 | tf_op jit(solution)/shard_map/ppermute | solution.py:1059
  169.8 1.4 last_stage.2
  172.8 1.5 collective-permute-done.27.refs_1_
  174.5 1.6 collective-permute-start.28
  176.0 12.9 %collective-permute-done.29.refs_1_ = bf16[208,1536]{1,0:T(8,128)(2,1)S(1)} collective-permute-done((bf16[208,1536]{1,0:T(8,128)(2,1)S(1)}, bf16[208,1536]{1,0:T(8,128)(2,1)S(1)}, u32[]{:S(2)}, u32[]{:S(2)}) %collective-permute-start.29) | collective-permute-done | bytes 639008 | tf_op jit(solution)/shard_map/ppermute | solution.py:1059
  189.9 1.6 collective-permute-start.31
  191.5 2.3 %collective-permute-start.32 = (bf16[112,1536]{1,0:T(8,128)(2,1)S(1)}, bf16[112,1536]{1,0:T(8,128)(2,1)S(1)}, u32[]{:S(2)}, u32[]{:S(2)}) collective-permute-start(bf16[112,1536]{1,0:T(8,128)(2,1)S(1)} %get-tuple-element.193), channel_id=1, source_target_pairs={{0,16},{4,20},{8,24},{12,28},{16,0},{20,4},{24,8},{28,12},{1,17},{... | collective-permute-start | bytes 1032200 | tf_op jit(solution)/shard_map/ppermute | solution.py:1059
  193.8 1.5 join_halves.2
  195.3 1.8 join_halves.3
  197.1 9.7 %collective-permute-done.31 = bf16[416,768]{1,0:T(8,128)(2,1)S(1)} collective-permute-done((bf16[416,768]{1,0:T(8,128)(2,1)S(1)}, bf16[416,768]{1,0:T(8,128)(2,1)S(1)}, u32[]{:S(2)}, u32[]{:S(2)}) %collective-permute-start.31) | collective-permute-done | bytes 639008 | tf_op jit(solution)/shard_map/ppermute | solution.py:1056
  208.0 1.9 collective-permute-done.32.refs_1_
  209.9 1.5 last_stage.3
  (104 shorter events, 20.7 us)
Async XLA Ops:
  0.7 9.2 %copy-start.6 = (bf16[1,416,768]{2,1,0:T(8,128)(2,1)S(1)}, bf16[1,416,768]{2,1,0:T(8,128)(2,1)}, u32[]{:S(2)}) copy-start(bf16[1,416,768]{2,1,0:T(8,128)(2,1)} %param.20) | copy-start | bytes 1916932
  9.3 6.2 %copy-start.12 = (s32[7]{0:T(128)S(1)}, s32[7]{0:T(128)}, u32[]{:S(2)}) copy-start(s32[7]{0:T(128)} %stack.33.at_ref) | copy-start | bytes 88
  9.3 3.1 %collective-permute-start = (bf16[256,768]{1,0:T(8,128)(2,1)}, bf16[256,768]{1,0:T(8,128)(2,1)S(1)}, u32[]{:S(2)}, u32[]{:S(2)}) collective-permute-start(bf16[256,768]{1,0:T(8,128)(2,1)} %get-tuple-element.114), channel_id=1, source_target_pairs={{0,1},{1,0},{2,3},{3,2},{4,5},{5,4},{6,7},{7,6},{8,9},{9,8},{10,11... | collective-permute-start | bytes 1179656 | tf_op jit(solution)/shard_map/ppermute | solution.py:1053
  9.8 18.1 %collective-permute-start.2 = (bf16[416,768]{1,0:T(8,128)(2,1)S(1)}, bf16[416,768]{1,0:T(8,128)(2,1)S(1)}, u32[]{:S(2)}, u32[]{:S(2)}) collective-permute-start(bf16[416,768]{1,0:T(8,128)(2,1)S(1)} %bitcast.31), channel_id=1, source_target_pairs={{0,2},{1,3},{2,0},{3,1},{4,6},{5,7},{6,4},{7,5},{8,10},{9,11},{10,... | collective-permute-start | bytes 1916936 | tf_op jit(solution)/shard_map/ppermute | solution.py:1056
  13.6 24.6 %collective-permute-start.1 = (bf16[256,768]{1,0:T(8,128)(2,1)S(1)}, bf16[256,768]{1,0:T(8,128)(2,1)S(1)}, u32[]{:S(2)}, u32[]{:S(2)}) collective-permute-start(bf16[256,768]{1,0:T(8,128)(2,1)S(1)} %add_convert_fusion.6.refs_0_), channel_id=1, source_target_pairs={{0,2},{1,3},{2,0},{3,1},{4,6},{5,7},{6,4},{7,5},{8,10},{9,11},{10,... | collective-permute-start | bytes 1179656 | tf_op jit(solution)/shard_map/ppermute | solution.py:1056
  18.3 10.2 %copy-start.17 = (f32[768]{0:T(1024)S(1)}, f32[768]{0:T(1024)}, u32[]{:S(2)}) copy-start(f32[768]{0:T(1024)} %param.27) | copy-start | bytes 9220
  28.0 11.4 %collective-permute-start.3 = (bf16[416,768]{1,0:T(8,128)(2,1)S(1)}, bf16[416,768]{1,0:T(8,128)(2,1)S(1)}, u32[]{:S(2)}, u32[]{:S(2)}) collective-permute-start(bf16[416,768]{1,0:T(8,128)(2,1)S(1)} %bitcast.32), channel_id=1, source_target_pairs={{0,1},{1,0},{2,3},{3,2},{4,5},{5,4},{6,7},{7,6},{8,9},{9,8},{10,11... | collective-permute-start | bytes 1916936 | tf_op jit(solution)/shard_map/ppermute | solution.py:1053
  28.0 11.3 %collective-permute-start.4 = (bf16[416,768]{1,0:T(8,128)(2,1)S(1)}, bf16[416,768]{1,0:T(8,128)(2,1)S(1)}, u32[]{:S(2)}, u32[]{:S(2)}) collective-permute-start(bf16[416,768]{1,0:T(8,128)(2,1)S(1)} %collective-permute-done.2.refs_2_), channel_id=1, source_target_pairs={{0,1},{1,0},{2,3},{3,2},{4,5},{5,4},{6,7},{7,6},{8,9},{9,8},{10,11... | collective-permute-start | bytes 1916936 | tf_op jit(solution)/shard_map/ppermute | solution.py:1053
  28.5 9.7 %copy-start.2 = (bf16[512,768]{1,0:T(8,128)(2,1)S(1)}, bf16[512,768]{1,0:T(8,128)(2,1)}, u32[]{:S(2)}) copy-start(bf16[512,768]{1,0:T(8,128)(2,1)} %refs_5_.7) | copy-start | bytes 2359300
  28.5 9.7 %copy-start.13 = (f32[3,768]{1,0:T(4,128)S(1)}, f32[3,768]{1,0:T(4,128)}, u32[]{:S(2)}) copy-start(f32[3,768]{1,0:T(4,128)} %refs_4_.7) | copy-start | bytes 27652
  28.6 9.7 %copy-start.15 = (f32[3,768]{1,0:T(4,128)S(1)}, f32[3,768]{1,0:T(4,128)}, u32[]{:S(2)}) copy-start(f32[3,768]{1,0:T(4,128)} %refs_6_.1) | copy-start | bytes 27652
  39.2 2.5 %collective-permute-start.5 = (bf16[256,768]{1,0:T(8,128)(2,1)S(1)}, bf16[256,768]{1,0:T(8,128)(2,1)S(1)}, u32[]{:S(2)}, u32[]{:S(2)}) collective-permute-start(bf16[256,768]{1,0:T(8,128)(2,1)S(1)} %get-tuple-element.119.refs_0_.refs_6_), channel_id=1, source_target_pairs={{0,1},{1,0},{2,3},{3,2},{4,5},{5,4},{6,7},{7,6},{8,9},{9,8},{10,11... | collective-permute-start | bytes 1179656 | tf_op jit(solution)/shard_map/ppermute | solution.py:1053
  49.4 1.8 collective-permute-start.6
  51.3 12.6 %copy-start.19 = (f32[768]{0:T(1024)S(1)}, f32[768]{0:T(1024)}, u32[]{:S(2)}) copy-start(f32[768]{0:T(1024)} %param.33) | copy-start | bytes 9220
  51.3 14.3 %copy-start.3 = (bf16[768,768]{1,0:T(8,128)(2,1)S(1)}, bf16[768,768]{1,0:T(8,128)(2,1)}, u32[]{:S(2)}) copy-start(bf16[768,768]{1,0:T(8,128)(2,1)} %refs_2_.9) | copy-start | bytes 3538948
  51.3 14.3 %copy-start.4 = (bf16[768,768]{1,0:T(8,128)(2,1)S(1)}, bf16[768,768]{1,0:T(8,128)(2,1)}, u32[]{:S(2)}) copy-start(bf16[768,768]{1,0:T(8,128)(2,1)} %refs_3_.7) | copy-start | bytes 3538948
  51.4 11.5 %collective-permute-start.7 = (bf16[256,768]{1,0:T(8,128)(2,1)S(1)}, bf16[256,768]{1,0:T(8,128)(2,1)S(1)}, u32[]{:S(2)}, u32[]{:S(2)}) collective-permute-start(bf16[256,768]{1,0:T(8,128)(2,1)S(1)} %add_convert_fusion.5.refs_1_), channel_id=1, source_target_pairs={{0,2},{1,3},{2,0},{3,1},{4,6},{5,7},{6,4},{7,5},{8,10},{9,11},{10,... | collective-permute-start | bytes 1179656 | tf_op jit(solution)/shard_map/ppermute | solution.py:1056
  63.8 1.8 collective-permute-start.8
  69.1 13.1 %copy-start.10 = (bf16[512,768]{1,0:T(8,128)(2,1)S(1)}, bf16[512,768]{1,0:T(8,128)(2,1)}, u32[]{:S(2)}) copy-start(bf16[512,768]{1,0:T(8,128)(2,1)} %refs_3_.6) | copy-start | bytes 2359300
  69.1 1.8 collective-permute-start.9
  71.0 11.2 %collective-permute-start.10 = (bf16[256,768]{1,0:T(8,128)(2,1)S(1)}, bf16[256,768]{1,0:T(8,128)(2,1)S(1)}, u32[]{:S(2)}, u32[]{:S(2)}) collective-permute-start(bf16[256,768]{1,0:T(8,128)(2,1)S(1)} %add_convert_fusion.4.refs_1_), channel_id=1, source_target_pairs={{0,2},{1,3},{2,0},{3,1},{4,6},{5,7},{6,4},{7,5},{8,10},{9,11},{10,... | collective-permute-start | bytes 1179656 | tf_op jit(solution)/shard_map/ppermute | solution.py:1056
  83.9 1.8 collective-permute-start.11
  87.8 1.8 collective-permute-start.12
  89.7 11.2 %collective-permute-start.13 = (bf16[256,768]{1,0:T(8,128)(2,1)S(1)}, bf16[256,768]{1,0:T(8,128)(2,1)S(1)}, u32[]{:S(2)}, u32[]{:S(2)}) collective-permute-start(bf16[256,768]{1,0:T(8,128)(2,1)S(1)} %add_convert_fusion.3.refs_1_), channel_id=1, source_target_pairs={{0,2},{1,3},{2,0},{3,1},{4,6},{5,7},{6,4},{7,5},{8,10},{9,11},{10,... | collective-permute-start | bytes 1179656 | tf_op jit(solution)/shard_map/ppermute | solution.py:1056
  102.2 1.8 collective-permute-start.14
  102.2 28.4 %collective-permute-start.17 = (bf16[384,1536]{1,0:T(8,128)(2,1)S(1)}, bf16[384,1536]{1,0:T(8,128)(2,1)S(1)}, u32[]{:S(2)}, u32[]{:S(2)}) collective-permute-start(bf16[384,1536]{1,0:T(8,128)(2,1)S(1)} %get-tuple-element.140), channel_id=1, source_target_pairs={{0,4},{4,0},{8,12},{12,8},{16,20},{20,16},{24,28},{28,24},{1,5},{5... | collective-permute-start | bytes 3538952 | tf_op jit(solution)/shard_map/ppermute | solution.py:1059
  114.5 1.8 collective-permute-start.15
  116.4 17.2 %collective-permute-start.16 = (bf16[256,768]{1,0:T(8,128)(2,1)S(1)}, bf16[256,768]{1,0:T(8,128)(2,1)S(1)}, u32[]{:S(2)}, u32[]{:S(2)}) collective-permute-start(bf16[256,768]{1,0:T(8,128)(2,1)S(1)} %add_convert_fusion.2.refs_1_), channel_id=1, source_target_pairs={{0,2},{1,3},{2,0},{3,1},{4,6},{5,7},{6,4},{7,5},{8,10},{9,11},{10,... | collective-permute-start | bytes 1179656 | tf_op jit(solution)/shard_map/ppermute | solution.py:1056
  131.5 10.2 %copy-start.7 = (bf16[3,512,512]{2,1,0:T(8,128)(2,1)S(1)}, bf16[3,512,512]{2,1,0:T(8,128)(2,1)}, u32[]{:S(2)}) copy-start(bf16[3,512,512]{2,1,0:T(8,128)(2,1)} %get-tuple-element.166.refs_4_) | copy-start | bytes 4718596
  133.5 8.1 %copy-start.5 = (bf16[3,768,192]{1,2,0:T(8,128)(2,1)S(1)}, bf16[3,768,192]{1,2,0:T(8,128)(2,1)}, u32[]{:S(2)}) copy-start(bf16[3,768,192]{1,2,0:T(8,128)(2,1)} %param.24) | copy-start | bytes 2654212
  133.5 8.1 %copy-start.9 = (bf16[192,768]{1,0:T(8,128)(2,1)S(1)}, bf16[192,768]{1,0:T(8,128)(2,1)}, u32[]{:S(2)}) copy-start(bf16[192,768]{1,0:T(8,128)(2,1)} %refs_2_.11) | copy-start | bytes 884740
  133.6 8.1 %copy-start.11 = (bf16[3,512,192]{2,1,0:T(8,128)(2,1)S(1)}, bf16[3,512,192]{2,1,0:T(8,128)(2,1)}, u32[]{:S(2)}) copy-start(bf16[3,512,192]{2,1,0:T(8,128)(2,1)} %get-tuple-element.165.refs_3_) | copy-start | bytes 1769476
  133.6 8.1 %copy-start.14 = (bf16[512,192]{1,0:T(8,128)(2,1)S(1)}, bf16[512,192]{1,0:T(8,128)(2,1)}, u32[]{:S(2)}) copy-start(bf16[512,192]{1,0:T(8,128)(2,1)} %get-tuple-element.168.refs_8_) | copy-start | bytes 589828
  134.8 1.8 collective-permute-start.18
  136.6 3.8 %collective-permute-start.19 = (bf16[2,416,768]{2,1,0:T(8,128)(2,1)S(1)}, bf16[2,416,768]{2,1,0:T(8,128)(2,1)S(1)}, u32[]{:S(2)}, u32[]{:S(2)}) collective-permute-start(bf16[2,416,768]{2,1,0:T(8,128)(2,1)S(1)} %get-tuple-element.163), channel_id=1, source_target_pairs={{0,1},{1,0},{2,3},{3,2},{4,5},{5,4},{6,7},{7,6},{8,9},{9,8},{10,11... | collective-permute-start | bytes 3833864 | tf_op jit(solution)/shard_map/ppermute | solution.py:1053
  136.7 16.2 %collective-permute-start.23 = (bf16[384,768]{1,0:T(8,128)(2,1)S(1)}, bf16[384,768]{1,0:T(8,128)(2,1)S(1)}, u32[]{:S(2)}, u32[]{:S(2)}) collective-permute-start(bf16[384,768]{1,0:T(8,128)(2,1)S(1)} %get-tuple-element.153), channel_id=1, source_target_pairs={{0,4},{4,0},{8,12},{12,8},{16,20},{20,16},{24,28},{28,24},{1,5},{5... | collective-permute-start | bytes 1769480 | tf_op jit(solution)/shard_map/ppermute | solution.py:1059
  138.4 15.3 %collective-permute-start.24 = (bf16[192,1536]{1,0:T(8,128)(2,1)S(1)}, bf16[192,1536]{1,0:T(8,128)(2,1)S(1)}, u32[]{:S(2)}, u32[]{:S(2)}) collective-permute-start(bf16[192,1536]{1,0:T(8,128)(2,1)S(1)} %get-tuple-element.156), channel_id=1, source_target_pairs={{0,8},{4,12},{8,0},{12,4},{16,24},{20,28},{24,16},{28,20},{1,9},{5... | collective-permute-start | bytes 1769480 | tf_op jit(solution)/shard_map/ppermute | solution.py:1059
  139.9 1.2 collective-permute-start.20
  139.9 1.4 collective-permute-start.21
  140.4 1.2 collective-permute-start.22
  147.2 24.0 %collective-permute-start.26 = (bf16[416,768]{1,0:T(8,128)(2,1)S(1)}, bf16[416,768]{1,0:T(8,128)(2,1)S(1)}, u32[]{:S(2)}, u32[]{:S(2)}) collective-permute-start(bf16[416,768]{1,0:T(8,128)(2,1)S(1)} %get-tuple-element.187), channel_id=1, source_target_pairs={{0,4},{4,0},{8,12},{12,8},{16,20},{20,16},{24,28},{28,24},{1,5},{5... | collective-permute-start | bytes 1916936 | tf_op jit(solution)/shard_map/ppermute | solution.py:1059
  154.4 15.4 %collective-permute-start.25 = (bf16[96,1536]{1,0:T(8,128)(2,1)S(1)}, bf16[96,1536]{1,0:T(8,128)(2,1)S(1)}, u32[]{:S(2)}, u32[]{:S(2)}) collective-permute-start(bf16[96,1536]{1,0:T(8,128)(2,1)S(1)} %get-tuple-element.180), channel_id=1, source_target_pairs={{0,16},{4,20},{8,24},{12,28},{16,0},{20,4},{24,8},{28,12},{1,17},{... | collective-permute-start | bytes 884744 | tf_op jit(solution)/shard_map/ppermute | solution.py:1059
  172.0 2.4 %collective-permute-start.27 = (bf16[512,768]{1,0:T(8,128)(2,1)S(1)}, bf16[512,768]{1,0:T(8,128)(2,1)S(1)}, u32[]{:S(2)}, u32[]{:S(2)}) collective-permute-start(bf16[512,768]{1,0:T(8,128)(2,1)S(1)} %get-tuple-element.189), channel_id=1, source_target_pairs={{0,1},{1,0},{2,3},{3,2},{4,5},{5,4},{6,7},{7,6},{8,9},{9,8},{10,11... | collective-permute-start | bytes 2359304 | tf_op jit(solution)/shard_map/ppermute | solution.py:1053
  172.1 16.8 %collective-permute-start.29 = (bf16[208,1536]{1,0:T(8,128)(2,1)S(1)}, bf16[208,1536]{1,0:T(8,128)(2,1)S(1)}, u32[]{:S(2)}, u32[]{:S(2)}) collective-permute-start(bf16[208,1536]{1,0:T(8,128)(2,1)S(1)} %get-tuple-element.188), channel_id=1, source_target_pairs={{0,8},{4,12},{8,0},{12,4},{16,24},{20,28},{24,16},{28,20},{1,9},{5... | collective-permute-start | bytes 1916936 | tf_op jit(solution)/shard_map/ppermute | solution.py:1059
  174.5 15.1 %collective-permute-start.28 = (bf16[256,768]{1,0:T(8,128)(2,1)S(1)}, bf16[256,768]{1,0:T(8,128)(2,1)S(1)}, u32[]{:S(2)}, u32[]{:S(2)}) collective-permute-start(bf16[256,768]{1,0:T(8,128)(2,1)S(1)} %add_convert_fusion.1), channel_id=1, source_target_pairs={{0,2},{1,3},{2,0},{3,1},{4,6},{5,7},{6,4},{7,5},{8,10},{9,11},{10,... | collective-permute-start | bytes 1179656 | tf_op jit(solution)/shard_map/ppermute | solution.py:1056
  189.7 5.6 %collective-permute-start.30 = (f32[256,768]{1,0:T(8,128)S(1)}, f32[256,768]{1,0:T(8,128)S(1)}, u32[]{:S(2)}, u32[]{:S(2)}) collective-permute-start(f32[256,768]{1,0:T(8,128)S(1)} %add_add_fusion.refs_0_), channel_id=1, source_target_pairs={{0,1},{1,0},{2,3},{3,2},{4,5},{5,4},{6,7},{7,6},{8,9},{9,8},{10,11... | collective-permute-start | bytes 2359304 | tf_op jit(solution)/shard_map/ppermute | solution.py:1053
  189.9 16.8 %collective-permute-start.31 = (bf16[416,768]{1,0:T(8,128)(2,1)S(1)}, bf16[416,768]{1,0:T(8,128)(2,1)S(1)}, u32[]{:S(2)}, u32[]{:S(2)}) collective-permute-start(bf16[416,768]{1,0:T(8,128)(2,1)S(1)} %fusion.1), channel_id=1, source_target_pairs={{0,2},{1,3},{2,0},{3,1},{4,6},{5,7},{6,4},{7,5},{8,10},{9,11},{10,... | collective-permute-start | bytes 1916936 | tf_op jit(solution)/shard_map/ppermute | solution.py:1056
  191.5 18.5 %collective-permute-start.32 = (bf16[112,1536]{1,0:T(8,128)(2,1)S(1)}, bf16[112,1536]{1,0:T(8,128)(2,1)S(1)}, u32[]{:S(2)}, u32[]{:S(2)}) collective-permute-start(bf16[112,1536]{1,0:T(8,128)(2,1)S(1)} %get-tuple-element.193), channel_id=1, source_target_pairs={{0,16},{4,20},{8,24},{12,28},{16,0},{20,4},{24,8},{28,12},{1,17},{... | collective-permute-start | bytes 1032200 | tf_op jit(solution)/shard_map/ppermute | solution.py:1059
  (6 other events, 15.7 us)

commit v3 on v2

--- a/solution.py
+++ b/solution.py
@@ -642,9 +642,9 @@
                 dscore = (weighed - e * mean).astype(BF)
                 both = mm(dscore, keys[h])
                 found[h, span, :] = both[:, :hd] + both[:, hd:]
-                part = mm(dscore, right[h, 0, span, :], TN) + mm(low, right[h, 1, span, :], TN)
+                part = mm(right[h, 0, span, :], dscore, TN) + mm(right[h, 1, span, :], low, TN)
                 grad = part if grad is None else grad + part
-            dkv[h] = grad.astype(BF)
+            dkv[h] = grad.astype(BF).T
             return 0
 
         lax.fori_loop(0, nh, one_head, 0)
@@ -851,19 +851,17 @@
             weighed = weights * mm(dself[:, part], v[:, part], NT)
             dscore = (weighed - weights * jnp.sum(weighed, axis=1, keepdims=True)).astype(BF)
             dq.append(mm(dscore, k[:, part]))
-            dk.append(mm(dscore, q[:, part], TN))
-            dv.append(mm(weights_low, dself[:, part], TN))
+            dk.append(mm(q[:, part], dscore, TN))
+            dv.append(mm(dself[:, part], weights_low, TN))
         dquery = jnp.concatenate(dq, axis=1) * scale
-        dvalue = jnp.concatenate(dv, axis=1)
-        dqkv[0] = dquery.astype(BF)
-        dqkv[1] = (jnp.concatenate(dk, axis=1) * scale).astype(BF)
-        dqkv[2] = dvalue.astype(BF)
+        dvalue = jnp.concatenate(dv, axis=0).T
+        dqkv[:, 0:local] = dquery.astype(BF)
+        dqkv[:, local : 2 * local] = (jnp.concatenate(dk, axis=0) * scale).astype(BF).T
+        dqkv[:, 2 * local :] = dvalue.astype(BF)
         x = tok[...]
-        for i in range(3):
-            grad[...] = mm(x, dqkv[i], TN)
-            emit_group(at, grad, group, blocks, i * local, local)
-        grad[...] = mm(z[...], flat[...], TN)
-        emit_group(at, grad, group, blocks, 3 * local, local)
+        grad[:, 0 : 3 * local] = mm(x, dqkv[...], TN)
+        grad[:, 3 * local :] = mm(z[...], flat[...], TN)
+        emit_group(at, grad, group, blocks, 0, 4 * local)
         pad = jnp.zeros((1, width - 2 * local), F32)
         small = jnp.concatenate(
             [
@@ -882,7 +880,8 @@
             group[0][blocks[0] * blocks[1] :, :] = two_terms(small)
         send[half:, :] = mixed[...]
         for place, out in ((distant, send), (own, keep)):
-            total = mm(dqkv[0, place, :], w[0]) + mm(dqkv[1, place, :], w[1]) + mm(dqkv[2, place, :], w[2])
+            rows_now = dqkv[place, :]
+            total = sum(mm(rows_now[:, i * local : (i + 1) * local], w[i]) for i in range(3))
             out[0:half, :] = total.astype(out.dtype)
 
     return launch(
@@ -895,8 +894,8 @@
         + [shape(EXTRA, width)],
         scratch=[
             pltpu.VMEM((rows, width), BF),
-            pltpu.VMEM((3, rows, local), BF),
-            pltpu.VMEM((width, local), F32),
+            pltpu.VMEM((rows, 3 * local), BF),
+            pltpu.VMEM((width, 4 * local), F32),
         ],
         mib=20,
         us=6,
@@ -974,7 +973,14 @@
                     out[i] = total[:, (first + i) * each : (first + i + 1) * each]
             first += count
         if reach:
-            outs[-1][...] = ins[2][...] + unfold_lines(from_terms(ins[1][rows:, :]), reach)
+            value = ins[2][...] + unfold_lines(from_terms(ins[1][rows:, :]), reach)
+            outs[-1][...] = value
+            gains, shifts, cross_line, self_line = outs[-5:-1]
+            gains[...] = jnp.concatenate([value[6:7], value[3:4], value[0:1]], axis=0)
+            shifts[...] = jnp.concatenate([value[7:8], value[4:5], value[1:2]], axis=0)
+            half = cross_line.shape[1]
+            for line, row in ((cross_line, value[10:11]), (self_line, value[11:12])):
+                line[...] = jnp.concatenate([row[:, :half], row[:, half : 2 * half]], axis=0)
 
     outs = []
     for count, turned in parts:
@@ -983,7 +989,7 @@
     ins = [near(keep), near(got)]
     if reach:
         ins.append(near(small))
-        outs.append(shape(small.shape[0], reach))
+        outs += [shape(3, reach), shape(3, reach), shape(2, reach // 4), shape(2, reach // 4), shape(small.shape[0], reach)]
     return launch(body, "last_stage", at, ins, outs, us=1)
 
 
@@ -1158,7 +1164,7 @@
     store_grad = (store_keep[0] + store_close[0].astype(F32) + store_distant.astype(F32))[None]
 
     if blocks:
-        qkv_grad, out_grad, self_qkv_grad, self_out_grad, small = last_stage(
+        qkv_grad, out_grad, self_qkv_grad, self_out_grad, *lines, small = last_stage(
             tie(at, store_grad), both_keep, both_next, small, [(3, False), (1, True), (3, False), (1, True)]
         )
     else:
@@ -1171,27 +1177,31 @@
         self_qkv_grad = scatter(parts(self_out[0]), scatter_dimension=1)
         self_out_grad = scatter(self_out[0][:, 3 * local :].T, scatter_dimension=1)
         small = butterfly(small, "wide", wide)
-    gain_last, shift_last, fc2_b, gain_mid, shift_mid, out_b, gain_first, shift_first, self_out_b = (
-        small[i] for i in range(9)
-    )
+        lines = (
+            jnp.stack([small[6], small[3], small[0]]),
+            jnp.stack([small[7], small[4], small[1]]),
+            small[10, : 2 * local].reshape(2, local),
+            small[11, : 2 * local].reshape(2, local),
+        )
+    gain_grad, shift_grad, qv_grad, self_qv_grad = lines
     return (
         mixed,
         tokens_grad,
         store_grad,
         self_qkv_grad,
-        small[11, : 2 * local].reshape(2, local),
+        self_qv_grad,
         self_out_grad,
-        self_out_b,
+        small[8],
         qkv_grad,
-        small[10, : 2 * local].reshape(2, local),
+        qv_grad,
         out_grad,
-        out_b,
+        small[5],
         fc1_grad,
         small[9],
         fc2_grad,
-        fc2_b,
-        jnp.stack([gain_first, gain_mid, gain_last]),
-        jnp.stack([shift_first, shift_mid, shift_last]),
+        small[2],
+        gain_grad,
+        shift_grad,
     )
 
 

time: 214 us -> 212 us (level)
  no operation moved by 1% of the time
where the time goes in v3:
time: 212 us
  waiting for transfers between devices  93.3 us (44%)
  Pallas kernels  80.8 us (38%)
  starting transfers between devices  28.8 us (14%)
  local copies, waits for them, and re-layouts  4.14 us (2%)
  other arithmetic  3.08 us (1%)
    pallas_call x25, Pallas kernels, launch(): pl.pallas_call(kernel, in_specs=in_specs, out_specs=out_specs, out_shape=...  80.8 us
    ppermute x7, waiting for transfers between devices, over(): return lax.ppermute(v, 'wide', flip(bit, wide))  44 us
    ppermute x8, waiting for transfers between devices, to_across(): return lax.ppermute(v, 'narrow', ACROSS)  35.3 us
    ppermute x8, starting transfers between devices, to_across(): return lax.ppermute(v, 'narrow', ACROSS)  14.1 us
    ppermute x18, waiting for transfers between devices, to_core(): return lax.ppermute(v, 'narrow', CORE)  14 us
    ppermute x7, starting transfers between devices, over(): return lax.ppermute(v, 'wide', flip(bit, wide))  11.3 us
  transfers between devices with their start and end apart: 33, of which 22 were waited for; matrix products, arithmetic and copies ran while one was open for 1% of the time, Pallas kernels for 25%

profile of v3, /device:TPU:0, one launch (start us, length us, event | category | flops | bytes accessed | tf_op | source)
XLA Modules:
  0.0 212.1 jit_solution(7004067396293475029)
XLA Ops:
  2.0 7.3 %self_fwd.1 = (bf16[3,512,192]{2,1,0:T(8,128)(2,1)}, bf16[3,512,512]{2,1,0:T(8,128)(2,1)}, bf16[512,192]{1,0:T(8,128)(2,1)}, bf16[256,768]{1,0:T(8,128)(2,1)}, f32[256,768]{1,0:T(8,128)}) custom-call(s32[7]{0:T(128)} %stack.27.at_ref, bf16[512,768]{1,0:T(8,128)(2,1)} %refs_5_.7, bf16[3,192,768]{2,1,0:T(8,128)(2,1)} %bitcast.29, bf16[192,768]{1,0:T(8,128)(2,1)} %refs_2_.11, ...), custom_call_target="tpu_custom_call" | custom-call | flops 440000000 | bytes 1000 | tf_op jit(solution)/shard_map/self_fwd/pallas_call | solution.py:160
  9.8 2.6 %collective-permute-start.2 = (bf16[416,768]{1,0:T(8,128)(2,1)S(1)}, bf16[416,768]{1,0:T(8,128)(2,1)S(1)}, u32[]{:S(2)}, u32[]{:S(2)}) collective-permute-start(bf16[416,768]{1,0:T(8,128)(2,1)S(1)} %bitcast.31), channel_id=1, source_target_pairs={{0,2},{1,3},{2,0},{3,1},{4,6},{5,7},{6,4},{7,5},{8,10},{9,11},{10,... | collective-permute-start | bytes 1916936 | tf_op jit(solution)/shard_map/ppermute | solution.py:1062
  13.6 1.9 collective-permute-start.1
  15.5 2.8 %copy-done = s32[512,3,4,256]{3,2,1,0:T(4,128)S(1)} copy-done((s32[512,3,4,256]{3,2,1,0:T(4,128)S(1)}, s32[512,3,4,256]{3,2,1,0:T(4,128)}, u32[]{:S(2)}) %copy-start) | copy-done | bytes 6291480
  18.3 9.6 %mask.2.refs_4_ = bf16[3,256,1664]{2,1,0:T(8,128)(2,1)S(1)} custom-call(s32[7]{0:T(128)S(1)} %copy-done.12, s32[4,3072,128]{2,1,0:T(8,128)S(1)} %bitcast.23), custom_call_target="tpu_custom_call" | custom-call | flops 1100000000 | bytes 1000 | tf_op jit(solution)/shard_map/mask/pallas_call | solution.py:160
  28.6 9.6 %mask.3.refs_5_ = bf16[3,256,1664]{2,1,0:T(8,128)(2,1)S(1)} custom-call(s32[7]{0:T(128)S(1)} %copy-done.12, s32[4,3072,128]{2,1,0:T(8,128)S(1)} %bitcast.24), custom_call_target="tpu_custom_call" | custom-call | flops 1100000000 | bytes 1000 | tf_op jit(solution)/shard_map/mask/pallas_call | solution.py:160
  39.4 2.3 %keys_values.1 = (bf16[3,1664,128]{2,1,0:T(8,128)(2,1)S(1)}, bf16[3,1664,128]{2,1,0:T(8,128)(2,1)S(1)}) custom-call(s32[7]{0:T(128)S(1)} %copy-done.12, bf16[416,768]{1,0:T(8,128)(2,1)S(1)} %bitcast.33, bf16[416,768]{1,0:T(8,128)(2,1)S(1)} %collective-permute-done.3.refs_1_, bf16[416,768]{1,0:T(8,128)(2,1)S(1)} %collective-permute-done.2.refs_2_, ...), custom_call_target="tpu_custom_call" | custom-call | flops 220000000 | bytes 1000 | tf_op jit(solution)/shard_map/keys_values/pallas_call | solution.py:160
  41.7 7.7 %cross_fwd.1 = (f32[256,768]{1,0:T(8,128)S(1)}, bf16[256,768]{1,0:T(8,128)(2,1)S(1)}, bf16[3,512,1664]{2,1,0:T(8,128)(2,1)S(1)}, f32[3,512,128]{2,1,0:T(8,128)S(...) custom-call(s32[7]{0:T(128)S(1)} %copy-done.12, bf16[256,768]{1,0:T(8,128)(2,1)S(1)} %get-tuple-element.123.refs_0_.refs_6_, ...), custom_call_target="tpu_custom_call" | custom-call | flops 990000000 | bytes 1000 | tf_op jit(solution)/shard_map/cross_fwd/pallas_call | solution.py:160
  49.9 1.3 collective-permute-done.6
  51.4 1.6 collective-permute-start.7
  53.0 9.8 %collective-permute-done.7.refs_2_ = bf16[256,768]{1,0:T(8,128)(2,1)S(1)} collective-permute-done((bf16[256,768]{1,0:T(8,128)(2,1)S(1)}, bf16[256,768]{1,0:T(8,128)(2,1)S(1)}, u32[]{:S(2)}, u32[]{:S(2)}) %collective-permute-start.7) | collective-permute-done | bytes 393248 | tf_op jit(solution)/shard_map/ppermute | solution.py:1062
  63.9 1.7 collective-permute-done.8.refs_1_
  65.6 3.5 %feed_up.1 = (f32[256,768]{1,0:T(8,128)S(1)}, bf16[256,768]{1,0:T(8,128)(2,1)S(1)}, bf16[512,768]{1,0:T(8,128)(2,1)S(1)}, f32[512,768]{1,0:T(8,128)S(1)}) custom-call(s32[7]{0:T(128)S(1)} %copy-done.12, bf16[256,768]{1,0:T(8,128)(2,1)S(1)} %get-tuple-element.133.refs_0_, bf16[256,768]{1,0:T(8,128)(2,1)S(1)} %collective-permute-done.8.refs_1_, ...), custom_call_target="tpu_custom_call" | custom-call | flops 440000000 | bytes 1000 | tf_op jit(solution)/shard_map/feed_up/pallas_call | solution.py:160
  69.3 1.6 collective-permute-done.9
  71.0 1.6 collective-permute-start.10
  72.6 9.6 %collective-permute-done.10.refs_2_ = bf16[256,768]{1,0:T(8,128)(2,1)S(1)} collective-permute-done((bf16[256,768]{1,0:T(8,128)(2,1)S(1)}, bf16[256,768]{1,0:T(8,128)(2,1)S(1)}, u32[]{:S(2)}, u32[]{:S(2)}) %collective-permute-start.10) | collective-permute-done | bytes 393248 | tf_op jit(solution)/shard_map/ppermute | solution.py:1062
  82.2 1.7 third_norm.1
  84.0 1.7 collective-permute-done.11.refs_1_.refs_4_
  85.7 2.1 %feed_down.1 = (f32[256,768]{1,0:T(8,128)S(1)}, bf16[256,768]{1,0:T(8,128)(2,1)S(1)}, bf16[512,768]{1,0:T(8,128)(2,1)S(1)}, f32[1,768]{1,0:T(1,128)S(1)}) custom-call(s32[7]{0:T(128)S(1)} %copy-done.12, bf16[256,768]{1,0:T(8,128)(2,1)S(1)} %get-tuple-element.137.refs_0_.refs_3_, bf16[256,768]{1,0:T(8,128)(2,1)S(1)} %collective-permute-done.11.refs_1_.refs_4_, ...), custom_call_target="tpu_custom_call" | custom-call | flops 330000000 | bytes 1000 | tf_op jit(solution)/shard_map/feed_down/pallas_call | solution.py:160
  88.0 1.6 collective-permute-done.12
  89.7 1.6 collective-permute-start.13
  91.3 3.4 %feed_grads.1 = (bf16[384,1536]{1,0:T(8,128)(2,1)S(1)}, f32[4,96,1536]{2,1,0:T(8,128)S(1)}) custom-call(s32[7]{0:T(128)S(1)} %copy-done.12, bf16[256,768]{1,0:T(8,128)(2,1)S(1)} %get-tuple-element.133.refs_0_, bf16[256,768]{1,0:T(8,128)(2,1)S(1)} %collective-permute-done.8.refs_1_, bf16[512,768]{1,0:T(8,128)(2,1)S(1)} %get-tuple-element.142.refs_2_, ...), custom_call_target="tpu_custom_call" | custom-call | flops 440000000 | bytes 1000 | tf_op jit(solution)/shard_map/feed_grads/pallas_call | solution.py:160
  94.8 6.2 %collective-permute-done.13.refs_2_ = bf16[256,768]{1,0:T(8,128)(2,1)S(1)} collective-permute-done((bf16[256,768]{1,0:T(8,128)(2,1)S(1)}, bf16[256,768]{1,0:T(8,128)(2,1)S(1)}, u32[]{:S(2)}, u32[]{:S(2)}) %collective-permute-start.13) | collective-permute-done | bytes 393248 | tf_op jit(solution)/shard_map/ppermute | solution.py:1062
  102.2 1.6 collective-permute-start.17
  103.9 9.3 %cross_bwd.1 = (f32[256,768]{1,0:T(8,128)S(1)}, bf16[256,768]{1,0:T(8,128)(2,1)S(1)}, bf16[512,192]{1,0:T(8,128)(2,1)S(1)}, bf16[3,1664,128]{2,1,0:T(8,128)(2,1)S(1)}, f32[2,192]{1,0:T(2,128)S(1)}) custom-call(s32[7]{0:T(128)S(1)} %copy-done.12, bf16[256,768]{1,0:T(8,128)(2,1)S(1)} %get-tuple-element.147.refs_0_.refs_4_, ...), custom_call_target="tpu_custom_call" | custom-call | flops 1210000000 | bytes 1000 | tf_op jit(solution)/shard_map/cross_bwd/pallas_call | solution.py:160
  113.5 1.6 collective-permute-done.15
  115.1 1.6 collective-permute-start.16
  116.7 3.5 %cross_grads.1 = (bf16[384,768]{1,0:T(8,128)(2,1)S(1)}, f32[4,96,768]{2,1,0:T(8,128)S(1)}) custom-call(s32[7]{0:T(128)S(1)} %copy-done.12, bf16[416,768]{1,0:T(8,128)(2,1)S(1)} %bitcast.34, bf16[416,768]{1,0:T(8,128)(2,1)S(1)} %collective-permute-done.3.refs_1_, bf16[416,768]{1,0:T(8,128)(2,1)S(1)} %collective-permute-done.2.refs_2_, ...), custom_call_target="tpu_custom_call" | custom-call | flops 440000000 | bytes 1000 | tf_op jit(solution)/shard_map/cross_grads/pallas_call | solution.py:160
  120.2 10.4 %collective-permute-done.17.refs_1_ = bf16[384,1536]{1,0:T(8,128)(2,1)S(1)} collective-permute-done((bf16[384,1536]{1,0:T(8,128)(2,1)S(1)}, bf16[384,1536]{1,0:T(8,128)(2,1)S(1)}, u32[]{:S(2)}, u32[]{:S(2)}) %collective-permute-start.17) | collective-permute-done | bytes 1179680 | tf_op jit(solution)/shard_map/ppermute | solution.py:1065
  131.5 2.1 store_grad.1
  134.9 1.7 collective-permute-done.18.refs_1_
  136.8 1.6 collective-permute-start.23
  138.3 1.6 collective-permute-start.24
  141.7 5.2 %self_bwd.1 = (bf16[512,768]{1,0:T(8,128)(2,1)S(1)}, f32[256,768]{1,0:T(8,128)S(1)}, bf16[416,768]{1,0:T(8,128)(2,1)S(1)}, f32[4,96,768]{2,1,0:T(8,128)S(1)}, f32[16,768]{1,0:T(8,128)S(1)}) custom-call(s32[7]{0:T(128)S(1)} %copy-done.12, bf16[256,768]{1,0:T(8,128)(2,1)S(1)} %get-tuple-element.166.refs_0_, ...), custom_call_target="tpu_custom_call" | custom-call | flops 660000000 | bytes 1000 | tf_op jit(solution)/shard_map/self_bwd/pallas_call | solution.py:160
  147.7 5.3 %collective-permute-done.23.refs_2_ = bf16[384,768]{1,0:T(8,128)(2,1)S(1)} collective-permute-done((bf16[384,768]{1,0:T(8,128)(2,1)S(1)}, bf16[384,768]{1,0:T(8,128)(2,1)S(1)}, u32[]{:S(2)}, u32[]{:S(2)}) %collective-permute-start.23) | collective-permute-done | bytes 589856 | tf_op jit(solution)/shard_map/ppermute | solution.py:1065
  154.4 2.7 %collective-permute-start.25 = (bf16[96,1536]{1,0:T(8,128)(2,1)S(1)}, bf16[96,1536]{1,0:T(8,128)(2,1)S(1)}, u32[]{:S(2)}, u32[]{:S(2)}) collective-permute-start(bf16[96,1536]{1,0:T(8,128)(2,1)S(1)} %get-tuple-element.184), channel_id=1, source_target_pairs={{0,16},{4,20},{8,24},{12,28},{16,0},{20,4},{24,8},{28,12},{1,17},{... | collective-permute-start | bytes 884744 | tf_op jit(solution)/shard_map/ppermute | solution.py:1065
  157.0 12.8 %collective-permute-done.25.refs_1_ = bf16[96,1536]{1,0:T(8,128)(2,1)S(1)} collective-permute-done((bf16[96,1536]{1,0:T(8,128)(2,1)S(1)}, bf16[96,1536]{1,0:T(8,128)(2,1)S(1)}, u32[]{:S(2)}, u32[]{:S(2)}) %collective-permute-start.25) | collective-permute-done | bytes 294944 | tf_op jit(solution)/shard_map/ppermute | solution.py:1065
  169.8 1.4 last_stage.2
  172.8 1.5 collective-permute-done.27.refs_1_
  174.5 1.6 collective-permute-start.28
  176.0 12.9 %collective-permute-done.29.refs_1_ = bf16[208,1536]{1,0:T(8,128)(2,1)S(1)} collective-permute-done((bf16[208,1536]{1,0:T(8,128)(2,1)S(1)}, bf16[208,1536]{1,0:T(8,128)(2,1)S(1)}, u32[]{:S(2)}, u32[]{:S(2)}) %collective-permute-start.29) | collective-permute-done | bytes 639008 | tf_op jit(solution)/shard_map/ppermute | solution.py:1065
  189.9 1.6 collective-permute-start.31
  191.5 2.3 %collective-permute-start.32 = (bf16[112,1536]{1,0:T(8,128)(2,1)S(1)}, bf16[112,1536]{1,0:T(8,128)(2,1)S(1)}, u32[]{:S(2)}, u32[]{:S(2)}) collective-permute-start(bf16[112,1536]{1,0:T(8,128)(2,1)S(1)} %get-tuple-element.197), channel_id=1, source_target_pairs={{0,16},{4,20},{8,24},{12,28},{16,0},{20,4},{24,8},{28,12},{1,17},{... | collective-permute-start | bytes 1032200 | tf_op jit(solution)/shard_map/ppermute | solution.py:1065
  193.8 1.5 join_halves.2
  195.3 1.8 join_halves.3
  197.1 9.7 %collective-permute-done.31 = bf16[416,768]{1,0:T(8,128)(2,1)S(1)} collective-permute-done((bf16[416,768]{1,0:T(8,128)(2,1)S(1)}, bf16[416,768]{1,0:T(8,128)(2,1)S(1)}, u32[]{:S(2)}, u32[]{:S(2)}) %collective-permute-start.31) | collective-permute-done | bytes 639008 | tf_op jit(solution)/shard_map/ppermute | solution.py:1062
  208.0 1.9 collective-permute-done.32.refs_1_
  209.9 1.6 last_stage.3
  (100 shorter events, 18.7 us)
Async XLA Ops:
  0.7 9.2 %copy-start.6 = (bf16[1,416,768]{2,1,0:T(8,128)(2,1)S(1)}, bf16[1,416,768]{2,1,0:T(8,128)(2,1)}, u32[]{:S(2)}) copy-start(bf16[1,416,768]{2,1,0:T(8,128)(2,1)} %param.20) | copy-start | bytes 1916932
  9.3 6.2 %copy-start.12 = (s32[7]{0:T(128)S(1)}, s32[7]{0:T(128)}, u32[]{:S(2)}) copy-start(s32[7]{0:T(128)} %stack.27.at_ref) | copy-start | bytes 88
  9.3 3.1 %collective-permute-start = (bf16[256,768]{1,0:T(8,128)(2,1)}, bf16[256,768]{1,0:T(8,128)(2,1)S(1)}, u32[]{:S(2)}, u32[]{:S(2)}) collective-permute-start(bf16[256,768]{1,0:T(8,128)(2,1)} %get-tuple-element.118), channel_id=1, source_target_pairs={{0,1},{1,0},{2,3},{3,2},{4,5},{5,4},{6,7},{7,6},{8,9},{9,8},{10,11... | collective-permute-start | bytes 1179656 | tf_op jit(solution)/shard_map/ppermute | solution.py:1059
  9.8 18.1 %collective-permute-start.2 = (bf16[416,768]{1,0:T(8,128)(2,1)S(1)}, bf16[416,768]{1,0:T(8,128)(2,1)S(1)}, u32[]{:S(2)}, u32[]{:S(2)}) collective-permute-start(bf16[416,768]{1,0:T(8,128)(2,1)S(1)} %bitcast.31), channel_id=1, source_target_pairs={{0,2},{1,3},{2,0},{3,1},{4,6},{5,7},{6,4},{7,5},{8,10},{9,11},{10,... | collective-permute-start | bytes 1916936 | tf_op jit(solution)/shard_map/ppermute | solution.py:1062
  13.6 24.6 %collective-permute-start.1 = (bf16[256,768]{1,0:T(8,128)(2,1)S(1)}, bf16[256,768]{1,0:T(8,128)(2,1)S(1)}, u32[]{:S(2)}, u32[]{:S(2)}) collective-permute-start(bf16[256,768]{1,0:T(8,128)(2,1)S(1)} %add_convert_fusion.6.refs_0_), channel_id=1, source_target_pairs={{0,2},{1,3},{2,0},{3,1},{4,6},{5,7},{6,4},{7,5},{8,10},{9,11},{10,... | collective-permute-start | bytes 1179656 | tf_op jit(solution)/shard_map/ppermute | solution.py:1062
  18.3 10.2 %copy-start.17 = (f32[768]{0:T(1024)S(1)}, f32[768]{0:T(1024)}, u32[]{:S(2)}) copy-start(f32[768]{0:T(1024)} %param.27) | copy-start | bytes 9220
  28.0 11.4 %collective-permute-start.3 = (bf16[416,768]{1,0:T(8,128)(2,1)S(1)}, bf16[416,768]{1,0:T(8,128)(2,1)S(1)}, u32[]{:S(2)}, u32[]{:S(2)}) collective-permute-start(bf16[416,768]{1,0:T(8,128)(2,1)S(1)} %bitcast.32), channel_id=1, source_target_pairs={{0,1},{1,0},{2,3},{3,2},{4,5},{5,4},{6,7},{7,6},{8,9},{9,8},{10,11... | collective-permute-start | bytes 1916936 | tf_op jit(solution)/shard_map/ppermute | solution.py:1059
  28.0 11.3 %collective-permute-start.4 = (bf16[416,768]{1,0:T(8,128)(2,1)S(1)}, bf16[416,768]{1,0:T(8,128)(2,1)S(1)}, u32[]{:S(2)}, u32[]{:S(2)}) collective-permute-start(bf16[416,768]{1,0:T(8,128)(2,1)S(1)} %collective-permute-done.2.refs_2_), channel_id=1, source_target_pairs={{0,1},{1,0},{2,3},{3,2},{4,5},{5,4},{6,7},{7,6},{8,9},{9,8},{10,11... | collective-permute-start | bytes 1916936 | tf_op jit(solution)/shard_map/ppermute | solution.py:1059
  28.5 9.7 %copy-start.2 = (bf16[512,768]{1,0:T(8,128)(2,1)S(1)}, bf16[512,768]{1,0:T(8,128)(2,1)}, u32[]{:S(2)}) copy-start(bf16[512,768]{1,0:T(8,128)(2,1)} %refs_5_.7) | copy-start | bytes 2359300
  28.6 9.7 %copy-start.13 = (f32[3,768]{1,0:T(4,128)S(1)}, f32[3,768]{1,0:T(4,128)}, u32[]{:S(2)}) copy-start(f32[3,768]{1,0:T(4,128)} %refs_4_.7) | copy-start | bytes 27652
  28.6 9.7 %copy-start.15 = (f32[3,768]{1,0:T(4,128)S(1)}, f32[3,768]{1,0:T(4,128)}, u32[]{:S(2)}) copy-start(f32[3,768]{1,0:T(4,128)} %refs_6_.1) | copy-start | bytes 27652
  39.2 2.5 %collective-permute-start.5 = (bf16[256,768]{1,0:T(8,128)(2,1)S(1)}, bf16[256,768]{1,0:T(8,128)(2,1)S(1)}, u32[]{:S(2)}, u32[]{:S(2)}) collective-permute-start(bf16[256,768]{1,0:T(8,128)(2,1)S(1)} %get-tuple-element.123.refs_0_.refs_6_), channel_id=1, source_target_pairs={{0,1},{1,0},{2,3},{3,2},{4,5},{5,4},{6,7},{7,6},{8,9},{9,8},{10,11... | collective-permute-start | bytes 1179656 | tf_op jit(solution)/shard_map/ppermute | solution.py:1059
  49.5 1.8 collective-permute-start.6
  51.3 12.6 %copy-start.19 = (f32[768]{0:T(1024)S(1)}, f32[768]{0:T(1024)}, u32[]{:S(2)}) copy-start(f32[768]{0:T(1024)} %param.33) | copy-start | bytes 9220
  51.3 14.3 %copy-start.3 = (bf16[768,768]{1,0:T(8,128)(2,1)S(1)}, bf16[768,768]{1,0:T(8,128)(2,1)}, u32[]{:S(2)}) copy-start(bf16[768,768]{1,0:T(8,128)(2,1)} %refs_2_.9) | copy-start | bytes 3538948
  51.3 14.3 %copy-start.4 = (bf16[768,768]{1,0:T(8,128)(2,1)S(1)}, bf16[768,768]{1,0:T(8,128)(2,1)}, u32[]{:S(2)}) copy-start(bf16[768,768]{1,0:T(8,128)(2,1)} %refs_3_.7) | copy-start | bytes 3538948
  51.4 11.5 %collective-permute-start.7 = (bf16[256,768]{1,0:T(8,128)(2,1)S(1)}, bf16[256,768]{1,0:T(8,128)(2,1)S(1)}, u32[]{:S(2)}, u32[]{:S(2)}) collective-permute-start(bf16[256,768]{1,0:T(8,128)(2,1)S(1)} %add_convert_fusion.5.refs_1_), channel_id=1, source_target_pairs={{0,2},{1,3},{2,0},{3,1},{4,6},{5,7},{6,4},{7,5},{8,10},{9,11},{10,... | collective-permute-start | bytes 1179656 | tf_op jit(solution)/shard_map/ppermute | solution.py:1062
  63.8 1.8 collective-permute-start.8
  69.1 13.1 %copy-start.10 = (bf16[512,768]{1,0:T(8,128)(2,1)S(1)}, bf16[512,768]{1,0:T(8,128)(2,1)}, u32[]{:S(2)}) copy-start(bf16[512,768]{1,0:T(8,128)(2,1)} %refs_3_.6) | copy-start | bytes 2359300
  69.1 1.8 collective-permute-start.9
  71.0 11.2 %collective-permute-start.10 = (bf16[256,768]{1,0:T(8,128)(2,1)S(1)}, bf16[256,768]{1,0:T(8,128)(2,1)S(1)}, u32[]{:S(2)}, u32[]{:S(2)}) collective-permute-start(bf16[256,768]{1,0:T(8,128)(2,1)S(1)} %add_convert_fusion.4.refs_1_), channel_id=1, source_target_pairs={{0,2},{1,3},{2,0},{3,1},{4,6},{5,7},{6,4},{7,5},{8,10},{9,11},{10,... | collective-permute-start | bytes 1179656 | tf_op jit(solution)/shard_map/ppermute | solution.py:1062
  83.9 1.8 collective-permute-start.11
  87.8 1.8 collective-permute-start.12
  89.7 11.2 %collective-permute-start.13 = (bf16[256,768]{1,0:T(8,128)(2,1)S(1)}, bf16[256,768]{1,0:T(8,128)(2,1)S(1)}, u32[]{:S(2)}, u32[]{:S(2)}) collective-permute-start(bf16[256,768]{1,0:T(8,128)(2,1)S(1)} %add_convert_fusion.3.refs_1_), channel_id=1, source_target_pairs={{0,2},{1,3},{2,0},{3,1},{4,6},{5,7},{6,4},{7,5},{8,10},{9,11},{10,... | collective-permute-start | bytes 1179656 | tf_op jit(solution)/shard_map/ppermute | solution.py:1062
  102.2 1.8 collective-permute-start.14
  102.2 28.4 %collective-permute-start.17 = (bf16[384,1536]{1,0:T(8,128)(2,1)S(1)}, bf16[384,1536]{1,0:T(8,128)(2,1)S(1)}, u32[]{:S(2)}, u32[]{:S(2)}) collective-permute-start(bf16[384,1536]{1,0:T(8,128)(2,1)S(1)} %get-tuple-element.144), channel_id=1, source_target_pairs={{0,4},{4,0},{8,12},{12,8},{16,20},{20,16},{24,28},{28,24},{1,5},{5... | collective-permute-start | bytes 3538952 | tf_op jit(solution)/shard_map/ppermute | solution.py:1065
  113.3 1.8 collective-permute-start.15
  115.1 18.5 %collective-permute-start.16 = (bf16[256,768]{1,0:T(8,128)(2,1)S(1)}, bf16[256,768]{1,0:T(8,128)(2,1)S(1)}, u32[]{:S(2)}, u32[]{:S(2)}) collective-permute-start(bf16[256,768]{1,0:T(8,128)(2,1)S(1)} %add_convert_fusion.2.refs_1_), channel_id=1, source_target_pairs={{0,2},{1,3},{2,0},{3,1},{4,6},{5,7},{6,4},{7,5},{8,10},{9,11},{10,... | collective-permute-start | bytes 1179656 | tf_op jit(solution)/shard_map/ppermute | solution.py:1062
  131.5 10.2 %copy-start.7 = (bf16[3,512,512]{2,1,0:T(8,128)(2,1)S(1)}, bf16[3,512,512]{2,1,0:T(8,128)(2,1)}, u32[]{:S(2)}) copy-start(bf16[3,512,512]{2,1,0:T(8,128)(2,1)} %get-tuple-element.170.refs_4_) | copy-start | bytes 4718596
  133.5 8.1 %copy-start.5 = (bf16[3,768,192]{1,2,0:T(8,128)(2,1)S(1)}, bf16[3,768,192]{1,2,0:T(8,128)(2,1)}, u32[]{:S(2)}) copy-start(bf16[3,768,192]{1,2,0:T(8,128)(2,1)} %param.24) | copy-start | bytes 2654212
  133.6 8.1 %copy-start.9 = (bf16[192,768]{1,0:T(8,128)(2,1)S(1)}, bf16[192,768]{1,0:T(8,128)(2,1)}, u32[]{:S(2)}) copy-start(bf16[192,768]{1,0:T(8,128)(2,1)} %refs_2_.11) | copy-start | bytes 884740
  133.6 8.1 %copy-start.11 = (bf16[3,512,192]{2,1,0:T(8,128)(2,1)S(1)}, bf16[3,512,192]{2,1,0:T(8,128)(2,1)}, u32[]{:S(2)}) copy-start(bf16[3,512,192]{2,1,0:T(8,128)(2,1)} %get-tuple-element.169.refs_3_) | copy-start | bytes 1769476
  133.6 8.1 %copy-start.14 = (bf16[512,192]{1,0:T(8,128)(2,1)S(1)}, bf16[512,192]{1,0:T(8,128)(2,1)}, u32[]{:S(2)}) copy-start(bf16[512,192]{1,0:T(8,128)(2,1)} %get-tuple-element.172.refs_8_) | copy-start | bytes 589828
  134.8 1.8 collective-permute-start.18
  136.6 3.8 %collective-permute-start.19 = (bf16[2,416,768]{2,1,0:T(8,128)(2,1)S(1)}, bf16[2,416,768]{2,1,0:T(8,128)(2,1)S(1)}, u32[]{:S(2)}, u32[]{:S(2)}) collective-permute-start(bf16[2,416,768]{2,1,0:T(8,128)(2,1)S(1)} %get-tuple-element.167), channel_id=1, source_target_pairs={{0,1},{1,0},{2,3},{3,2},{4,5},{5,4},{6,7},{7,6},{8,9},{9,8},{10,11... | collective-permute-start | bytes 3833864 | tf_op jit(solution)/shard_map/ppermute | solution.py:1059
  136.8 16.2 %collective-permute-start.23 = (bf16[384,768]{1,0:T(8,128)(2,1)S(1)}, bf16[384,768]{1,0:T(8,128)(2,1)S(1)}, u32[]{:S(2)}, u32[]{:S(2)}) collective-permute-start(bf16[384,768]{1,0:T(8,128)(2,1)S(1)} %get-tuple-element.157), channel_id=1, source_target_pairs={{0,4},{4,0},{8,12},{12,8},{16,20},{20,16},{24,28},{28,24},{1,5},{5... | collective-permute-start | bytes 1769480 | tf_op jit(solution)/shard_map/ppermute | solution.py:1065
  138.3 15.3 %collective-permute-start.24 = (bf16[192,1536]{1,0:T(8,128)(2,1)S(1)}, bf16[192,1536]{1,0:T(8,128)(2,1)S(1)}, u32[]{:S(2)}, u32[]{:S(2)}) collective-permute-start(bf16[192,1536]{1,0:T(8,128)(2,1)S(1)} %get-tuple-element.160), channel_id=1, source_target_pairs={{0,8},{4,12},{8,0},{12,4},{16,24},{20,28},{24,16},{28,20},{1,9},{5... | collective-permute-start | bytes 1769480 | tf_op jit(solution)/shard_map/ppermute | solution.py:1065
  139.9 1.2 collective-permute-start.20
  139.9 1.4 collective-permute-start.21
  140.4 1.2 collective-permute-start.22
  146.9 24.4 %collective-permute-start.26 = (bf16[416,768]{1,0:T(8,128)(2,1)S(1)}, bf16[416,768]{1,0:T(8,128)(2,1)S(1)}, u32[]{:S(2)}, u32[]{:S(2)}) collective-permute-start(bf16[416,768]{1,0:T(8,128)(2,1)S(1)} %get-tuple-element.191), channel_id=1, source_target_pairs={{0,4},{4,0},{8,12},{12,8},{16,20},{20,16},{24,28},{28,24},{1,5},{5... | collective-permute-start | bytes 1916936 | tf_op jit(solution)/shard_map/ppermute | solution.py:1065
  154.4 15.4 %collective-permute-start.25 = (bf16[96,1536]{1,0:T(8,128)(2,1)S(1)}, bf16[96,1536]{1,0:T(8,128)(2,1)S(1)}, u32[]{:S(2)}, u32[]{:S(2)}) collective-permute-start(bf16[96,1536]{1,0:T(8,128)(2,1)S(1)} %get-tuple-element.184), channel_id=1, source_target_pairs={{0,16},{4,20},{8,24},{12,28},{16,0},{20,4},{24,8},{28,12},{1,17},{... | collective-permute-start | bytes 884744 | tf_op jit(solution)/shard_map/ppermute | solution.py:1065
  172.0 2.4 %collective-permute-start.27 = (bf16[512,768]{1,0:T(8,128)(2,1)S(1)}, bf16[512,768]{1,0:T(8,128)(2,1)S(1)}, u32[]{:S(2)}, u32[]{:S(2)}) collective-permute-start(bf16[512,768]{1,0:T(8,128)(2,1)S(1)} %get-tuple-element.193), channel_id=1, source_target_pairs={{0,1},{1,0},{2,3},{3,2},{4,5},{5,4},{6,7},{7,6},{8,9},{9,8},{10,11... | collective-permute-start | bytes 2359304 | tf_op jit(solution)/shard_map/ppermute | solution.py:1059
  172.1 16.8 %collective-permute-start.29 = (bf16[208,1536]{1,0:T(8,128)(2,1)S(1)}, bf16[208,1536]{1,0:T(8,128)(2,1)S(1)}, u32[]{:S(2)}, u32[]{:S(2)}) collective-permute-start(bf16[208,1536]{1,0:T(8,128)(2,1)S(1)} %get-tuple-element.192), channel_id=1, source_target_pairs={{0,8},{4,12},{8,0},{12,4},{16,24},{20,28},{24,16},{28,20},{1,9},{5... | collective-permute-start | bytes 1916936 | tf_op jit(solution)/shard_map/ppermute | solution.py:1065
  174.5 15.1 %collective-permute-start.28 = (bf16[256,768]{1,0:T(8,128)(2,1)S(1)}, bf16[256,768]{1,0:T(8,128)(2,1)S(1)}, u32[]{:S(2)}, u32[]{:S(2)}) collective-permute-start(bf16[256,768]{1,0:T(8,128)(2,1)S(1)} %add_convert_fusion.1), channel_id=1, source_target_pairs={{0,2},{1,3},{2,0},{3,1},{4,6},{5,7},{6,4},{7,5},{8,10},{9,11},{10,... | collective-permute-start | bytes 1179656 | tf_op jit(solution)/shard_map/ppermute | solution.py:1062
  189.7 5.6 %collective-permute-start.30 = (f32[256,768]{1,0:T(8,128)S(1)}, f32[256,768]{1,0:T(8,128)S(1)}, u32[]{:S(2)}, u32[]{:S(2)}) collective-permute-start(f32[256,768]{1,0:T(8,128)S(1)} %add_add_fusion.refs_0_), channel_id=1, source_target_pairs={{0,1},{1,0},{2,3},{3,2},{4,5},{5,4},{6,7},{7,6},{8,9},{9,8},{10,11... | collective-permute-start | bytes 2359304 | tf_op jit(solution)/shard_map/ppermute | solution.py:1059
  189.9 16.8 %collective-permute-start.31 = (bf16[416,768]{1,0:T(8,128)(2,1)S(1)}, bf16[416,768]{1,0:T(8,128)(2,1)S(1)}, u32[]{:S(2)}, u32[]{:S(2)}) collective-permute-start(bf16[416,768]{1,0:T(8,128)(2,1)S(1)} %fusion.1), channel_id=1, source_target_pairs={{0,2},{1,3},{2,0},{3,1},{4,6},{5,7},{6,4},{7,5},{8,10},{9,11},{10,... | collective-permute-start | bytes 1916936 | tf_op jit(solution)/shard_map/ppermute | solution.py:1062
  191.5 18.5 %collective-permute-start.32 = (bf16[112,1536]{1,0:T(8,128)(2,1)S(1)}, bf16[112,1536]{1,0:T(8,128)(2,1)S(1)}, u32[]{:S(2)}, u32[]{:S(2)}) collective-permute-start(bf16[112,1536]{1,0:T(8,128)(2,1)S(1)} %get-tuple-element.197), channel_id=1, source_target_pairs={{0,16},{4,20},{8,24},{12,28},{16,0},{20,4},{24,8},{28,12},{1,17},{... | collective-permute-start | bytes 1032200 | tf_op jit(solution)/shard_map/ppermute | solution.py:1065
  (6 other events, 15.7 us)

commit v4 on v3

--- a/solution.py
+++ b/solution.py
@@ -680,38 +680,6 @@
     )
 
 
-def store_gradient(at, dkv, w, nh):
-    _, slots, twice = dkv.shape
-    _, local, width = w.shape
-    hd = twice // 2
-    seg = slots // 4
-
-    def body(at, ins, outs, _):
-        dkv, w = ins
-        keep, send = outs
-        weights = []
-        for h in range(nh):
-            part = slice(h * hd, (h + 1) * hd)
-            weights += [w[1][part], w[2][part]]
-        weight = jnp.concatenate(weights, axis=0)
-        for slot in (1, 3, 0, 2):
-            rows = jnp.concatenate([dkv[h, slot * seg : (slot + 1) * seg, :] for h in range(nh)], axis=1)
-            part = mm(rows, weight)
-            if slot % 2 == 0:
-                keep[slot // 2] = part
-            else:
-                send[slot // 2] = part.astype(BF)
-
-    return launch(
-        body,
-        "store_grad",
-        at,
-        [near(dkv), near(w)],
-        [shape(2, seg, width), shape(2, seg, width, dtype=BF)],
-        us=2.6,
-    )
-
-
 def group_outs(width, columns, blocks, tail=0):
     if not blocks:
         return [shape(width, columns)]
@@ -774,36 +742,49 @@
     )
 
 
-def cross_grads(at, z_mine, z_other, mine, other, dquery, heads, shards, dkv, nh, blocks):
+def cross_grads(at, z_mine, z_other, mine, other, dquery, heads, shards, dkv, w, nh, blocks):
     half, width = mine.shape
     local = dquery.shape[1]
     hd = local // nh
     seg = shards[0].shape[0]
 
     def body(at, ins, outs, scratch):
-        shards, (z_mine, z_other, mine, other, dquery, heads, dkv) = ins[0:4], ins[4:]
+        shards, (dkv, w, z_mine, z_other, mine, other, dquery, heads) = ins[0:4], ins[4:]
+        store_send, store_keep = outs[:2]
+        group = outs[2:]
         (grad,) = scratch
-        grad[...] = mm(mine[...], dquery[:half], TN) + mm(other[...], dquery[half:], TN)
-        emit_group(at, grad, outs, blocks, 0, local)
-        grad[...] = mm(z_mine[...], heads[:half], TN) + mm(z_other[...], heads[half:], TN)
-        emit_group(at, grad, outs, blocks, 3 * local, local)
+        weights = []
+        for h in range(nh):
+            part = slice(h * hd, (h + 1) * hd)
+            weights += [w[1][part], w[2][part]]
+        weight = jnp.concatenate(weights, axis=0)
         both = None
         for slot, block in enumerate(shards):
             rows = jnp.concatenate([dkv[h, slot * seg : (slot + 1) * seg, :] for h in range(nh)], axis=1)
+            found = mm(rows, weight)
+            if slot % 2 == 0:
+                store_keep[slot // 2] = found
+            else:
+                store_send[slot // 2] = found.astype(BF)
             part = mm(block[...], rows, TN)
             both = part if both is None else both + part
         for i in range(2):
             grad[...] = jnp.concatenate([both[:, (2 * h + i) * hd : (2 * h + i + 1) * hd] for h in range(nh)], axis=1)
-            emit_group(at, grad, outs, blocks, (1 + i) * local, local)
+            emit_group(at, grad, group, blocks, (1 + i) * local, local)
+        grad[...] = mm(mine[...], dquery[:half], TN) + mm(other[...], dquery[half:], TN)
+        emit_group(at, grad, group, blocks, 0, local)
+        grad[...] = mm(z_mine[...], heads[:half], TN) + mm(z_other[...], heads[half:], TN)
+        emit_group(at, grad, group, blocks, 3 * local, local)
 
     return launch(
         body,
         "cross_grads",
         at,
-        [near(a) for a in (*shards, z_mine, z_other, mine, other, dquery, heads, dkv)],
-        group_outs(width, 4 * local, blocks),
+        [near(a) for a in (*shards, dkv, w, z_mine, z_other, mine, other, dquery, heads)],
+        [shape(2, seg, width, dtype=BF), shape(2, seg, width)] + group_outs(width, 4 * local, blocks),
         scratch=[pltpu.VMEM((width, local), F32)],
-        us=4,
+        mib=24,
+        us=5,
     )
 
 
@@ -1093,34 +1074,32 @@
     mixed_half, dlast, dlast_low, third_sums = third_norm(
         at, second_total, mine, to_across(mine), cotangent, row(fc2_bias), norm_gain, norm_shift
     )
-    dlast_other, third_other = to_core(dlast_low), to_core(third_sums)
+    dlast_other, third_other = tie((to_core(dlast_low), to_core(third_sums)))
     keep, send, dpre, fc1_sum = feed_down(at, dlast_low, dlast_other, fc1_weight, fc2_weight, slope)
     mine = chip_sum(keep, send)
     other = to_across(mine)
     feed_out = feed_grads(tie(at, mine), mid_low, mid_other, dpre, dlast_low, dlast_other, hidden, blocks)
     other = tie(other, feed_out[0])
     dsecond, z, second_sums = second_back(at, dlast, mine, other, second_total, norm_gain)
-    z_other, second_other = to_core(z), to_core(second_sums)
+    z_other, second_other = tie((to_core(z), to_core(second_sums)))
 
     keep, send, dquery, dkv, cross_sums = cross_backward(
         at, z, z_other, raised, inverse, query, keys, values, cross_w, out_weight, nh
     )
     mine = chip_sum(keep, send)
     other = to_across(mine)
-    cross_out = cross_grads(
-        tie(at, mine), z, z_other, after_low, after_other, dquery, heads, shards, dkv, nh, blocks
-    )
-    started = cross_out[0]
+    store_send, store_keep, *cross_out = cross_grads(
+        tie(at, mine), z, z_other, after_low, after_other, dquery, heads, shards, dkv, cross_w, nh, blocks
+    )
+    started = store_send
     if blocks:
-        feed_send, feed_keep = add_stage(tie(at, started), [feed_out[1]], [over(feed_out[0], 1)], None, 5)
+        feed_send, feed_keep = add_stage(tie(at, store_send), [feed_out[1]], [over(feed_out[0], 1)], None, 5)
         feed_next = over(feed_send, 2)
         started = feed_send
-    store_keep, store_send = store_gradient(tie(at, started), dkv, cross_w, nh)
-    other = tie(other, store_send)
+    other, store_send = tie((other, store_send), started)
+    store_close = to_core(store_send)
     dfirst, dfirst_low, first_sums = first_back(at, dsecond, mine, other, first_total, norm_gain)
-    dfirst_other, first_other = to_core(dfirst_low), to_core(first_sums)
-    store_close = to_core(tie(store_send, dfirst_other))
-    started = dfirst_low
+    dfirst_other, first_other = tie((to_core(dfirst_low), to_core(first_sums)))
 
     send, keep, *self_out, small = self_backward(
         tie(at, dfirst_other, store_close),

time: 212 us -> 208 us (0.981)
  waiting for transfers between devices: 93.3 us -> 90 us
    pallas_call x25 -> x24, Pallas kernels: 80.8 us -> 79.9 us  [launch(): pl.pallas_call(kernel, in_specs=in_specs, out_specs=out_specs, out_shape=...]
  transfers between devices with their start and end apart: 33 -> 33, of which waited for: 22 -> 19; matrix products, arithmetic and copies ran while one was open for 1% -> 1% of each run, Pallas kernels for 25% -> 26%
where the time goes in v4:
time: 208 us
  waiting for transfers between devices  90 us (43%)
  Pallas kernels  79.9 us (38%)
  starting transfers between devices  29 us (14%)
  local copies, waits for them, and re-layouts  4.14 us (2%)
  other arithmetic  3.17 us (2%)
    pallas_call x24, Pallas kernels, launch(): pl.pallas_call(kernel, in_specs=in_specs, out_specs=out_specs, out_shape=...  79.9 us
    ppermute x7, waiting for transfers between devices, over(): return lax.ppermute(v, 'wide', flip(bit, wide))  41.9 us
    ppermute x8, waiting for transfers between devices, to_across(): return lax.ppermute(v, 'narrow', ACROSS)  35.3 us
    ppermute x8, starting transfers between devices, to_across(): return lax.ppermute(v, 'narrow', ACROSS)  14 us
    ppermute x18, waiting for transfers between devices, to_core(): return lax.ppermute(v, 'narrow', CORE)  12.8 us
    ppermute x7, starting transfers between devices, over(): return lax.ppermute(v, 'wide', flip(bit, wide))  11 us
  transfers between devices with their start and end apart: 33, of which 19 were waited for; matrix products, arithmetic and copies ran while one was open for 1% of the time, Pallas kernels for 26%

profile of v4, /device:TPU:0, one launch (start us, length us, event | category | flops | bytes accessed | tf_op | source)
XLA Modules:
  0.0 208.2 jit_solution(4964782641894121185)
XLA Ops:
  2.0 7.2 %self_fwd.1 = (bf16[3,512,192]{2,1,0:T(8,128)(2,1)}, bf16[3,512,512]{2,1,0:T(8,128)(2,1)}, bf16[512,192]{1,0:T(8,128)(2,1)}, bf16[256,768]{1,0:T(8,128)(2,1)}, f32[256,768]{1,0:T(8,128)}) custom-call(s32[7]{0:T(128)} %stack.27.at_ref, bf16[512,768]{1,0:T(8,128)(2,1)} %refs_5_.7, bf16[3,192,768]{2,1,0:T(8,128)(2,1)} %bitcast.29, bf16[192,768]{1,0:T(8,128)(2,1)} %refs_2_.11, ...), custom_call_target="tpu_custom_call" | custom-call | flops 440000000 | bytes 1000 | tf_op jit(solution)/shard_map/self_fwd/pallas_call | solution.py:160
  9.8 2.6 %collective-permute-start.2 = (bf16[416,768]{1,0:T(8,128)(2,1)S(1)}, bf16[416,768]{1,0:T(8,128)(2,1)S(1)}, u32[]{:S(2)}, u32[]{:S(2)}) collective-permute-start(bf16[416,768]{1,0:T(8,128)(2,1)S(1)} %bitcast.31), channel_id=1, source_target_pairs={{0,2},{1,3},{2,0},{3,1},{4,6},{5,7},{6,4},{7,5},{8,10},{9,11},{10,... | collective-permute-start | bytes 1916936 | tf_op jit(solution)/shard_map/ppermute | solution.py:1043
  13.6 1.9 collective-permute-start.1
  15.5 2.8 %copy-done = s32[512,3,4,256]{3,2,1,0:T(4,128)S(1)} copy-done((s32[512,3,4,256]{3,2,1,0:T(4,128)S(1)}, s32[512,3,4,256]{3,2,1,0:T(4,128)}, u32[]{:S(2)}) %copy-start) | copy-done | bytes 6291480
  18.3 9.6 %mask.2.refs_4_ = bf16[3,256,1664]{2,1,0:T(8,128)(2,1)S(1)} custom-call(s32[7]{0:T(128)S(1)} %copy-done.12, s32[4,3072,128]{2,1,0:T(8,128)S(1)} %bitcast.23), custom_call_target="tpu_custom_call" | custom-call | flops 1100000000 | bytes 1000 | tf_op jit(solution)/shard_map/mask/pallas_call | solution.py:160
  28.6 9.6 %mask.3.refs_5_ = bf16[3,256,1664]{2,1,0:T(8,128)(2,1)S(1)} custom-call(s32[7]{0:T(128)S(1)} %copy-done.12, s32[4,3072,128]{2,1,0:T(8,128)S(1)} %bitcast.24), custom_call_target="tpu_custom_call" | custom-call | flops 1100000000 | bytes 1000 | tf_op jit(solution)/shard_map/mask/pallas_call | solution.py:160
  39.4 2.3 %keys_values.1 = (bf16[3,1664,128]{2,1,0:T(8,128)(2,1)S(1)}, bf16[3,1664,128]{2,1,0:T(8,128)(2,1)S(1)}) custom-call(s32[7]{0:T(128)S(1)} %copy-done.12, bf16[416,768]{1,0:T(8,128)(2,1)S(1)} %bitcast.33, bf16[416,768]{1,0:T(8,128)(2,1)S(1)} %collective-permute-done.3.refs_1_, bf16[416,768]{1,0:T(8,128)(2,1)S(1)} %collective-permute-done.2.refs_2_, ...), custom_call_target="tpu_custom_call" | custom-call | flops 220000000 | bytes 1000 | tf_op jit(solution)/shard_map/keys_values/pallas_call | solution.py:160
  41.7 7.7 %cross_fwd.1 = (f32[256,768]{1,0:T(8,128)S(1)}, bf16[256,768]{1,0:T(8,128)(2,1)S(1)}, bf16[3,512,1664]{2,1,0:T(8,128)(2,1)S(1)}, f32[3,512,128]{2,1,0:T(8,128)S(...) custom-call(s32[7]{0:T(128)S(1)} %copy-done.12, bf16[256,768]{1,0:T(8,128)(2,1)S(1)} %get-tuple-element.128.refs_0_.refs_8_, ...), custom_call_target="tpu_custom_call" | custom-call | flops 990000000 | bytes 1000 | tf_op jit(solution)/shard_map/cross_fwd/pallas_call | solution.py:160
  49.9 1.3 collective-permute-done.6
  51.4 1.6 collective-permute-start.7
  53.0 9.8 %collective-permute-done.7.refs_2_ = bf16[256,768]{1,0:T(8,128)(2,1)S(1)} collective-permute-done((bf16[256,768]{1,0:T(8,128)(2,1)S(1)}, bf16[256,768]{1,0:T(8,128)(2,1)S(1)}, u32[]{:S(2)}, u32[]{:S(2)}) %collective-permute-start.7) | collective-permute-done | bytes 393248 | tf_op jit(solution)/shard_map/ppermute | solution.py:1043
  63.8 1.7 collective-permute-done.8.refs_1_
  65.5 3.5 %feed_up.1 = (f32[256,768]{1,0:T(8,128)S(1)}, bf16[256,768]{1,0:T(8,128)(2,1)S(1)}, bf16[512,768]{1,0:T(8,128)(2,1)S(1)}, f32[512,768]{1,0:T(8,128)S(1)}) custom-call(s32[7]{0:T(128)S(1)} %copy-done.12, bf16[256,768]{1,0:T(8,128)(2,1)S(1)} %get-tuple-element.138.refs_0_, bf16[256,768]{1,0:T(8,128)(2,1)S(1)} %collective-permute-done.8.refs_1_, ...), custom_call_target="tpu_custom_call" | custom-call | flops 440000000 | bytes 1000 | tf_op jit(solution)/shard_map/feed_up/pallas_call | solution.py:160
  69.3 1.6 collective-permute-done.9
  71.0 1.6 collective-permute-start.10
  72.6 9.6 %collective-permute-done.10.refs_2_ = bf16[256,768]{1,0:T(8,128)(2,1)S(1)} collective-permute-done((bf16[256,768]{1,0:T(8,128)(2,1)S(1)}, bf16[256,768]{1,0:T(8,128)(2,1)S(1)}, u32[]{:S(2)}, u32[]{:S(2)}) %collective-permute-start.10) | collective-permute-done | bytes 393248 | tf_op jit(solution)/shard_map/ppermute | solution.py:1043
  82.2 1.7 third_norm.1
  84.5 1.2 collective-permute-done.12.refs_12_
  85.7 2.1 %feed_down.1 = (f32[256,768]{1,0:T(8,128)S(1)}, bf16[256,768]{1,0:T(8,128)(2,1)S(1)}, bf16[512,768]{1,0:T(8,128)(2,1)S(1)}, f32[1,768]{1,0:T(1,128)S(1)}) custom-call(s32[7]{0:T(128)S(1)} %copy-done.12, bf16[256,768]{1,0:T(8,128)(2,1)S(1)} %get-tuple-element.142.refs_0_.refs_3_, bf16[256,768]{1,0:T(8,128)(2,1)S(1)} %collective-permute-done.11.refs_1_.refs_4_, ...), custom_call_target="tpu_custom_call" | custom-call | flops 330000000 | bytes 1000 | tf_op jit(solution)/shard_map/feed_down/pallas_call | solution.py:160
  88.0 1.6 collective-permute-done.13
  89.7 1.6 collective-permute-start.14
  91.3 3.4 %feed_grads.1 = (bf16[384,1536]{1,0:T(8,128)(2,1)S(1)}, f32[4,96,1536]{2,1,0:T(8,128)S(1)}) custom-call(s32[7]{0:T(128)S(1)} %copy-done.12, bf16[256,768]{1,0:T(8,128)(2,1)S(1)} %get-tuple-element.138.refs_0_, bf16[256,768]{1,0:T(8,128)(2,1)S(1)} %collective-permute-done.8.refs_1_, bf16[512,768]{1,0:T(8,128)(2,1)S(1)} %get-tuple-element.149.refs_2_, ...), custom_call_target="tpu_custom_call" | custom-call | flops 440000000 | bytes 1000 | tf_op jit(solution)/shard_map/feed_grads/pallas_call | solution.py:160
  94.8 6.2 %collective-permute-done.14.refs_2_ = bf16[256,768]{1,0:T(8,128)(2,1)S(1)} collective-permute-done((bf16[256,768]{1,0:T(8,128)(2,1)S(1)}, bf16[256,768]{1,0:T(8,128)(2,1)S(1)}, u32[]{:S(2)}, u32[]{:S(2)}) %collective-permute-start.14) | collective-permute-done | bytes 393248 | tf_op jit(solution)/shard_map/ppermute | solution.py:1043
  102.3 1.6 collective-permute-start.19
  105.1 9.3 %cross_bwd.1 = (f32[256,768]{1,0:T(8,128)S(1)}, bf16[256,768]{1,0:T(8,128)(2,1)S(1)}, bf16[512,192]{1,0:T(8,128)(2,1)S(1)}, bf16[3,1664,128]{2,1,0:T(8,128)(2,1)S(1)}, f32[2,192]{1,0:T(2,128)S(1)}) custom-call(s32[7]{0:T(128)S(1)} %copy-done.12, bf16[256,768]{1,0:T(8,128)(2,1)S(1)} %get-tuple-element.154.refs_0_.refs_6_, ...), custom_call_target="tpu_custom_call" | custom-call | flops 1210000000 | bytes 1000 | tf_op jit(solution)/shard_map/cross_bwd/pallas_call | solution.py:160
  114.6 1.6 collective-permute-done.17
  116.3 1.5 collective-permute-start.18
  117.8 4.6 %cross_grads.1 = (bf16[2,416,768]{2,1,0:T(8,128)(2,1)S(1)}, f32[2,416,768]{2,1,0:T(8,128)S(1)}, bf16[384,768]{1,0:T(8,128)(2,1)S(1)}, f32[4,96,768]{2,1,0:T(8,128)S(1)}) custom-call(s32[7]{0:T(128)S(1)} %copy-done.12, bf16[416,768]{1,0:T(8,128)(2,1)S(1)} %bitcast.34, bf16[416,768]{1,0:T(8,128)(2,1)S(1)} %collective-permute-done.3.refs_1_, ...), custom_call_target="tpu_custom_call" | custom-call | flops 550000000 | bytes 1000 | tf_op jit(solution)/shard_map/cross_grads/pallas_call | solution.py:160
  122.4 8.2 %collective-permute-done.19.refs_1_ = bf16[384,1536]{1,0:T(8,128)(2,1)S(1)} collective-permute-done((bf16[384,1536]{1,0:T(8,128)(2,1)S(1)}, bf16[384,1536]{1,0:T(8,128)(2,1)S(1)}, u32[]{:S(2)}, u32[]{:S(2)}) %collective-permute-start.19) | collective-permute-done | bytes 1179680 | tf_op jit(solution)/shard_map/ppermute | solution.py:1046
  131.6 1.2 first_back.1
  133.4 1.6 collective-permute-start.23
  135.0 1.6 collective-permute-start.24
  137.8 5.2 %self_bwd.1 = (bf16[512,768]{1,0:T(8,128)(2,1)S(1)}, f32[256,768]{1,0:T(8,128)S(1)}, bf16[416,768]{1,0:T(8,128)(2,1)S(1)}, f32[4,96,768]{2,1,0:T(8,128)S(1)}, f32[16,768]{1,0:T(8,128)S(1)}) custom-call(s32[7]{0:T(128)S(1)} %copy-done.12, bf16[256,768]{1,0:T(8,128)(2,1)S(1)} %get-tuple-element.173.refs_0_, ...), custom_call_target="tpu_custom_call" | custom-call | flops 660000000 | bytes 1000 | tf_op jit(solution)/shard_map/self_bwd/pallas_call | solution.py:160
  143.6 6.0 %collective-permute-done.23.refs_2_ = bf16[384,768]{1,0:T(8,128)(2,1)S(1)} collective-permute-done((bf16[384,768]{1,0:T(8,128)(2,1)S(1)}, bf16[384,768]{1,0:T(8,128)(2,1)S(1)}, u32[]{:S(2)}, u32[]{:S(2)}) %collective-permute-start.23) | collective-permute-done | bytes 589856 | tf_op jit(solution)/shard_map/ppermute | solution.py:1046
  150.7 2.6 %collective-permute-start.25 = (bf16[96,1536]{1,0:T(8,128)(2,1)S(1)}, bf16[96,1536]{1,0:T(8,128)(2,1)S(1)}, u32[]{:S(2)}, u32[]{:S(2)}) collective-permute-start(bf16[96,1536]{1,0:T(8,128)(2,1)S(1)} %get-tuple-element.194), channel_id=1, source_target_pairs={{0,16},{4,20},{8,24},{12,28},{16,0},{20,4},{24,8},{28,12},{1,17},{... | collective-permute-start | bytes 884744 | tf_op jit(solution)/shard_map/ppermute | solution.py:1046
  153.3 12.5 %collective-permute-done.25.refs_1_ = bf16[96,1536]{1,0:T(8,128)(2,1)S(1)} collective-permute-done((bf16[96,1536]{1,0:T(8,128)(2,1)S(1)}, bf16[96,1536]{1,0:T(8,128)(2,1)S(1)}, u32[]{:S(2)}, u32[]{:S(2)}) %collective-permute-start.25) | collective-permute-done | bytes 294944 | tf_op jit(solution)/shard_map/ppermute | solution.py:1046
  165.8 1.4 last_stage.2
  168.9 1.5 collective-permute-done.27.refs_1_
  170.5 1.6 collective-permute-start.28
  172.0 12.9 %collective-permute-done.29.refs_1_ = bf16[208,1536]{1,0:T(8,128)(2,1)S(1)} collective-permute-done((bf16[208,1536]{1,0:T(8,128)(2,1)S(1)}, bf16[208,1536]{1,0:T(8,128)(2,1)S(1)}, u32[]{:S(2)}, u32[]{:S(2)}) %collective-permute-start.29) | collective-permute-done | bytes 639008 | tf_op jit(solution)/shard_map/ppermute | solution.py:1046
  186.0 1.6 collective-permute-start.31
  187.5 2.3 %collective-permute-start.32 = (bf16[112,1536]{1,0:T(8,128)(2,1)S(1)}, bf16[112,1536]{1,0:T(8,128)(2,1)S(1)}, u32[]{:S(2)}, u32[]{:S(2)}) collective-permute-start(bf16[112,1536]{1,0:T(8,128)(2,1)S(1)} %get-tuple-element.207), channel_id=1, source_target_pairs={{0,16},{4,20},{8,24},{12,28},{16,0},{20,4},{24,8},{28,12},{1,17},{... | collective-permute-start | bytes 1032200 | tf_op jit(solution)/shard_map/ppermute | solution.py:1046
  189.8 1.5 join_halves.2
  191.3 1.8 join_halves.3
  193.2 9.7 %collective-permute-done.31 = bf16[416,768]{1,0:T(8,128)(2,1)S(1)} collective-permute-done((bf16[416,768]{1,0:T(8,128)(2,1)S(1)}, bf16[416,768]{1,0:T(8,128)(2,1)S(1)}, u32[]{:S(2)}, u32[]{:S(2)}) %collective-permute-start.31) | collective-permute-done | bytes 639008 | tf_op jit(solution)/shard_map/ppermute | solution.py:1043
  202.8 1.3 fusion
  204.1 1.9 collective-permute-done.32.refs_1_
  206.0 1.6 last_stage.3
  (99 shorter events, 17.3 us)
Async XLA Ops:
  0.7 9.1 %copy-start.6 = (bf16[1,416,768]{2,1,0:T(8,128)(2,1)S(1)}, bf16[1,416,768]{2,1,0:T(8,128)(2,1)}, u32[]{:S(2)}) copy-start(bf16[1,416,768]{2,1,0:T(8,128)(2,1)} %param.20) | copy-start | bytes 1916932
  9.3 6.2 %copy-start.12 = (s32[7]{0:T(128)S(1)}, s32[7]{0:T(128)}, u32[]{:S(2)}) copy-start(s32[7]{0:T(128)} %stack.27.at_ref) | copy-start | bytes 88
  9.3 3.1 %collective-permute-start = (bf16[256,768]{1,0:T(8,128)(2,1)}, bf16[256,768]{1,0:T(8,128)(2,1)S(1)}, u32[]{:S(2)}, u32[]{:S(2)}) collective-permute-start(bf16[256,768]{1,0:T(8,128)(2,1)} %get-tuple-element.123), channel_id=1, source_target_pairs={{0,1},{1,0},{2,3},{3,2},{4,5},{5,4},{6,7},{7,6},{8,9},{9,8},{10,11... | collective-permute-start | bytes 1179656 | tf_op jit(solution)/shard_map/ppermute | solution.py:1040
  9.8 18.1 %collective-permute-start.2 = (bf16[416,768]{1,0:T(8,128)(2,1)S(1)}, bf16[416,768]{1,0:T(8,128)(2,1)S(1)}, u32[]{:S(2)}, u32[]{:S(2)}) collective-permute-start(bf16[416,768]{1,0:T(8,128)(2,1)S(1)} %bitcast.31), channel_id=1, source_target_pairs={{0,2},{1,3},{2,0},{3,1},{4,6},{5,7},{6,4},{7,5},{8,10},{9,11},{10,... | collective-permute-start | bytes 1916936 | tf_op jit(solution)/shard_map/ppermute | solution.py:1043
  13.6 24.6 %collective-permute-start.1 = (bf16[256,768]{1,0:T(8,128)(2,1)S(1)}, bf16[256,768]{1,0:T(8,128)(2,1)S(1)}, u32[]{:S(2)}, u32[]{:S(2)}) collective-permute-start(bf16[256,768]{1,0:T(8,128)(2,1)S(1)} %add_convert_fusion.6.refs_0_), channel_id=1, source_target_pairs={{0,2},{1,3},{2,0},{3,1},{4,6},{5,7},{6,4},{7,5},{8,10},{9,11},{10,... | collective-permute-start | bytes 1179656 | tf_op jit(solution)/shard_map/ppermute | solution.py:1043
  18.3 10.2 %copy-start.17 = (f32[768]{0:T(1024)S(1)}, f32[768]{0:T(1024)}, u32[]{:S(2)}) copy-start(f32[768]{0:T(1024)} %param.27) | copy-start | bytes 9220
  27.9 11.4 %collective-permute-start.3 = (bf16[416,768]{1,0:T(8,128)(2,1)S(1)}, bf16[416,768]{1,0:T(8,128)(2,1)S(1)}, u32[]{:S(2)}, u32[]{:S(2)}) collective-permute-start(bf16[416,768]{1,0:T(8,128)(2,1)S(1)} %bitcast.32), channel_id=1, source_target_pairs={{0,1},{1,0},{2,3},{3,2},{4,5},{5,4},{6,7},{7,6},{8,9},{9,8},{10,11... | collective-permute-start | bytes 1916936 | tf_op jit(solution)/shard_map/ppermute | solution.py:1040
  28.0 11.3 %collective-permute-start.4 = (bf16[416,768]{1,0:T(8,128)(2,1)S(1)}, bf16[416,768]{1,0:T(8,128)(2,1)S(1)}, u32[]{:S(2)}, u32[]{:S(2)}) collective-permute-start(bf16[416,768]{1,0:T(8,128)(2,1)S(1)} %collective-permute-done.2.refs_2_), channel_id=1, source_target_pairs={{0,1},{1,0},{2,3},{3,2},{4,5},{5,4},{6,7},{7,6},{8,9},{9,8},{10,11... | collective-permute-start | bytes 1916936 | tf_op jit(solution)/shard_map/ppermute | solution.py:1040
  28.5 9.7 %copy-start.2 = (bf16[512,768]{1,0:T(8,128)(2,1)S(1)}, bf16[512,768]{1,0:T(8,128)(2,1)}, u32[]{:S(2)}) copy-start(bf16[512,768]{1,0:T(8,128)(2,1)} %refs_5_.7) | copy-start | bytes 2359300
  28.5 9.7 %copy-start.13 = (f32[3,768]{1,0:T(4,128)S(1)}, f32[3,768]{1,0:T(4,128)}, u32[]{:S(2)}) copy-start(f32[3,768]{1,0:T(4,128)} %refs_4_.7) | copy-start | bytes 27652
  28.5 9.7 %copy-start.15 = (f32[3,768]{1,0:T(4,128)S(1)}, f32[3,768]{1,0:T(4,128)}, u32[]{:S(2)}) copy-start(f32[3,768]{1,0:T(4,128)} %refs_6_.1) | copy-start | bytes 27652
  39.2 2.5 %collective-permute-start.5 = (bf16[256,768]{1,0:T(8,128)(2,1)S(1)}, bf16[256,768]{1,0:T(8,128)(2,1)S(1)}, u32[]{:S(2)}, u32[]{:S(2)}) collective-permute-start(bf16[256,768]{1,0:T(8,128)(2,1)S(1)} %get-tuple-element.128.refs_0_.refs_8_), channel_id=1, source_target_pairs={{0,1},{1,0},{2,3},{3,2},{4,5},{5,4},{6,7},{7,6},{8,9},{9,8},{10,11... | collective-permute-start | bytes 1179656 | tf_op jit(solution)/shard_map/ppermute | solution.py:1040
  49.4 1.8 collective-permute-start.6
  51.3 12.6 %copy-start.19 = (f32[768]{0:T(1024)S(1)}, f32[768]{0:T(1024)}, u32[]{:S(2)}) copy-start(f32[768]{0:T(1024)} %param.33) | copy-start | bytes 9220
  51.3 14.3 %copy-start.3 = (bf16[768,768]{1,0:T(8,128)(2,1)S(1)}, bf16[768,768]{1,0:T(8,128)(2,1)}, u32[]{:S(2)}) copy-start(bf16[768,768]{1,0:T(8,128)(2,1)} %refs_2_.9) | copy-start | bytes 3538948
  51.3 14.3 %copy-start.4 = (bf16[768,768]{1,0:T(8,128)(2,1)S(1)}, bf16[768,768]{1,0:T(8,128)(2,1)}, u32[]{:S(2)}) copy-start(bf16[768,768]{1,0:T(8,128)(2,1)} %refs_3_.7) | copy-start | bytes 3538948
  51.4 11.5 %collective-permute-start.7 = (bf16[256,768]{1,0:T(8,128)(2,1)S(1)}, bf16[256,768]{1,0:T(8,128)(2,1)S(1)}, u32[]{:S(2)}, u32[]{:S(2)}) collective-permute-start(bf16[256,768]{1,0:T(8,128)(2,1)S(1)} %add_convert_fusion.5.refs_1_), channel_id=1, source_target_pairs={{0,2},{1,3},{2,0},{3,1},{4,6},{5,7},{6,4},{7,5},{8,10},{9,11},{10,... | collective-permute-start | bytes 1179656 | tf_op jit(solution)/shard_map/ppermute | solution.py:1043
  63.7 1.8 collective-permute-start.8
  69.1 13.1 %copy-start.10 = (bf16[512,768]{1,0:T(8,128)(2,1)S(1)}, bf16[512,768]{1,0:T(8,128)(2,1)}, u32[]{:S(2)}) copy-start(bf16[512,768]{1,0:T(8,128)(2,1)} %refs_3_.6) | copy-start | bytes 2359300
  69.1 1.8 collective-permute-start.9
  71.0 11.2 %collective-permute-start.10 = (bf16[256,768]{1,0:T(8,128)(2,1)S(1)}, bf16[256,768]{1,0:T(8,128)(2,1)S(1)}, u32[]{:S(2)}, u32[]{:S(2)}) collective-permute-start(bf16[256,768]{1,0:T(8,128)(2,1)S(1)} %add_convert_fusion.4.refs_1_), channel_id=1, source_target_pairs={{0,2},{1,3},{2,0},{3,1},{4,6},{5,7},{6,4},{7,5},{8,10},{9,11},{10,... | collective-permute-start | bytes 1179656 | tf_op jit(solution)/shard_map/ppermute | solution.py:1043
  83.9 1.8 collective-permute-start.11
  84.0 1.7 collective-permute-start.12
  87.8 1.8 collective-permute-start.13
  89.7 11.2 %collective-permute-start.14 = (bf16[256,768]{1,0:T(8,128)(2,1)S(1)}, bf16[256,768]{1,0:T(8,128)(2,1)S(1)}, u32[]{:S(2)}, u32[]{:S(2)}) collective-permute-start(bf16[256,768]{1,0:T(8,128)(2,1)S(1)} %add_convert_fusion.3.refs_1_), channel_id=1, source_target_pairs={{0,2},{1,3},{2,0},{3,1},{4,6},{5,7},{6,4},{7,5},{8,10},{9,11},{10,... | collective-permute-start | bytes 1179656 | tf_op jit(solution)/shard_map/ppermute | solution.py:1043
  102.2 2.9 %collective-permute-start.15 = (bf16[256,768]{1,0:T(8,128)(2,1)S(1)}, bf16[256,768]{1,0:T(8,128)(2,1)S(1)}, u32[]{:S(2)}, u32[]{:S(2)}) collective-permute-start(bf16[256,768]{1,0:T(8,128)(2,1)S(1)} %get-tuple-element.154.refs_0_.refs_6_), channel_id=1, source_target_pairs={{0,1},{1,0},{2,3},{3,2},{4,5},{5,4},{6,7},{7,6},{8,9},{9,8},{10,11... | collective-permute-start | bytes 1179656 | tf_op jit(solution)/shard_map/ppermute | solution.py:1040
  102.3 28.4 %collective-permute-start.19 = (bf16[384,1536]{1,0:T(8,128)(2,1)S(1)}, bf16[384,1536]{1,0:T(8,128)(2,1)S(1)}, u32[]{:S(2)}, u32[]{:S(2)}) collective-permute-start(bf16[384,1536]{1,0:T(8,128)(2,1)S(1)} %get-tuple-element.151), channel_id=1, source_target_pairs={{0,4},{4,0},{8,12},{12,8},{16,20},{20,16},{24,28},{28,24},{1,5},{5... | collective-permute-start | bytes 3538952 | tf_op jit(solution)/shard_map/ppermute | solution.py:1046
  103.9 1.2 collective-permute-start.16
  114.4 1.8 collective-permute-start.17
  116.3 15.2 %collective-permute-start.18 = (bf16[256,768]{1,0:T(8,128)(2,1)S(1)}, bf16[256,768]{1,0:T(8,128)(2,1)S(1)}, u32[]{:S(2)}, u32[]{:S(2)}) collective-permute-start(bf16[256,768]{1,0:T(8,128)(2,1)S(1)} %add_convert_fusion.2.refs_1_), channel_id=1, source_target_pairs={{0,2},{1,3},{2,0},{3,1},{4,6},{5,7},{6,4},{7,5},{8,10},{9,11},{10,... | collective-permute-start | bytes 1179656 | tf_op jit(solution)/shard_map/ppermute | solution.py:1043
  130.6 7.1 %copy-start.7 = (bf16[3,512,512]{2,1,0:T(8,128)(2,1)S(1)}, bf16[3,512,512]{2,1,0:T(8,128)(2,1)}, u32[]{:S(2)}) copy-start(bf16[3,512,512]{2,1,0:T(8,128)(2,1)} %get-tuple-element.179.refs_4_) | copy-start | bytes 4718596
  131.5 6.3 %copy-start.5 = (bf16[3,768,192]{1,2,0:T(8,128)(2,1)S(1)}, bf16[3,768,192]{1,2,0:T(8,128)(2,1)}, u32[]{:S(2)}) copy-start(bf16[3,768,192]{1,2,0:T(8,128)(2,1)} %param.24) | copy-start | bytes 2654212
  131.5 6.3 %copy-start.9 = (bf16[192,768]{1,0:T(8,128)(2,1)S(1)}, bf16[192,768]{1,0:T(8,128)(2,1)}, u32[]{:S(2)}) copy-start(bf16[192,768]{1,0:T(8,128)(2,1)} %refs_2_.11) | copy-start | bytes 884740
  131.5 6.3 %copy-start.11 = (bf16[3,512,192]{2,1,0:T(8,128)(2,1)S(1)}, bf16[3,512,192]{2,1,0:T(8,128)(2,1)}, u32[]{:S(2)}) copy-start(bf16[3,512,192]{2,1,0:T(8,128)(2,1)} %get-tuple-element.178.refs_3_) | copy-start | bytes 1769476
  131.5 6.3 %copy-start.14 = (bf16[512,192]{1,0:T(8,128)(2,1)S(1)}, bf16[512,192]{1,0:T(8,128)(2,1)}, u32[]{:S(2)}) copy-start(bf16[512,192]{1,0:T(8,128)(2,1)} %get-tuple-element.181.refs_8_) | copy-start | bytes 589828
  131.5 6.2 %collective-permute-start.22 = (bf16[2,416,768]{2,1,0:T(8,128)(2,1)S(1)}, bf16[2,416,768]{2,1,0:T(8,128)(2,1)S(1)}, u32[]{:S(2)}, u32[]{:S(2)}) collective-permute-start(bf16[2,416,768]{2,1,0:T(8,128)(2,1)S(1)} %get-tuple-element.176), channel_id=1, source_target_pairs={{0,1},{1,0},{2,3},{3,2},{4,5},{5,4},{6,7},{7,6},{8,9},{9,8},{10,11... | collective-permute-start | bytes 3833864 | tf_op jit(solution)/shard_map/ppermute | solution.py:1040
  132.9 4.9 %collective-permute-start.20 = (bf16[256,768]{1,0:T(8,128)(2,1)S(1)}, bf16[256,768]{1,0:T(8,128)(2,1)S(1)}, u32[]{:S(2)}, u32[]{:S(2)}) collective-permute-start(bf16[256,768]{1,0:T(8,128)(2,1)S(1)} %get-tuple-element.173.refs_0_), channel_id=1, source_target_pairs={{0,1},{1,0},{2,3},{3,2},{4,5},{5,4},{6,7},{7,6},{8,9},{9,8},{10,11... | collective-permute-start | bytes 1179656 | tf_op jit(solution)/shard_map/ppermute | solution.py:1040
  133.4 16.2 %collective-permute-start.23 = (bf16[384,768]{1,0:T(8,128)(2,1)S(1)}, bf16[384,768]{1,0:T(8,128)(2,1)S(1)}, u32[]{:S(2)}, u32[]{:S(2)}) collective-permute-start(bf16[384,768]{1,0:T(8,128)(2,1)S(1)} %get-tuple-element.189), channel_id=1, source_target_pairs={{0,4},{4,0},{8,12},{12,8},{16,20},{20,16},{24,28},{28,24},{1,5},{5... | collective-permute-start | bytes 1769480 | tf_op jit(solution)/shard_map/ppermute | solution.py:1046
  135.0 15.0 %collective-permute-start.24 = (bf16[192,1536]{1,0:T(8,128)(2,1)S(1)}, bf16[192,1536]{1,0:T(8,128)(2,1)S(1)}, u32[]{:S(2)}, u32[]{:S(2)}) collective-permute-start(bf16[192,1536]{1,0:T(8,128)(2,1)S(1)} %get-tuple-element.169), channel_id=1, source_target_pairs={{0,8},{4,12},{8,0},{12,4},{16,24},{20,28},{24,16},{28,20},{1,9},{5... | collective-permute-start | bytes 1769480 | tf_op jit(solution)/shard_map/ppermute | solution.py:1046
  136.6 1.2 collective-permute-start.21
  143.0 24.3 %collective-permute-start.26 = (bf16[416,768]{1,0:T(8,128)(2,1)S(1)}, bf16[416,768]{1,0:T(8,128)(2,1)S(1)}, u32[]{:S(2)}, u32[]{:S(2)}) collective-permute-start(bf16[416,768]{1,0:T(8,128)(2,1)S(1)} %get-tuple-element.201), channel_id=1, source_target_pairs={{0,4},{4,0},{8,12},{12,8},{16,20},{20,16},{24,28},{28,24},{1,5},{5... | collective-permute-start | bytes 1916936 | tf_op jit(solution)/shard_map/ppermute | solution.py:1046
  150.7 15.1 %collective-permute-start.25 = (bf16[96,1536]{1,0:T(8,128)(2,1)S(1)}, bf16[96,1536]{1,0:T(8,128)(2,1)S(1)}, u32[]{:S(2)}, u32[]{:S(2)}) collective-permute-start(bf16[96,1536]{1,0:T(8,128)(2,1)S(1)} %get-tuple-element.194), channel_id=1, source_target_pairs={{0,16},{4,20},{8,24},{12,28},{16,0},{20,4},{24,8},{28,12},{1,17},{... | collective-permute-start | bytes 884744 | tf_op jit(solution)/shard_map/ppermute | solution.py:1046
  168.0 2.4 %collective-permute-start.27 = (bf16[512,768]{1,0:T(8,128)(2,1)S(1)}, bf16[512,768]{1,0:T(8,128)(2,1)S(1)}, u32[]{:S(2)}, u32[]{:S(2)}) collective-permute-start(bf16[512,768]{1,0:T(8,128)(2,1)S(1)} %get-tuple-element.203), channel_id=1, source_target_pairs={{0,1},{1,0},{2,3},{3,2},{4,5},{5,4},{6,7},{7,6},{8,9},{9,8},{10,11... | collective-permute-start | bytes 2359304 | tf_op jit(solution)/shard_map/ppermute | solution.py:1040
  168.1 16.8 %collective-permute-start.29 = (bf16[208,1536]{1,0:T(8,128)(2,1)S(1)}, bf16[208,1536]{1,0:T(8,128)(2,1)S(1)}, u32[]{:S(2)}, u32[]{:S(2)}) collective-permute-start(bf16[208,1536]{1,0:T(8,128)(2,1)S(1)} %get-tuple-element.202), channel_id=1, source_target_pairs={{0,8},{4,12},{8,0},{12,4},{16,24},{20,28},{24,16},{28,20},{1,9},{5... | collective-permute-start | bytes 1916936 | tf_op jit(solution)/shard_map/ppermute | solution.py:1046
  170.5 15.1 %collective-permute-start.28 = (bf16[256,768]{1,0:T(8,128)(2,1)S(1)}, bf16[256,768]{1,0:T(8,128)(2,1)S(1)}, u32[]{:S(2)}, u32[]{:S(2)}) collective-permute-start(bf16[256,768]{1,0:T(8,128)(2,1)S(1)} %add_convert_fusion.1), channel_id=1, source_target_pairs={{0,2},{1,3},{2,0},{3,1},{4,6},{5,7},{6,4},{7,5},{8,10},{9,11},{10,... | collective-permute-start | bytes 1179656 | tf_op jit(solution)/shard_map/ppermute | solution.py:1043
  185.7 5.6 %collective-permute-start.30 = (f32[256,768]{1,0:T(8,128)S(1)}, f32[256,768]{1,0:T(8,128)S(1)}, u32[]{:S(2)}, u32[]{:S(2)}) collective-permute-start(f32[256,768]{1,0:T(8,128)S(1)} %add_add_fusion.refs_0_), channel_id=1, source_target_pairs={{0,1},{1,0},{2,3},{3,2},{4,5},{5,4},{6,7},{7,6},{8,9},{9,8},{10,11... | collective-permute-start | bytes 2359304 | tf_op jit(solution)/shard_map/ppermute | solution.py:1040
  186.0 16.8 %collective-permute-start.31 = (bf16[416,768]{1,0:T(8,128)(2,1)S(1)}, bf16[416,768]{1,0:T(8,128)(2,1)S(1)}, u32[]{:S(2)}, u32[]{:S(2)}) collective-permute-start(bf16[416,768]{1,0:T(8,128)(2,1)S(1)} %fusion.1), channel_id=1, source_target_pairs={{0,2},{1,3},{2,0},{3,1},{4,6},{5,7},{6,4},{7,5},{8,10},{9,11},{10,... | collective-permute-start | bytes 1916936 | tf_op jit(solution)/shard_map/ppermute | solution.py:1043
  187.5 18.5 %collective-permute-start.32 = (bf16[112,1536]{1,0:T(8,128)(2,1)S(1)}, bf16[112,1536]{1,0:T(8,128)(2,1)S(1)}, u32[]{:S(2)}, u32[]{:S(2)}) collective-permute-start(bf16[112,1536]{1,0:T(8,128)(2,1)S(1)} %get-tuple-element.207), channel_id=1, source_target_pairs={{0,16},{4,20},{8,24},{12,28},{16,0},{20,4},{24,8},{28,12},{1,17},{... | collective-permute-start | bytes 1032200 | tf_op jit(solution)/shard_map/ppermute | solution.py:1046
  (6 other events, 15.7 us)
